TPU v7x, 512 devices: a whole 4x8x8 slice. The times are simulated.
512 devices in a mesh: seq: 64 (over z, y_lo, core), chan: 8 (over x, y_hi).
Axes of the slice: x: 4, y: 8 (y_hi: 2, y_lo: 4; y = y_hi * 4 + y_lo), z: 8, core: 2. Of those that a mesh axis runs over, the one named last changes fastest.
Arguments:
- tokens: bfloat16 [16384, 512], P('seq', 'chan'), may hold values from -6 to 6
- out_grad: bfloat16 [16384, 512], P('seq', 'chan'), may hold values from -6 to 6
- in_weight: bfloat16 [512, 1024], P('seq', 'chan'), may hold values from -0.25 to 0.25
- dt_weight: bfloat16 [512, 16], P('seq', 'chan'), may hold values from -0.25 to 0.25
- bc_weight: bfloat16 [512, 128], P('seq'), may hold values from -0.0625 to 0.0625
- out_weight: bfloat16 [1024, 512], P('chan', 'seq'), may hold values from -0.1875 to 0.1875
- decay_rate: float32 [2, 16], P(None, 'chan'), may hold values from 0.00036621094 to 8
- dt_bias: float32 [2, 16], P(None, 'chan'), may hold values from -5 to -4
- skip_gain: float32 [16], P('chan'), may hold values from 0.5 to 1.5
Outputs:
- tokens_grad: bfloat16 [16384, 512], P('seq', 'chan')
- in_weight_grad: float32 [512, 1024], P('seq', 'chan')
- dt_weight_grad: float32 [512, 16], P('seq', 'chan')
- bc_weight_grad: float32 [512, 128], P('seq')
- out_weight_grad: float32 [1024, 512], P('chan', 'seq')
- rate_grad: float32 [2, 16], P(None, 'chan')
- bias_grad: float32 [2, 16], P(None, 'chan')
- skip_grad: float32 [16], P('chan')
All inputs are finite; a program needn't handle non-finite values.
Results may differ from a plain program's by a relative error of at most 0.0034.
Values may be sent and summed in bfloat16 or wider, within the bound.
No kernel may reach another device: no remote copies, remote signals or barrier semaphores. Data moves between devices by JAX's collectives and lax.ppermute only.
A program may use at most 64 MiB of HBM per device.

v0:
```python
import jax
import jax.numpy as jnp
from jax import lax
from jax.sharding import Mesh
from jax.sharding import PartitionSpec as P

STATE = 64
GROUP = 256
SEQ = ("seq_0", "seq_1", "seq_2")


def laid_out(pieces, dim):
    dims = list(pieces.shape[1:])
    dims[dim] *= pieces.shape[0]
    return jnp.moveaxis(pieces, 0, dim).reshape(dims)


def copy_for_each(array, axis):
    size = lax.axis_size(axis)
    return lax.all_to_all(
        jnp.broadcast_to(array[None], (size, *array.shape)), axis, 0, 0, tiled=True
    )


def gather_directly(array, axis, dim):
    return laid_out(copy_for_each(array, axis), dim)


def neutral_like(array, identity):
    return jax.tree.map(
        lambda part, zero: jnp.zeros_like(part) + jnp.asarray(zero, part.dtype), array, identity
    )


def all_in_one(array, axis):
    leaves = jax.tree.leaves(array)
    sequence = sorted(range(len(leaves)), key=lambda k: -leaves[k].size)
    width = (1, *leaves[sequence[0]].shape)[-1]
    lines = [
        jnp.pad(leaves[k].reshape(-1), (0, -leaves[k].size % width)).reshape(-1, width)
        for k in sequence
    ]
    both, at, found = (lax.all_gather(jnp.concatenate(lines), axis), 0, {})
    for k, line in zip(sequence, lines):
        share = both[:, at : at + len(line)].reshape(len(both), -1)
        found[k] = share[:, : leaves[k].size].reshape(-1, *leaves[k].shape)
        at += len(line)
    numbers = iter(range(len(leaves)))
    return jax.tree.map(lambda _: found[next(numbers)], array)


def carried_in(array, axes, combine, identity):
    before = start = neutral_like(array, identity)
    running = array
    for axis in reversed(axes):
        size, index = (lax.axis_size(axis), lax.axis_index(axis))
        pieces = all_in_one(running, axis)
        inside, running = (start, start)
        for k in range(size):
            passed = k < index
            running = combine(running, jax.tree.map(lambda part: part[k], pieces))
            inside = jax.tree.map(lambda new, old: jnp.where(passed, new, old), running, inside)
        before = combine(inside, before)
    return before


def carried_in_2(array, axes, combine, identity):
    before = start = neutral_like(array, identity)
    running = array
    for axis in reversed(axes):
        size, index = (lax.axis_size(axis), lax.axis_index(axis))
        pieces = jax.tree.map(lambda part: lax.all_gather(part, axis), running)
        inside, running = (start, start)
        for k in reversed(range(size)):
            passed = k > index
            running = combine(running, jax.tree.map(lambda part: part[k], pieces))
            inside = jax.tree.map(lambda new, old: jnp.where(passed, new, old), running, inside)
        before = combine(inside, before)
    return before


def cut_along(array, dim, size):
    before, after = (array.shape[:dim], array.shape[dim + 1 :])
    return jnp.moveaxis(array.reshape(*before, size, -1, *after), dim, 0)


def summed_on_arrival(array, axis, dim):
    size = lax.axis_size(axis)
    pieces = lax.all_to_all(cut_along(array, dim, size), axis, 0, 0, tiled=True)
    return jnp.sum(pieces, axis=0)


def over_copies(array, axis):
    return copy_for_each(array, axis).sum(axis=0)


def together(arrays, axis):
    ends = [0]
    for a in arrays:
        ends.append(ends[-1] + a.size)
    running = over_copies(jnp.concatenate([a.ravel() for a in arrays]), axis)
    return tuple((running[b:e].reshape(a.shape) for a, b, e in zip(arrays, ends, ends[1:])))


def ssd_core(gated, step_size, b_proj, c_proj, rate, skip_gain, start_state):
    length, width = gated.shape
    heads = step_size.shape[1]
    head_dim = width // heads
    blocks = length // GROUP
    log_decay = -rate[None, :] * step_size
    driven = gated.reshape(length, heads, head_dim) * step_size[:, :, None]
    causal = lax.broadcasted_iota(jnp.int32, (GROUP, GROUP), 0) >= lax.broadcasted_iota(
        jnp.int32, (GROUP, GROUP), 1
    )

    def advance(memory, block):
        plain, pushed, decays, b_block, c_block = block
        running = jnp.cumsum(decays, axis=0)
        across = running.T
        spread = across[:, :, None] - across[:, None, :]
        kept = jnp.where(causal[None], jnp.exp(jnp.where(causal[None], spread, 0.0)), 0.0)
        scores = jnp.dot(c_block, b_block.T, precision=lax.Precision.HIGHEST)
        weighted = kept * scores[None]
        within = jnp.einsum("hts,shp->thp", weighted, pushed, precision=lax.Precision.HIGHEST)
        carried = (
            jnp.einsum("tn,hpn->thp", c_block, memory, precision=lax.Precision.HIGHEST)
            * jnp.exp(running)[:, :, None]
        )
        output = within + carried + skip_gain[None, :, None] * plain
        tail_decay = jnp.exp(running[-1][None, :] - running)
        memory = jnp.exp(running[-1])[:, None, None] * memory + jnp.einsum(
            "sh,shp,sn->hpn", tail_decay, pushed, b_block, precision=lax.Precision.HIGHEST
        )
        return (memory, output.reshape(GROUP, width))

    final_state, outputs = lax.scan(
        jax.checkpoint(advance),
        start_state,
        (
            gated.reshape(blocks, GROUP, heads, head_dim),
            driven.reshape(blocks, GROUP, heads, head_dim),
            log_decay.reshape(blocks, GROUP, heads),
            b_proj.reshape(blocks, GROUP, b_proj.shape[1]),
            c_proj.reshape(blocks, GROUP, c_proj.shape[1]),
        ),
    )
    return (outputs.reshape(length, width), final_state)


def combine(earlier, later):
    return (earlier[0] * later[0], later[0][:, :, None, None] * earlier[1] + later[1])


def body(
    tokens, out_grad, in_weight, dt_weight, bc_weight, out_weight, decay_rate, dt_bias, skip_gain
):
    seq_count = lax.axis_size(SEQ)
    tok_rows = tokens.shape[0]
    width = in_weight.shape[1]
    heads = dt_weight.shape[1]
    head_dim = width // heads
    front = width + heads
    grad_scale = (tok_rows * seq_count) ** (-0.5)
    own_rows = jnp.stack([tokens, out_grad])
    gathered = gather_directly(own_rows, "chan", 2)
    inputs_all = jnp.stack([gathered[0], gathered[0, ::-1]])
    every_gradient = jnp.stack([gathered[1], gathered[1, ::-1]])
    packed = jnp.concatenate([in_weight, dt_weight, bc_weight, out_weight.T], 1)
    full_weights = gather_directly(packed, SEQ, 0)
    primary_weight = full_weights[:, :front]
    bc_full = full_weights[:, front : front + 2 * STATE]
    reverse_direction_weight = full_weights[:, front + 2 * STATE :]
    projected = jnp.einsum(
        "euq,qn->eun",
        inputs_all,
        full_weights[:, : front + 2 * STATE],
        preferred_element_type=jnp.float32,
    )
    preact = projected[..., :width]
    dt_pre = projected[..., width:front] + dt_bias[:, None, :]
    bc_proj = projected[..., front:]
    gated = jax.nn.silu(preact)
    step_size = jax.nn.softplus(dt_pre)
    output_adjoint = jnp.einsum(
        "nah,hm->nam", every_gradient, reverse_direction_weight, preferred_element_type=jnp.float32
    )
    log_decay = -decay_rate[:, None, :] * step_size
    running = jnp.cumsum(log_decay, axis=1)
    total_decay = running[:, -1]
    driven = gated.reshape(2, tok_rows, heads, head_dim) * step_size[..., None]
    pushed_sum = jnp.einsum(
        "slh,slhp,sln->shpn",
        jnp.exp(total_decay[:, None, :] - running),
        driven,
        bc_proj[..., :STATE],
        precision=lax.Precision.HIGHEST,
    )
    pulled_sum = jnp.einsum(
        "slh,slhp,sln->shpn",
        jnp.exp(running),
        output_adjoint.reshape(2, tok_rows, heads, head_dim),
        bc_proj[..., STATE:],
        precision=lax.Precision.HIGHEST,
    )
    block_decay = jnp.exp(total_decay)
    identity = (jnp.ones_like(block_decay), jnp.zeros_like(pushed_sum))
    upward = carried_in(
        (block_decay, jnp.stack([pushed_sum[0], pulled_sum[1]])), SEQ, combine, identity
    )[1]
    downward = carried_in_2(
        (block_decay, jnp.stack([pulled_sum[0], pushed_sum[1]])), SEQ, combine, identity
    )[1]
    start_states = jnp.stack([upward[0], downward[1]])
    end_cots = jnp.stack([downward[0], upward[1]])

    def local_core(gated_in, step_in, bc_in, rate_in, gain_in, start_in):
        return ssd_core(
            gated_in, step_in, bc_in[:, :STATE], bc_in[:, STATE:], rate_in, gain_in, start_in
        )

    batched = jax.vmap(local_core, in_axes=(0, 0, 0, 0, None, 0))

    def pinned(gated_in, step_in, bc_in, rate_in, gain_in):
        return batched(gated_in, step_in, bc_in, rate_in, gain_in, start_states)

    (mixed, finals), pullback = jax.vjp(pinned, gated, step_size, bc_proj, decay_rate, skip_gain)
    d_gated, d_step, d_bc, d_rate, d_skip = pullback((output_adjoint, end_cots))
    sig_pre = jax.nn.sigmoid(preact)
    d_pre = d_gated * sig_pre * (1.0 + preact * (1.0 - sig_pre))
    d_z = d_step * jax.nn.sigmoid(dt_pre)
    leading_gradient = jnp.concatenate([d_pre, d_z], 2).astype(jnp.bfloat16)
    partial_grad = jnp.einsum(
        "pqx,ux->pqu", leading_gradient, primary_weight, preferred_element_type=jnp.float32
    )
    partial_input = partial_grad + jnp.einsum(
        "pqx,ux->pqu", d_bc, bc_full.astype(jnp.float32), precision=lax.Precision.HIGHEST
    )
    folded = partial_input[0] + partial_input[1, ::-1]
    result_grad = summed_on_arrival(folded, "chan", 1)
    tokens_grad = result_grad.astype(jnp.bfloat16)
    blended_lower_half = mixed.astype(jnp.bfloat16)
    initial_section = jnp.einsum(
        "taz,tao->zo", inputs_all, leading_gradient, preferred_element_type=jnp.float32
    )
    second_part = jnp.einsum(
        "taz,tao->zo", inputs_all.astype(jnp.float32), d_bc, precision=lax.Precision.HIGHEST
    )
    final_section = jnp.einsum(
        "taz,tao->zo", every_gradient, blended_lower_half, preferred_element_type=jnp.float32
    )
    summed = summed_on_arrival(
        grad_scale * jnp.concatenate([initial_section, second_part, final_section], 1), SEQ, 0
    )
    in_weight_grad = summed[:, :width]
    dt_weight_grad = summed[:, width:front]
    bc_weight_grad = summed[:, front : front + 2 * STATE]
    bc_weight_grad = over_copies(bc_weight_grad, "chan")
    out_weight_grad = summed[:, front + 2 * STATE :].T
    rate_grad, bias_grad, skip_grad = together(
        (grad_scale * d_rate * decay_rate, grad_scale * jnp.sum(d_z, axis=1), grad_scale * d_skip),
        SEQ,
    )
    return (
        tokens_grad,
        in_weight_grad,
        dt_weight_grad,
        bc_weight_grad,
        out_weight_grad,
        rate_grad,
        bias_grad,
        skip_grad,
    )


def solution(mesh):
    split = Mesh(
        mesh.devices.reshape(8, 4, 2, mesh.shape["chan"]), ("seq_0", "seq_1", "seq_2", "chan")
    )
    return jax.shard_map(
        body,
        mesh=split,
        in_specs=(
            P(SEQ, "chan"),
            P(SEQ, "chan"),
            P(SEQ, "chan"),
            P(SEQ, "chan"),
            P(SEQ, None),
            P("chan", SEQ),
            P(None, "chan"),
            P(None, "chan"),
            P("chan"),
        ),
        out_specs=(
            P(SEQ, "chan"),
            P(SEQ, "chan"),
            P(SEQ, "chan"),
            P(SEQ, None),
            P("chan", SEQ),
            P(None, "chan"),
            P(None, "chan"),
            P("chan"),
        ),
        check_vma=False,
    )
```

profile of v0, /device:TPU:8, one launch (start us, length us, event | category | flops | bytes accessed | tf_op | source)
XLA Modules:
  0.0 332.6 jit_solution(12275307032756212886)
XLA Ops:
  0.6 0.8 pad_maximum_fusion.13
  1.4 0.8 broadcast_in_dim.145
  2.3 8.8 %all-to-all-start = ((bf16[8,2,256,64]{2,3,1,0:T(8,128)(2,1)}), bf16[8,2,256,64]{2,3,1,0:T(8,128)(2,1)S(1)}, u32[]{:S(2)}, u32[]{:S(2)}) async-start(bf16[8,2,256,64]{2,3,1,0:T(8,128)(2,1)} %broadcast_in_dim.145), calls=%async_computation | async-start | bytes 1048576 | tf_op jit(solution)/shard_map/all_to_all | solution.py:20
  11.8 18.8 %all-to-all-done = bf16[8,2,256,64]{2,3,1,0:T(8,128)(2,1)S(1)} async-done(((bf16[8,2,256,64]{2,3,1,0:T(8,128)(2,1)}), bf16[8,2,256,64]{2,3,1,0:T(8,128)(2,1)S(1)}, u32[]{:S(2)}, u32[]{:S(2)}) %all-to-all-start) | async-done | bytes 524320 | tf_op jit(solution)/shard_map/all_to_all | solution.py:20
  30.7 0.8 broadcast_in_dim.146
  31.5 12.4 %all-to-all-start.1 = ((bf16[64,8,386]{2,1,0:T(8,128)(2,1)}), bf16[64,8,386]{2,1,0:T(8,128)(2,1)S(1)}, u32[]{:S(2)}, u32[]{:S(2)}) async-start(bf16[64,8,386]{2,1,0:T(8,128)(2,1)} %broadcast_in_dim.146), calls=%async_computation.1 | async-start | bytes 1048576 | tf_op jit(solution)/shard_map/all_to_all | solution.py:20
  45.9 16.2 %all-to-all-done.1 = bf16[64,8,386]{2,1,0:T(8,128)(2,1)S(1)} async-done(((bf16[64,8,386]{2,1,0:T(8,128)(2,1)}), bf16[64,8,386]{2,1,0:T(8,128)(2,1)S(1)}, u32[]{:S(2)}, u32[]{:S(2)}) %all-to-all-start.1) | async-done | bytes 395296 | tf_op jit(solution)/shard_map/all_to_all | solution.py:20
  63.8 1.2 reduce-window.38
  68.4 0.7 fusion.97
  69.4 1.9 all-gather.6
  72.5 14.6 %all-gather.7 = f32[4,257,64]{1,2,0:T(8,128)S(1)} all-gather(f32[1,257,64]{1,2,0:T(8,128)S(1)} %maximum_bitcast_fusion.1), channel_id=3, replica_groups=mesh['seq_0'=8,'seq_1'=4,'seq_2'=2,'chan'=8] {'seq_1'}, dimensions={0}, use_global_device_ids=true | all-gather | bytes 328960 | tf_op jit(solution)/shard_map/all_gather | solution.py:43
  89.4 26.4 %all-gather.8 = f32[8,257,64]{1,2,0:T(8,128)S(1)} all-gather(f32[1,257,64]{1,2,0:T(8,128)S(1)} %maximum_bitcast_fusion.2), channel_id=4, replica_groups=mesh['seq_0'=8,'seq_1'=4,'seq_2'=2,'chan'=8] {'seq_0'}, dimensions={0}, use_global_device_ids=true | all-gather | bytes 592128 | tf_op jit(solution)/shard_map/all_gather | solution.py:43
  115.8 0.8 fusion.90
  116.9 0.7 fusion.93
  118.6 1.4 fusion.83
  120.1 0.7 copy-done.13
  120.9 0.7 copy-done.12
  121.8 0.7 copy-done.11
  122.8 0.9 copy.403
  123.8 1.6 copy.404
  125.4 0.7 copy.449
  126.1 1.0 slice_reduce_fusion.13
  132.2 1.0 copy.405
  133.1 0.7 copy.406
  134.0 0.8 copy.407
  134.8 0.8 copy.408
  135.7 0.8 copy.409
  136.4 1.6 copy.410
  138.8 1.6 add_add_fusion
  140.4 0.8 copy.411
  141.4 1.8 all-gather.3
  143.2 8.1 %all-gather.5 = f32[8,1,2]{2,1,0:T(1,128)S(1)} all-gather(f32[2,1,2]{2,1,0:T(1,128)S(1)} %get-tuple-element.340), channel_id=7, replica_groups=mesh['seq_0'=8,'seq_1'=4,'seq_2'=2,'chan'=8] {'seq_1'}, dimensions={0}, use_global_device_ids=true | all-gather | bytes 80 | tf_op jit(solution)/shard_map/all_gather | solution.py:72
  151.4 2.0 all-gather.4
  153.5 15.7 %all_gather.55 = f32[4,2,2,64,64]{4,3,2,1,0:T(8,128)S(1)} all-gather(f32[1,2,2,64,64]{4,3,2,1,0:T(8,128)S(1)} %bitcast_add_fusion.5), channel_id=1, replica_groups=mesh['seq_0'=8,'seq_1'=4,'seq_2'=2,'chan'=8] {'seq_1'}, dimensions={0}, use_global_device_ids=true | all-gather | bytes 327680 | tf_op jit(solution)/shard_map/all_gather | solution.py:72
  169.3 26.7 %all_gather.56 = f32[8,2,2,64,64]{4,3,2,1,0:T(8,128)S(1)} all-gather(f32[1,2,2,64,64]{4,3,2,1,0:T(8,128)S(1)} %multiply_add_fusion), channel_id=1, replica_groups=mesh['seq_0'=8,'seq_1'=4,'seq_2'=2,'chan'=8] {'seq_0'}, dimensions={0}, use_global_device_ids=true | all-gather | bytes 589824 | tf_op jit(solution)/shard_map/all_gather | solution.py:72
  196.0 14.0 %all_gather.52 = f32[8,2,2]{2,1,0:T(2,128)S(1)} all-gather(f32[1,2,2]{2,1,0:T(2,128)S(1)} %bitcast.364), channel_id=1, replica_groups=mesh['seq_0'=8,'seq_1'=4,'seq_2'=2,'chan'=8] {'seq_0'}, dimensions={0}, use_global_device_ids=true | all-gather | bytes 144 | tf_op jit(solution)/shard_map/all_gather | solution.py:72
  211.1 1.2 reduce-window.40
  212.9 1.0 fusion.4
  213.9 1.4 fusion.100
  215.5 1.1 multiply_reduce_fusion.1
  216.6 0.7 exponential_multiply_fusion
  217.3 0.7 multiply_reduce_fusion.5
  218.6 1.0 convolution_bitcast_fusion.5
  219.7 2.7 fusion.14
  222.5 5.0 %reduce-window.42 = f32[2,2,2,128]{3,2,1,0:T(2,128)S(1)} reduce-window(f32[2,2,2,128]{3,2,1,0:T(2,128)S(1)} %reshape.563, f32[]{:T(128)} %constant.103.clone.1), window={size=1x1x1x128 pad=0_0x0_0x0_0x0_127}, to_apply=%region_10.11 | reduce-window | flops 130048 | bytes 8196 | tf_op jit(solution)/shard_map/reduce-window.4
  228.9 2.9 broadcast_multiply_fusion
  231.8 0.7 copy-done.55
  233.2 0.7 copy-done.64
  235.3 8.7 %all-to-all-start.5 = ((f32[64,1,10]{2,1,0:T(1,128)}), f32[64,1,10]{2,1,0:T(1,128)}, u32[]{:S(2)}, u32[]{:S(2)}) async-start(f32[64,1,10]{2,1,0:T(1,128)} %broadcast_in_dim.155), calls=%async_computation.5 | async-start | bytes 65536 | tf_op jit(solution)/shard_map/all_to_all | solution.py:20
  244.7 1.1 convolution_bitcast_fusion.6
  247.7 1.4 convolution_bitcast_fusion.3
  249.8 0.7 copy-done.10
  250.6 0.8 copy-done.4
  251.9 0.7 convolution_bitcast_fusion.2
  252.9 1.3 maximum_multiply_fusion
  254.2 10.9 %all-to-all-start.3 = ((f32[64,8,386]{2,1,0:T(8,128)}), f32[64,8,386]{2,1,0:T(8,128)S(1)}, u32[]{:S(2)}, u32[]{:S(2)}) async-start(f32[64,8,386]{2,1,0:T(8,128)} %maximum_multiply_fusion), calls=%async_computation.3 | async-start | bytes 2097152 | tf_op jit(solution)/shard_map/all_to_all | solution.py:89
  265.5 0.7 convolution_add_fusion
  266.6 1.0 copy.418
  267.7 26.5 %all-to-all-done.3 = f32[64,8,386]{2,1,0:T(8,128)S(1)} async-done(((f32[64,8,386]{2,1,0:T(8,128)}), f32[64,8,386]{2,1,0:T(8,128)S(1)}, u32[]{:S(2)}, u32[]{:S(2)}) %all-to-all-start.3) | async-done | bytes 790560 | tf_op jit(solution)/shard_map/all_to_all | solution.py:89
  294.1 3.5 %all-to-all-start.2 = ((f32[8,256,64]{1,2,0:T(8,128)}), f32[8,256,64]{1,2,0:T(8,128)S(1)}, u32[]{:S(2)}, u32[]{:S(2)}) async-start(f32[8,256,64]{1,2,0:T(8,128)} %bitcast.99), calls=%async_computation.2 | async-start | bytes 1048576 | tf_op jit(solution)/shard_map/all_to_all | solution.py:89
  297.6 0.8 reduce_sum.197
  299.2 18.7 %all-to-all-done.2 = f32[8,256,64]{1,2,0:T(8,128)S(1)} async-done(((f32[8,256,64]{1,2,0:T(8,128)}), f32[8,256,64]{1,2,0:T(8,128)S(1)}, u32[]{:S(2)}, u32[]{:S(2)}) %all-to-all-start.2) | async-done | bytes 524320 | tf_op jit(solution)/shard_map/all_to_all | solution.py:89
  318.5 3.3 %all-to-all-start.4 = ((f32[8,8,128]{2,1,0:T(8,128)}), f32[8,8,128]{2,1,0:T(8,128)S(1)}, u32[]{:S(2)}, u32[]{:S(2)}) async-start(f32[8,8,128]{2,1,0:T(8,128)} %broadcast_in_dim.154), calls=%async_computation.4 | async-start | bytes 65536 | tf_op jit(solution)/shard_map/all_to_all | solution.py:20
  325.1 6.9 %all-to-all-done.4 = f32[8,8,128]{2,1,0:T(8,128)S(1)} async-done(((f32[8,8,128]{2,1,0:T(8,128)}), f32[8,8,128]{2,1,0:T(8,128)S(1)}, u32[]{:S(2)}, u32[]{:S(2)}) %all-to-all-start.4) | async-done | bytes 32800 | tf_op jit(solution)/shard_map/all_to_all | solution.py:20
  (297 shorter events, 35.7 us)
Async XLA Ops:
  2.3 8.8 %copy-start.79 = (bf16[8,2]{0,1:T(2,128)(2,1)S(1)}, bf16[8,2]{0,1:T(2,128)(2,1)}, u32[]{:S(2)}) copy-start(bf16[8,2]{0,1:T(2,128)(2,1)} %param.12) | copy-start | bytes 100
  2.3 8.9 %copy-start.67 = (bf16[8,128]{1,0:T(8,128)(2,1)S(1)}, bf16[8,128]{1,0:T(8,128)(2,1)}, u32[]{:S(2)}) copy-start(bf16[8,128]{1,0:T(8,128)(2,1)} %param.11) | copy-start | bytes 6148
  2.3 28.4 %all-to-all-start = ((bf16[8,2,256,64]{2,3,1,0:T(8,128)(2,1)}), bf16[8,2,256,64]{2,3,1,0:T(8,128)(2,1)S(1)}, u32[]{:S(2)}, u32[]{:S(2)}) async-start(bf16[8,2,256,64]{2,3,1,0:T(8,128)(2,1)} %broadcast_in_dim.145), calls=%async_computation | async-start | bytes 1048576 | tf_op jit(solution)/shard_map/all_to_all | solution.py:20
  11.1 0.7 copy-start.66
  31.5 30.6 %all-to-all-start.1 = ((bf16[64,8,386]{2,1,0:T(8,128)(2,1)}), bf16[64,8,386]{2,1,0:T(8,128)(2,1)S(1)}, u32[]{:S(2)}, u32[]{:S(2)}) async-start(bf16[64,8,386]{2,1,0:T(8,128)(2,1)} %broadcast_in_dim.146), calls=%async_computation.1 | async-start | bytes 1048576 | tf_op jit(solution)/shard_map/all_to_all | solution.py:20
  44.7 17.9 %copy-start.54 = (f32[2,2]{1,0:T(2,128)}, f32[2,2]{1,0:T(2,128)S(1)}, u32[]{:S(2)}) copy-start(f32[2,2]{1,0:T(2,128)S(1)} %neg.31) | copy-start | bytes 52
  45.6 16.5 %copy-start.3 = (bf16[1,256,512]{2,1,0:T(8,128)(2,1)}, bf16[1,256,512]{2,1,0:T(8,128)(2,1)S(1)}, u32[]{:S(2)}) copy-start(bf16[1,256,512]{2,1,0:T(8,128)(2,1)S(1)} %copy.386) | copy-start | bytes 786436
  45.9 16.2 %copy-start.15 = (bf16[1,256,512]{2,1,0:T(8,128)(2,1)}, bf16[1,256,512]{2,1,0:T(8,128)(2,1)S(1)}, u32[]{:S(2)}) copy-start(bf16[1,256,512]{2,1,0:T(8,128)(2,1)S(1)} %rev.9) | copy-start | bytes 786436
  63.2 4.3 %copy-start.31 = (f32[2,256,2]{1,2,0:T(2,128)}, f32[2,256,2]{1,2,0:T(2,128)S(1)}, u32[]{:S(2)}) copy-start(f32[2,256,2]{1,2,0:T(2,128)S(1)} %get-tuple-element.287) | copy-start | bytes 12292
  66.4 1.6 copy-start.29
  66.9 0.7 copy-start.5
  71.3 1.2 copy-start.1
  72.2 15.3 %copy-start.42 = (f32[2,2]{1,0:T(2,128)}, f32[2,2]{1,0:T(2,128)S(1)}, u32[]{:S(2)}) copy-start(f32[2,2]{1,0:T(2,128)S(1)} %mul.732) | copy-start | bytes 52
  87.3 1.7 copy-start.44
  87.4 1.5 copy-start.46
  87.5 1.3 copy-start.48
  115.8 1.0 copy-start
  116.9 1.0 copy-start.2
  118.6 1.4 copy-start.14
  120.0 0.8 copy-start.13
  120.8 0.8 copy-start.12
  121.7 0.8 copy-start.11
  122.7 2.6 slice-start
  132.2 1.0 copy-start.20
  133.1 0.8 copy-start.19
  134.0 0.8 copy-start.18
  134.8 0.8 copy-start.17
  136.4 1.8 copy-start.7
  138.0 0.7 copy-start.74
  138.0 0.7 copy-start.71
  138.1 0.7 copy-start.59
  138.1 0.7 copy-start.51
  140.4 1.0 copy-start.6
  141.4 10.0 %copy-start.21 = (f32[1,2,64,64]{3,2,1,0:T(8,128)S(1)}, f32[1,2,64,64]{3,2,1,0:T(8,128)}, u32[]{:S(2)}) copy-start(f32[1,2,64,64]{3,2,1,0:T(8,128)} %get-tuple-element.313) | copy-start | bytes 98308
  141.4 10.0 %copy-start.22 = (f32[1,2,64,64]{3,2,1,0:T(8,128)S(1)}, f32[1,2,64,64]{3,2,1,0:T(8,128)}, u32[]{:S(2)}) copy-start(f32[1,2,64,64]{3,2,1,0:T(8,128)} %get-tuple-element.351) | copy-start | bytes 98308
  210.4 0.7 copy-start.38
  212.9 4.4 %copy-start.26 = (f32[2,2,256]{2,1,0:T(2,128)}, f32[2,2,256]{2,1,0:T(2,128)S(1)}, u32[]{:S(2)}) copy-start(f32[2,2,256]{2,1,0:T(2,128)S(1)} %reduce_window_sum.76) | copy-start | bytes 12292
  218.6 1.0 copy-start.23
  218.6 1.0 copy-start.27
  219.7 2.7 copy-start.34
  219.7 2.7 copy-start.36
  219.7 2.7 copy-start.41
  219.7 2.7 copy-start.57
  219.7 2.7 copy-start.58
  222.4 5.8 %copy-start.24 = (pred[256,256]{1,0:T(8,128)(4,1)S(1)}, pred[256,256]{1,0:T(8,128)(4,1)}, u32[]{:S(2)}) copy-start(pred[256,256]{1,0:T(8,128)(4,1)} %iota_compare_fusion) | copy-start | bytes 196612
  228.2 0.7 copy-start.28
  228.2 0.7 copy-start.32
  228.9 2.9 copy-start.62
  235.3 8.7 %copy-start.76 = (f32[2]{0:T(128)S(1)}, f32[2]{0:T(128)}, u32[]{:S(2)}) copy-start(f32[2]{0:T(128)} %param.17) | copy-start | bytes 28
  235.3 19.0 %all-to-all-start.5 = ((f32[64,1,10]{2,1,0:T(1,128)}), f32[64,1,10]{2,1,0:T(1,128)}, u32[]{:S(2)}, u32[]{:S(2)}) async-start(f32[64,1,10]{2,1,0:T(1,128)} %broadcast_in_dim.155), calls=%async_computation.5 | async-start | bytes 65536 | tf_op jit(solution)/shard_map/all_to_all | solution.py:20
  245.7 0.9 copy-start.9
  246.6 1.0 copy-start.8
  246.6 1.0 copy-start.25
  246.6 1.0 copy-start.40
  247.7 1.5 copy-start.30
  247.7 1.5 copy-start.77
  249.5 1.0 copy-start.10
  249.8 0.7 copy-start.78
  250.5 1.0 copy-start.4
  250.5 1.0 copy-start.16
  250.5 1.0 copy-start.56
  254.2 39.9 %all-to-all-start.3 = ((f32[64,8,386]{2,1,0:T(8,128)}), f32[64,8,386]{2,1,0:T(8,128)S(1)}, u32[]{:S(2)}, u32[]{:S(2)}) async-start(f32[64,8,386]{2,1,0:T(8,128)} %maximum_multiply_fusion), calls=%async_computation.3 | async-start | bytes 2097152 | tf_op jit(solution)/shard_map/all_to_all | solution.py:89
  294.1 23.8 %all-to-all-start.2 = ((f32[8,256,64]{1,2,0:T(8,128)}), f32[8,256,64]{1,2,0:T(8,128)S(1)}, u32[]{:S(2)}, u32[]{:S(2)}) async-start(f32[8,256,64]{1,2,0:T(8,128)} %bitcast.99), calls=%async_computation.2 | async-start | bytes 1048576 | tf_op jit(solution)/shard_map/all_to_all | solution.py:89
  318.5 13.4 %all-to-all-start.4 = ((f32[8,8,128]{2,1,0:T(8,128)}), f32[8,8,128]{2,1,0:T(8,128)S(1)}, u32[]{:S(2)}, u32[]{:S(2)}) async-start(f32[8,8,128]{2,1,0:T(8,128)} %broadcast_in_dim.154), calls=%async_computation.4 | async-start | bytes 65536 | tf_op jit(solution)/shard_map/all_to_all | solution.py:20
  (24 other events, 16.0 us)
where the time goes:
time: 334 us; the launch traced here: 333 us
  blocking collectives  111 us (33%)
  waiting for transfers between devices  87 us (26%)
  starting transfers between devices  47.7 us (14%)
  local copies, waits for them, and re-layouts  44.6 us (13%)
  other arithmetic  21 us (6%)
  matrix products  19.4 us (6%)
    all_gather x6, blocking collectives, carried_in_2(): pieces = jax.tree.map(lambda part: lax.all_gather(part, axis), running)  68.3 us
    all_to_all x2, waiting for transfers between devices, summed_on_arrival(): pieces = lax.all_to_all(cut_along(array, dim, size), axis, 0, 0, tiled=True)  45.1 us
    all_gather x3, blocking collectives, all_in_one(): both, at, found = (lax.all_gather(jnp.concatenate(lines), axis), 0, {})  42.9 us
    all_to_all x4, waiting for transfers between devices, copy_for_each(): lax.all_to_all(jnp.broadcast_to(array[None], (size, *array.shape)), axis,...  41.8 us
    all_to_all x4, starting transfers between devices, copy_for_each(): lax.all_to_all(jnp.broadcast_to(array[None], (size, *array.shape)), axis,...  33.3 us
    all_to_all x2, starting transfers between devices, summed_on_arrival(): pieces = lax.all_to_all(cut_along(array, dim, size), axis, 0, 0, tiled=True)  14.4 us
    unnamed x165, local copies, waits for them, and re-layouts  14.2 us
    slice x17, local copies, waits for them, and re-layouts, carried_in(): running = combine(running, jax.tree.map(lambda part: part[k], pieces))  10.8 us
  transfers between devices with their start and end apart: 6, of which 5 were waited for; matrix products, arithmetic and copies ran while one was open for 5% of the time, Pallas kernels for 0%

commit v1 on v0

v1 whole, which is shorter than its diff:
```python
import jax
import jax.numpy as jnp
from jax import lax
from jax.experimental import pallas as pl
from jax.experimental.pallas import tpu as pltpu
from jax.sharding import Mesh
from jax.sharding import PartitionSpec as P

STATE = 64
HEAD = 64
SEQ = ("seq_0", "seq_1", "seq_2")
NN = (((1,), (0,)), ((), ()))
NT = (((1,), (1,)), ((), ()))
TN = (((0,), (0,)), ((), ()))
F32 = jnp.float32
BF16 = jnp.bfloat16
INTERPRET = False


def low(x, y, dims):
    return lax.dot_general(x.astype(BF16), y.astype(BF16), dims, preferred_element_type=F32)


def halves(x):
    top = x.astype(BF16)
    return top, (x - top.astype(F32)).astype(BF16)


def mid(x, y, dims):
    xt, xl = halves(x)
    yt, yl = halves(y)
    return low(xt, yt, dims) + (low(xt, yl, dims) + low(xl, yt, dims))


def exact(x, y, dims):
    return lax.dot_general(
        x, y, dims, precision=lax.Precision.HIGHEST, preferred_element_type=F32
    )


def before(n, flip=False):
    i = lax.broadcasted_iota(jnp.int32, (n, n), 0)
    j = lax.broadcasted_iota(jnp.int32, (n, n), 1)
    return (i >= j if flip else i <= j).astype(F32)


def by_head(x, r, width):
    n = x.shape[1]
    return jnp.concatenate(
        [
            jnp.broadcast_to(x[2 * r : 2 * r + 1], (width // 2, n)),
            jnp.broadcast_to(x[2 * r + 1 : 2 * r + 2], (width // 2, n)),
        ],
        0,
    )


def forward_rows(n):
    return lax.broadcasted_iota(jnp.int32, (8, n), 0) < 2


def sigmoid(x):
    return 1.0 / (1.0 + jnp.exp(-x))


def features(both):
    n = both.shape[0] // 128
    up = [both[128 * k : 128 * k + 64] for k in range(n)]
    down = [both[128 * k + 64 : 128 * k + 128] for k in range(n)]
    return jnp.concatenate(up, 0), jnp.concatenate(down, 0)


def stage_project(both, weights, params):
    width = 128
    n = both.shape[1]
    u, q = features(both)
    pre = lax.dot_general(weights[:, :width], u, TN, preferred_element_type=F32)
    bc = lax.dot_general(weights[:, 128:256], u, TN, preferred_element_type=F32)
    cot = lax.dot_general(weights[:, 256:384], q, TN, preferred_element_type=F32)
    z = lax.dot_general(weights[:, 384:512], u, TN, preferred_element_type=F32)[:8]
    rate, bias = params[:, 0:1], params[:, 1:2]
    v = z + bias
    step = jnp.maximum(v, 0.0) + jnp.log1p(jnp.exp(-jnp.abs(v)))
    slope = sigmoid(v)
    decay = -rate * step
    run = jnp.where(
        forward_rows(n), exact(decay, before(n), NN), exact(decay, before(n, True), NN)
    )
    total = jnp.sum(decay, axis=1, keepdims=True)
    grown = jnp.exp(run)
    tail = jnp.exp(total - run)
    gated = pre * sigmoid(pre)
    b, c = bc[:STATE], bc[STATE:]
    push = step * tail
    pushed = jnp.concatenate([gated * by_head(push, r, width) for r in (0, 1)], 0)
    pulled = jnp.concatenate([cot * by_head(grown, r, width) for r in (0, 1)], 0)
    ps = mid(b, pushed, NT)
    pl_ = mid(c, pulled, NT)
    kept = jnp.broadcast_to(jnp.exp(total), (8, width))
    lane = lax.broadcasted_iota(jnp.int32, (1, width), 1)
    kept = [
        jnp.broadcast_to(
            jnp.where(lane < HEAD, kept[2 * r : 2 * r + 1], kept[2 * r + 1 : 2 * r + 2]),
            (STATE, width),
        )
        for r in (0, 1)
    ]
    sends = [
        ps[:, :width],
        pl_[:, width:],
        pl_[:, :width],
        ps[:, width:],
        kept[0],
        kept[1],
        kept[0],
        kept[1],
    ]
    vec = jnp.concatenate(
        [step, run, grown, tail, slope, jnp.broadcast_to(jnp.exp(total), (8, n))], 0
    )
    return sends, pre, bc, cot, vec


def stage_within(pre, bc, cot, vec, params):
    n = pre.shape[1]
    gated = pre * sigmoid(pre)
    b, c = bc[:STATE], bc[STATE:]
    step, run = vec[0:8], vec[8:16]
    columns = jnp.concatenate([run, jnp.zeros((120, n), F32)], 0).T
    t = lax.broadcasted_iota(jnp.int32, (n, n), 0)
    s = lax.broadcasted_iota(jnp.int32, (n, n), 1)
    later, same = t >= s, t == s
    earlier = t <= s
    scores = mid(c.T, b, NN)
    dscores = jnp.zeros((n, n), F32)
    mixed, dgated = ([], []), ([], [])
    lanes = lax.broadcasted_iota(jnp.int32, (n, 128), 1)
    rows = jnp.zeros((n, 128), F32)
    direct = [None] * 4
    for h in (0, 1):
        x = gated[HEAD * h : HEAD * (h + 1)]
        dy = cot[HEAD * h : HEAD * (h + 1)]
        step0, step1 = step[h : h + 1], step[2 + h : 3 + h]
        up = columns[:, h : h + 1] - run[h : h + 1]
        down = columns[:, 2 + h : 3 + h] - run[2 + h : 3 + h]
        fade = jnp.exp(jnp.where(later, up, down))
        pair = mid(dy.T, x, NN)
        faded = scores * fade
        moved = faded * pair
        scaled = fade * jnp.where(later, step0, step1) + jnp.where(same, step1, 0.0)
        dscores = dscores + scaled * pair
        for r, (mask, st) in enumerate(((later, step0), (earlier, step1))):
            part = jnp.where(mask, moved, 0.0)
            mix = jnp.where(mask, faded, 0.0) * st
            mixed[r].append(mid(x, mix, NT))
            dgated[r].append(mid(dy, mix, NN))
            direct[2 * r + h] = jnp.sum(part, axis=0, keepdims=True)
            rows = jnp.where(
                lanes == 2 * r + h, jnp.sum(part * st, axis=1, keepdims=True), rows
            )
    direct = jnp.concatenate(direct + [jnp.zeros((4, n), F32)], 0)
    drun = rows.T[:8] - step * direct
    gains = jnp.concatenate(
        [jnp.broadcast_to(params[h : h + 1, 2:3], (HEAD, n)) for h in (0, 1)], 0
    )
    mixed = jnp.concatenate([jnp.concatenate(m, 0) + gains * gated for m in mixed], 0)
    dgated = jnp.concatenate([jnp.concatenate(d, 0) + gains * cot for d in dgated], 0)
    both = gated * cot
    dskip = [
        2.0 * jnp.sum(both[HEAD * h : HEAD * (h + 1)], axis=0, keepdims=True) for h in (0, 1)
    ]
    dbc = jnp.concatenate([mid(c, dscores, NN), mid(b, dscores, NT)], 0)
    extra = jnp.concatenate([direct, drun] + dskip + [jnp.zeros((6, n), F32)], 0)
    return mixed, dgated, dbc, extra


def stage_finish(both, weights, params, pre, bc, cot, vec, mixed, dgated, dbc, extra, carried):
    width = 128
    n = pre.shape[1]
    u, q = features(both)
    sig = sigmoid(pre)
    gated = pre * sig
    b, c = bc[:STATE], bc[STATE:]
    step, grown, tail, slope = vec[0:8], vec[16:24], vec[24:32], vec[32:40]
    kept = vec[40:48, 0:1]
    rate = params[:, 0:1]
    h0, g1, g0, h1 = carried
    start = jnp.concatenate([h0, h1], 1)
    end = jnp.concatenate([g0, g1], 1)
    reach = mid(start.T, c, NN)
    pull = mid(end.T, b, NN)
    gains, falls, pushed, pulled = [], [], [], []
    dpre, lower = [], []
    bend = sig * (1.0 + pre * (1.0 - sig))
    for r in (0, 1):
        grow, tails, steps = (by_head(v, r, width) for v in (grown, tail, step))
        here = slice(width * r, width * (r + 1))
        got = reach[here] * grow
        lower.append((mixed[here] + got).astype(BF16))
        back = pull[here] * tails
        dpre.append(((dgated[here] + steps * back) * bend).astype(BF16))
        gain, fall = cot * got, gated * back
        for h in (0, 1):
            gains.append(jnp.sum(gain[HEAD * h : HEAD * (h + 1)], axis=0, keepdims=True))
            falls.append(jnp.sum(fall[HEAD * h : HEAD * (h + 1)], axis=0, keepdims=True))
        pulled.append(cot * grow)
        pushed.append(gated * steps * tails)
    none = [jnp.zeros((4, n), F32)]
    gains = jnp.concatenate(gains + none, 0)
    falls = jnp.concatenate(falls + none, 0)
    pulled = jnp.concatenate(pulled, 0)
    pushed = jnp.concatenate(pushed, 0)
    dbc = dbc + jnp.concatenate([mid(end, pushed, NN), mid(start, pulled, NN)], 0)
    lost = step * falls
    drun = extra[8:16] + gains - lost
    overlap = jnp.sum(start * end, axis=0, keepdims=True)
    lane = lax.broadcasted_iota(jnp.int32, (1, 2 * width), 1)
    ends = [
        jnp.sum(jnp.where(lane // HEAD == k, overlap, 0.0), axis=1, keepdims=True)
        for k in range(4)
    ]
    ends = jnp.concatenate(ends + [jnp.zeros((4, 1), F32)], 0)
    ends = kept * ends + jnp.sum(lost, axis=1, keepdims=True)
    ddecay = ends + jnp.where(
        forward_rows(n), exact(drun, before(n, True), NN), exact(drun, before(n), NN)
    )
    dstep = extra[0:8] + falls - rate * ddecay
    valid = lax.broadcasted_iota(jnp.int32, (8, n), 0) < 4
    dz = jnp.where(valid, dstep * slope, 0.0)
    drate = -jnp.sum(ddecay * step, axis=1, keepdims=True)
    dbias = jnp.sum(dz, axis=1, keepdims=True)
    dskip = jnp.sum(extra[16:24], axis=1, keepdims=True)
    dzs = jnp.concatenate([dz, jnp.zeros((120, n), F32)], 0).astype(BF16)
    dbcs = halves(dbc) if FINE else (dbc.astype(BF16),)
    front, inside = weights[:, :width], weights[:, 128:256]
    dinput = low(jnp.concatenate([front, front], 1), jnp.concatenate(dpre, 0), NN)
    dinput = dinput + low(
        jnp.concatenate([weights[:, 384:512]] + [inside] * len(dbcs), 1),
        jnp.concatenate([dzs, *dbcs], 0),
        NN,
    )
    dfront = low(u, dpre[0], NT) + low(u, dpre[1], NT)
    rest = low(u, jnp.concatenate([dbcs[0], dzs], 0), NT)
    dinside = rest[:, :width] + (low(u, dbcs[1], NT) if FINE else 0.0)
    dout = low(q, lower[0], NT) + low(q, lower[1], NT)
    lane = lax.broadcasted_iota(jnp.int32, (1, width), 1)
    numbers = jnp.zeros((1, width), F32)
    for k in range(4):
        numbers = jnp.where(lane == 8 + k, drate[k : k + 1], numbers)
        numbers = jnp.where(lane == 12 + k, dbias[k : k + 1], numbers)
    for k in range(2):
        numbers = jnp.where(lane == 16 + k, dskip[k : k + 1], numbers)
    rough = numbers.astype(BF16).astype(F32)
    fine = pltpu_roll(numbers - rough, 32)
    last = rest[:, width:] + jnp.broadcast_to(rough + fine, (u.shape[0], width))
    grads = jnp.concatenate([dfront, dinside, dout, last], 1)
    return dinput.astype(BF16), grads.astype(BF16)


def pltpu_roll(x, by):
    wide = jnp.broadcast_to(x, (8, x.shape[1]))
    return (jnp.roll(wide, by, 1) if PLAIN else pltpu.roll(wide, by, 1))[:1]


PLAIN = False
FINE = True


def call(fn, outs, args, flops):
    def kernel(*refs):
        ins, results = refs[: len(args)], refs[len(args) :]
        fn(ins, results)

    size = sum(a.size * a.dtype.itemsize for a in args)
    return pl.pallas_call(
        kernel,
        out_shape=[jax.ShapeDtypeStruct(s, d) for s, d in outs],
        cost_estimate=pl.CostEstimate(flops=flops, bytes_accessed=size, transcendentals=0),
        interpret=INTERPRET,
    )(*args)


def project(both, weights, params):
    if PLAIN:
        sends, *rest = stage_project(both, weights, params)
        return (jnp.stack(sends, 1).reshape(512, 128), *rest)

    def fn(ins, outs):
        sends, *rest = stage_project(*(r[...] for r in ins))
        for j, part in enumerate(sends):
            outs[0][pl.ds(j, STATE, stride=8), :] = part
        for ref, value in zip(outs[1:], rest):
            ref[...] = value

    n = both.shape[1]
    outs = [((512, 128), F32), ((128, n), F32), ((128, n), F32), ((128, n), F32), ((48, n), F32)]
    return call(fn, outs, (both, weights, params), 300_000_000)


def within(pre, bc, cot, vec, params):
    if PLAIN:
        return stage_within(pre, bc, cot, vec, params)

    def fn(ins, outs):
        for ref, value in zip(outs, stage_within(*(r[...] for r in ins))):
            ref[...] = value

    n = pre.shape[1]
    outs = [((256, n), F32), ((256, n), F32), ((128, n), F32), ((24, n), F32)]
    return call(fn, outs, (pre, bc, cot, vec, params), 300_000_000)


def finish(both, weights, params, pre, bc, cot, vec, mixed, dgated, dbc, extra, back):
    args = (both, weights, params, pre, bc, cot, vec, mixed, dgated, dbc, extra)
    if PLAIN:
        rows = back.reshape(64, 8, 128)
        return stage_finish(*args, [rows[:, j] for j in range(4)])

    def fn(ins, outs):
        carried = [ins[-1][pl.ds(j, STATE, stride=8), :] for j in range(4)]
        values = stage_finish(*(r[...] for r in ins[:-1]), carried)
        for ref, value in zip(outs, values):
            ref[...] = value

    n = pre.shape[1]
    outs = [((512, n), BF16), ((512, 512), BF16)]
    return call(fn, outs, (*args, back), 600_000_000)


def carry(blocks):
    count = blocks.shape[0] // 8
    if PLAIN:
        parts = blocks.reshape(count, 8, 128)
        kept, added = parts[:, 4:], parts[:, :4]
        up, down = [], []
        run = jnp.zeros((4, 128), F32)
        for k in range(count):
            up.append(run)
            run = kept[k] * run + added[k]
        run = jnp.zeros((4, 128), F32)
        for k in reversed(range(count)):
            down.append(run)
            run = kept[k] * run + added[k]
        up, down = jnp.stack(up), jnp.stack(down[::-1])
        out = jnp.concatenate([up[:, :2], down[:, 2:], jnp.zeros((count, 4, 128), F32)], 1)
        return out.reshape(-1, 128)

    def fn(ins, outs):
        src, dst = ins[0], outs[0]
        dst[...] = jnp.zeros(dst.shape, F32)
        up = jnp.zeros((2, 128), F32)
        down = jnp.zeros((2, 128), F32)
        for k in range(count):
            m = count - 1 - k
            dst[8 * k : 8 * k + 2, :] = up
            dst[8 * m + 2 : 8 * m + 4, :] = down
            up = src[8 * k + 4 : 8 * k + 6, :] * up + src[8 * k : 8 * k + 2, :]
            down = src[8 * m + 6 : 8 * m + 8, :] * down + src[8 * m + 2 : 8 * m + 4, :]

    return call(fn, [((8 * count, 128), F32)], (blocks,), 1_000_000)[0]


def exchange(array, axis):
    return lax.all_to_all(array, axis, 0, 0, tiled=True)


def to_all(array, axis):
    return exchange(jnp.broadcast_to(array[None], (lax.axis_size(axis), *array.shape)), axis)


def body(
    tokens, out_grad, in_weight, dt_weight, bc_weight, out_weight, decay_rate, dt_bias, skip_gain
):
    seq_count = lax.axis_size(SEQ)
    tok_rows = tokens.shape[0]
    width = in_weight.shape[1]
    heads = dt_weight.shape[1]
    scale = (tok_rows * seq_count) ** (-0.5)
    own = jnp.concatenate([tokens.T, out_grad.T], 0)
    both = to_all(own, "chan").reshape(-1, tok_rows)
    packed = jnp.concatenate(
        [
            in_weight,
            bc_weight,
            out_weight.T,
            dt_weight,
            dt_weight,
            jnp.zeros((in_weight.shape[0], 128 - 2 * heads), BF16),
        ],
        1,
    )
    weights = to_all(packed, SEQ).reshape(-1, 512)
    params = jnp.stack(
        [decay_rate.reshape(-1), dt_bias.reshape(-1), jnp.tile(skip_gain, 2)], 1
    )
    params = jnp.pad(params, ((0, 4), (0, 125)))
    sums, pre, bc, cot, vec = project(both, weights, params)
    sums = exchange(sums.reshape(64, 8, 128), SEQ).reshape(512, 128)
    mixed, dgated, dbc, extra = within(pre, bc, cot, vec, params)
    back = exchange(carry(sums).reshape(64, 8, 128), SEQ).reshape(512, 128)
    dinput, grads = finish(
        both, weights, params, pre, bc, cot, vec, mixed, dgated, dbc, extra, back
    )
    grads = exchange(grads.reshape(64, 8, 512), SEQ)
    summed = jnp.sum(grads.astype(F32), axis=0)
    parts = exchange(dinput.reshape(8, 64, tok_rows), "chan")
    tokens_grad = jnp.sum(parts.astype(F32), axis=0).astype(BF16).T
    in_weight_grad = scale * summed[:, :width]
    bc_weight_grad = scale * jnp.sum(to_all(summed[:, 128:256], "chan"), axis=0)
    out_weight_grad = scale * summed[:, 256:384].T
    dt_weight_grad = scale * (summed[:, 384:386] + summed[:, 386:388])
    numbers = summed[0, 392:402] + summed[0, 424:434]
    rate_grad = scale * decay_rate * numbers[:4].reshape(2, 2)
    bias_grad = scale * numbers[4:8].reshape(2, 2)
    skip_grad = scale * numbers[8:10]
    return (
        tokens_grad,
        in_weight_grad,
        dt_weight_grad,
        bc_weight_grad,
        out_weight_grad,
        rate_grad,
        bias_grad,
        skip_grad,
    )


def solution(mesh):
    split = Mesh(
        mesh.devices.reshape(8, 4, 2, mesh.shape["chan"]), ("seq_0", "seq_1", "seq_2", "chan")
    )
    return jax.shard_map(
        body,
        mesh=split,
        in_specs=(
            P(SEQ, "chan"),
            P(SEQ, "chan"),
            P(SEQ, "chan"),
            P(SEQ, "chan"),
            P(SEQ, None),
            P("chan", SEQ),
            P(None, "chan"),
            P(None, "chan"),
            P("chan"),
        ),
        out_specs=(
            P(SEQ, "chan"),
            P(SEQ, "chan"),
            P(SEQ, "chan"),
            P(SEQ, None),
            P("chan", SEQ),
            P(None, "chan"),
            P(None, "chan"),
            P("chan"),
        ),
        check_vma=False,
    )
```

time: 334 us -> 166 us (0.50)
  the two profiles are of different devices: /device:TPU:8 before, /device:TPU:1 now
where the time goes in v1:
time: 166 us
  waiting for transfers between devices  66 us (40%)
  starting transfers between devices  41.4 us (25%)
  blocking collectives  33 us (20%)
  Pallas kernels  12.1 us (7%)
  local copies, waits for them, and re-layouts  7.58 us (5%)
  other arithmetic  4.8 us (3%)
    all_to_all x5, waiting for transfers between devices, exchange(): return lax.all_to_all(array, axis, 0, 0, tiled=True)  66 us
    all_to_all x5, starting transfers between devices, exchange(): return lax.all_to_all(array, axis, 0, 0, tiled=True)  41.4 us
    all_to_all x2, blocking collectives, exchange(): return lax.all_to_all(array, axis, 0, 0, tiled=True)  33 us
    pallas_call x4, Pallas kernels, call(): pl.pallas_call(kernel, out_shape=[jax.ShapeDtypeStruct(s, d) for s, d in...  12.1 us
    unnamed x22, local copies, waits for them, and re-layouts  4.21 us
  transfers between devices with their start and end apart: 5, of which 5 were waited for; matrix products, arithmetic and copies ran while one was open for 2% of the time, Pallas kernels for 2%

profile of v1, /device:TPU:1, one launch (start us, length us, event | category | flops | bytes accessed | tf_op | source)
XLA Modules:
  0.0 165.6 jit_solution(3542610203999736275)
XLA Ops:
  0.6 0.8 pad_maximum_fusion
  1.4 0.8 broadcast_in_dim.8
  2.2 0.0 copy-start.8
  2.2 10.2 %all-to-all-start = ((bf16[8,128,256]{2,1,0:T(8,128)(2,1)}), bf16[8,128,256]{2,1,0:T(8,128)(2,1)S(1)}, u32[]{:S(2)}, u32[]{:S(2)}) async-start(bf16[8,128,256]{2,1,0:T(8,128)(2,1)} %broadcast_in_dim.8), calls=%async_computation | async-start | bytes 1048576 | tf_op jit(solution)/shard_map/all_to_all | solution.py:364
  12.5 0.0 copy-done.8
  12.5 0.0 copy-start.6
  12.5 0.1 copy.23
  12.6 0.0 copy-start.4
  12.6 0.0 copy-start.5
  12.6 0.6 copy-done.6
  13.2 0.1 copy-done.4
  13.3 0.0 copy-done.5
  13.3 0.1 concatenate.7
  13.4 14.2 %all-to-all-done = bf16[8,128,256]{2,1,0:T(8,128)(2,1)S(1)} async-done(((bf16[8,128,256]{2,1,0:T(8,128)(2,1)}), bf16[8,128,256]{2,1,0:T(8,128)(2,1)S(1)}, u32[]{:S(2)}, u32[]{:S(2)}) %all-to-all-start) | async-done | bytes 524320 | tf_op jit(solution)/shard_map/all_to_all | solution.py:364
  27.5 0.0 copy-start
  27.5 0.9 broadcast_in_dim.10
  28.4 0.0 copy-start.9
  28.4 0.1 copy-done
  28.5 16.6 %all-to-all-start.1 = ((bf16[64,8,512]{2,1,0:T(8,128)(2,1)}), bf16[64,8,512]{2,1,0:T(8,128)(2,1)S(1)}, u32[]{:S(2)}, u32[]{:S(2)}) async-start(bf16[64,8,512]{2,1,0:T(8,128)(2,1)} %broadcast_in_dim.10), calls=%async_computation.1 | async-start | bytes 1048576 | tf_op jit(solution)/shard_map/all_to_all | solution.py:364
  45.1 0.0 copy-done.9
  45.1 0.0 copy-start.7
  45.2 0.1 stack_tile.4
  45.2 0.6 copy-done.7
  45.8 0.0 copy-start.3
  45.8 0.1 stack_reshape.9
  45.9 0.6 copy-done.3
  46.5 0.1 stack_reshape.8
  46.6 0.7 select_maximum_fusion.refs_2_.refs_4_
  47.3 16.5 %all-to-all-done.1 = bf16[64,8,512]{2,1,0:T(8,128)(2,1)S(1)} async-done(((bf16[64,8,512]{2,1,0:T(8,128)(2,1)}), bf16[64,8,512]{2,1,0:T(8,128)(2,1)S(1)}, u32[]{:S(2)}, u32[]{:S(2)}) %all-to-all-start.1) | async-done | bytes 524320 | tf_op jit(solution)/shard_map/all_to_all | solution.py:364
  63.8 0.0 copy-start.1
  63.8 0.8 copy-done.1
  64.5 2.9 %shard_map.152 = (f32[512,128]{1,0:T(8,128)}, f32[128,256]{1,0:T(8,128)}, f32[128,256]{1,0:T(8,128)}, f32[128,256]{1,0:T(8,128)}, f32[48,256]{1,0:T(8,128)}) custom-call(bf16[1024,256]{1,0:T(8,128)(2,1)} %bitcast.16, bf16[512,512]{1,0:T(8,128)(2,1)} %bitcast.18, f32[8,128]{1,0:T(8,128)} %select_maximum_fusion.refs_2_.refs_4_), custom_call_target="tpu_custom_call" | custom-call | flops 300000000 | bytes 1052672 | tf_op jit(solution)/shard_map/pallas_call | solution.py:275
  67.5 18.7 %all_to_all.35 = f32[64,8,128]{2,1,0:T(8,128)} all-to-all(f32[64,8,128]{2,1,0:T(8,128)} %bitcast.24), channel_id=1, replica_groups=mesh['seq_0'=8,'seq_1'=4,'seq_2'=2,'chan'=8] {'seq_0','seq_1','seq_2'}, dimensions={0} | all-to-all | bytes 524288 | tf_op jit(solution)/shard_map/all_to_all | solution.py:364
  86.2 1.8 %shard_map.154 = f32[512,128]{1,0:T(8,128)} custom-call(f32[512,128]{1,0:T(8,128)} %bitcast.22), custom_call_target="tpu_custom_call" | custom-call | flops 1000000 | bytes 262144 | tf_op jit(solution)/shard_map/pallas_call | solution.py:275
  88.0 4.5 %all-to-all-start.3 = ((f32[64,8,128]{2,1,0:T(8,128)}), f32[64,8,128]{2,1,0:T(8,128)S(1)}, u32[]{:S(2)}, u32[]{:S(2)}) async-start(f32[64,8,128]{2,1,0:T(8,128)} %bitcast.21), calls=%async_computation.3 | async-start | bytes 524288 | tf_op jit(solution)/shard_map/all_to_all | solution.py:364
  92.5 3.4 %shard_map.153 = (f32[256,256]{1,0:T(8,128)}, f32[256,256]{1,0:T(8,128)}, f32[128,256]{1,0:T(8,128)}, f32[24,256]{1,0:T(8,128)}) custom-call(f32[128,256]{1,0:T(8,128)} %get-tuple-element.19.refs_0_.refs_3_, f32[128,256]{1,0:T(8,128)} %get-tuple-element.20.refs_1_.refs_4_, f32[128,256]{1,0:T(8,128)} %get-tuple-element.21.refs_2_.refs_5_, ...), custom_call_target="tpu_custom_call" | custom-call | flops 300000000 | bytes 446464 | tf_op jit(solution)/shard_map/pallas_call | solution.py:275
  95.9 10.2 %all-to-all-done.3 = f32[64,8,128]{2,1,0:T(8,128)S(1)} async-done(((f32[64,8,128]{2,1,0:T(8,128)}), f32[64,8,128]{2,1,0:T(8,128)S(1)}, u32[]{:S(2)}, u32[]{:S(2)}) %all-to-all-start.3) | async-done | bytes 262176 | tf_op jit(solution)/shard_map/all_to_all | solution.py:364
  106.1 0.0 copy-start.2
  106.1 0.7 copy-done.2
  106.8 4.0 %shard_map.155 = (bf16[512,256]{1,0:T(8,128)(2,1)}, bf16[512,512]{1,0:T(8,128)(2,1)}) custom-call(bf16[1024,256]{1,0:T(8,128)(2,1)} %bitcast.17, bf16[512,512]{1,0:T(8,128)(2,1)} %bitcast.19, f32[8,128]{1,0:T(8,128)} %select_maximum_fusion.refs_2_.refs_4_, f32[128,256]{1,0:T(8,128)} %get-tuple-element.19.refs_0_.refs_3_, ...), custom_call_target="tpu_custom_call" | custom-call | flops 600000000 | bytes 2437120 | tf_op jit(solution)/shard_map/pallas_call | solution.py:275
  110.8 14.3 %all_to_all.36 = bf16[8,64,256]{2,1,0:T(8,128)(2,1)S(1)} all-to-all(bf16[8,64,256]{2,1,0:T(8,128)(2,1)} %bitcast.23), channel_id=1, replica_groups=mesh['seq_0'=8,'seq_1'=4,'seq_2'=2,'chan'=8] {'chan'}, dimensions={0} | all-to-all | bytes 524288 | tf_op jit(solution)/shard_map/all_to_all | solution.py:364
  125.1 6.7 %all-to-all-start.5 = ((bf16[64,8,512]{2,1,0:T(8,128)(2,1)}), bf16[64,8,512]{2,1,0:T(8,128)(2,1)S(1)}, u32[]{:S(2)}, u32[]{:S(2)}) async-start(bf16[64,8,512]{2,1,0:T(8,128)(2,1)} %bitcast.11), calls=%async_computation.5 | async-start | bytes 1048576 | tf_op jit(solution)/shard_map/all_to_all | solution.py:364
  131.8 0.7 reduce_sum.30
  132.5 18.0 %all-to-all-done.5 = bf16[64,8,512]{2,1,0:T(8,128)(2,1)S(1)} async-done(((bf16[64,8,512]{2,1,0:T(8,128)(2,1)}), bf16[64,8,512]{2,1,0:T(8,128)(2,1)S(1)}, u32[]{:S(2)}, u32[]{:S(2)}) %all-to-all-start.5) | async-done | bytes 524320 | tf_op jit(solution)/shard_map/all_to_all | solution.py:364
  150.5 0.1 convert_reduce_fusion
  150.6 0.1 slice_add_fusion.1
  150.7 0.1 fusion.1
  150.7 0.6 fusion
  151.3 0.1 multiply_reduce_fusion
  151.4 0.1 slice.45
  151.5 0.6 multiply_multiply_fusion
  152.1 0.6 broadcast_in_dim.11
  152.7 3.3 %all-to-all-start.6 = ((f32[8,8,128]{2,1,0:T(8,128)}), f32[8,8,128]{2,1,0:T(8,128)S(1)}, u32[]{:S(2)}, u32[]{:S(2)}) async-start(f32[8,8,128]{2,1,0:T(8,128)} %broadcast_in_dim.11), calls=%async_computation.6 | async-start | bytes 65536 | tf_op jit(solution)/shard_map/all_to_all | solution.py:364
  156.0 0.6 multiply_bitcast_fusion
  156.6 0.6 mul.42
  157.3 0.6 copy.28
  157.9 7.1 %all-to-all-done.6 = f32[8,8,128]{2,1,0:T(8,128)S(1)} async-done(((f32[8,8,128]{2,1,0:T(8,128)}), f32[8,8,128]{2,1,0:T(8,128)S(1)}, u32[]{:S(2)}, u32[]{:S(2)}) %all-to-all-start.6) | async-done | bytes 32800 | tf_op jit(solution)/shard_map/all_to_all | solution.py:364
  165.0 0.6 broadcast_multiply_fusion
  (3 shorter events, 0.0 us)
Async XLA Ops:
  2.2 10.2 %copy-start.8 = (bf16[8,2]{0,1:T(2,128)(2,1)S(1)}, bf16[8,2]{0,1:T(2,128)(2,1)}, u32[]{:S(2)}) copy-start(bf16[8,2]{0,1:T(2,128)(2,1)} %param.12) | copy-start | bytes 100
  2.2 25.3 %all-to-all-start = ((bf16[8,128,256]{2,1,0:T(8,128)(2,1)}), bf16[8,128,256]{2,1,0:T(8,128)(2,1)S(1)}, u32[]{:S(2)}, u32[]{:S(2)}) async-start(bf16[8,128,256]{2,1,0:T(8,128)(2,1)} %broadcast_in_dim.8), calls=%async_computation | async-start | bytes 1048576 | tf_op jit(solution)/shard_map/all_to_all | solution.py:364
  12.5 0.7 copy-start.6
  12.6 0.7 copy-start.4
  12.6 0.7 copy-start.5
  27.5 1.0 copy-start
  28.4 16.7 %copy-start.9 = (f32[2]{0:T(128)S(1)}, f32[2]{0:T(128)}, u32[]{:S(2)}) copy-start(f32[2]{0:T(128)} %param.17) | copy-start | bytes 28
  28.5 35.3 %all-to-all-start.1 = ((bf16[64,8,512]{2,1,0:T(8,128)(2,1)}), bf16[64,8,512]{2,1,0:T(8,128)(2,1)S(1)}, u32[]{:S(2)}, u32[]{:S(2)}) async-start(bf16[64,8,512]{2,1,0:T(8,128)(2,1)} %broadcast_in_dim.10), calls=%async_computation.1 | async-start | bytes 1048576 | tf_op jit(solution)/shard_map/all_to_all | solution.py:364
  45.1 0.7 copy-start.7
  45.8 0.7 copy-start.3
  63.8 0.8 copy-start.1
  88.0 18.1 %all-to-all-start.3 = ((f32[64,8,128]{2,1,0:T(8,128)}), f32[64,8,128]{2,1,0:T(8,128)S(1)}, u32[]{:S(2)}, u32[]{:S(2)}) async-start(f32[64,8,128]{2,1,0:T(8,128)} %bitcast.21), calls=%async_computation.3 | async-start | bytes 524288 | tf_op jit(solution)/shard_map/all_to_all | solution.py:364
  106.1 0.7 copy-start.2
  125.1 25.4 %all-to-all-start.5 = ((bf16[64,8,512]{2,1,0:T(8,128)(2,1)}), bf16[64,8,512]{2,1,0:T(8,128)(2,1)S(1)}, u32[]{:S(2)}, u32[]{:S(2)}) async-start(bf16[64,8,512]{2,1,0:T(8,128)(2,1)} %bitcast.11), calls=%async_computation.5 | async-start | bytes 1048576 | tf_op jit(solution)/shard_map/all_to_all | solution.py:364
  152.7 12.3 %all-to-all-start.6 = ((f32[8,8,128]{2,1,0:T(8,128)}), f32[8,8,128]{2,1,0:T(8,128)S(1)}, u32[]{:S(2)}, u32[]{:S(2)}) async-start(f32[8,8,128]{2,1,0:T(8,128)} %broadcast_in_dim.11), calls=%async_computation.6 | async-start | bytes 65536 | tf_op jit(solution)/shard_map/all_to_all | solution.py:364

commit v2 on v1

--- a/solution.py
+++ b/solution.py
@@ -9,6 +9,7 @@
 STATE = 64
 HEAD = 64
 SEQ = ("seq_0", "seq_1", "seq_2")
+CHAN = ("chan_0", "chan_1")
 NN = (((1,), (0,)), ((), ()))
 NT = (((1,), (1,)), ((), ()))
 TN = (((0,), (0,)), ((), ()))
@@ -63,17 +64,18 @@
     return 1.0 / (1.0 + jnp.exp(-x))
 
 
-def features(both):
-    n = both.shape[0] // 128
-    up = [both[128 * k : 128 * k + 64] for k in range(n)]
-    down = [both[128 * k + 64 : 128 * k + 128] for k in range(n)]
+def features(parts):
+    up, down = [], []
+    for part in parts:
+        for k in range(part.shape[0] // 128):
+            up.append(part[128 * k : 128 * k + 64])
+            down.append(part[128 * k + 64 : 128 * k + 128])
     return jnp.concatenate(up, 0), jnp.concatenate(down, 0)
 
 
-def stage_project(both, weights, params):
+def stage_project(u, q, weights, params):
     width = 128
-    n = both.shape[1]
-    u, q = features(both)
+    n = u.shape[1]
     pre = lax.dot_general(weights[:, :width], u, TN, preferred_element_type=F32)
     bc = lax.dot_general(weights[:, 128:256], u, TN, preferred_element_type=F32)
     cot = lax.dot_general(weights[:, 256:384], q, TN, preferred_element_type=F32)
@@ -98,23 +100,10 @@
     pl_ = mid(c, pulled, NT)
     kept = jnp.broadcast_to(jnp.exp(total), (8, width))
     lane = lax.broadcasted_iota(jnp.int32, (1, width), 1)
-    kept = [
-        jnp.broadcast_to(
-            jnp.where(lane < HEAD, kept[2 * r : 2 * r + 1], kept[2 * r + 1 : 2 * r + 2]),
-            (STATE, width),
-        )
-        for r in (0, 1)
-    ]
-    sends = [
-        ps[:, :width],
-        pl_[:, width:],
-        pl_[:, :width],
-        ps[:, width:],
-        kept[0],
-        kept[1],
-        kept[0],
-        kept[1],
-    ]
+    sends = [ps[:, :width], pl_[:, width:], pl_[:, :width], ps[:, width:]]
+    for r in (0, 1, 0, 1):
+        row = jnp.where(lane < HEAD, kept[2 * r : 2 * r + 1], kept[2 * r + 1 : 2 * r + 2])
+        sends.append(jnp.broadcast_to(row, (STATE, width)))
     vec = jnp.concatenate(
         [step, run, grown, tail, slope, jnp.broadcast_to(jnp.exp(total), (8, n))], 0
     )
@@ -174,10 +163,9 @@
     return mixed, dgated, dbc, extra
 
 
-def stage_finish(both, weights, params, pre, bc, cot, vec, mixed, dgated, dbc, extra, carried):
+def stage_finish(u, q, weights, params, pre, bc, cot, vec, mixed, dgated, dbc, extra, carried):
     width = 128
     n = pre.shape[1]
-    u, q = features(both)
     sig = sigmoid(pre)
     gated = pre * sig
     b, c = bc[:STATE], bc[STATE:]
@@ -266,35 +254,50 @@
 FINE = True
 
 
-def call(fn, outs, args, flops):
+def call(fn, outs, args, flops, scratch=(), scalars=0):
     def kernel(*refs):
-        ins, results = refs[: len(args)], refs[len(args) :]
-        fn(ins, results)
+        k = len(args)
+        fn(refs[:k], refs[k : k + len(outs)], *refs[k + len(outs) :])
 
     size = sum(a.size * a.dtype.itemsize for a in args)
+    spaces = [pltpu.SMEM] * scalars + [pltpu.VMEM] * (len(args) - scalars)
     return pl.pallas_call(
         kernel,
         out_shape=[jax.ShapeDtypeStruct(s, d) for s, d in outs],
+        in_specs=[pl.BlockSpec(memory_space=m) for m in spaces],
+        scratch_shapes=list(scratch),
         cost_estimate=pl.CostEstimate(flops=flops, bytes_accessed=size, transcendentals=0),
+        compiler_params=pltpu.CompilerParams(vmem_limit_bytes=24 << 20),
         interpret=INTERPRET,
     )(*args)
 
 
-def project(both, weights, params):
+def in_order(order, weights):
     if PLAIN:
-        sends, *rest = stage_project(both, weights, params)
+        return weights.reshape(8, 64, -1)[order].reshape(weights.shape)
+    rows = [weights[pl.ds(pl.multiple_of(order[k] * 64, 64), 64), :] for k in range(8)]
+    return jnp.concatenate(rows, 0)
+
+
+def project(order, parts, weights, params):
+    if PLAIN:
+        sends, *rest = stage_project(*features(parts), in_order(order, weights), params)
         return (jnp.stack(sends, 1).reshape(512, 128), *rest)
 
+    count = len(parts)
+
     def fn(ins, outs):
-        sends, *rest = stage_project(*(r[...] for r in ins))
+        u, q = features([r[...] for r in ins[1 : 1 + count]])
+        rows = in_order(ins[0], ins[1 + count])
+        sends, *rest = stage_project(u, q, rows, ins[2 + count][...])
         for j, part in enumerate(sends):
             outs[0][pl.ds(j, STATE, stride=8), :] = part
         for ref, value in zip(outs[1:], rest):
             ref[...] = value
 
-    n = both.shape[1]
+    n = parts[0].shape[1]
     outs = [((512, 128), F32), ((128, n), F32), ((128, n), F32), ((128, n), F32), ((48, n), F32)]
-    return call(fn, outs, (both, weights, params), 300_000_000)
+    return call(fn, outs, (order, *parts, weights, params), 300_000_000, (), 1)
 
 
 def within(pre, bc, cot, vec, params):
@@ -310,54 +313,81 @@
     return call(fn, outs, (pre, bc, cot, vec, params), 300_000_000)
 
 
-def finish(both, weights, params, pre, bc, cot, vec, mixed, dgated, dbc, extra, back):
-    args = (both, weights, params, pre, bc, cot, vec, mixed, dgated, dbc, extra)
+def finish(order, parts, weights, params, pre, bc, cot, vec, mixed, dgated, dbc, extra, back):
+    more = (params, pre, bc, cot, vec, mixed, dgated, dbc, extra)
+    n = pre.shape[1]
+    count = len(parts)
     if PLAIN:
-        rows = back.reshape(64, 8, 128)
-        return stage_finish(*args, [rows[:, j] for j in range(4)])
-
-    def fn(ins, outs):
-        carried = [ins[-1][pl.ds(j, STATE, stride=8), :] for j in range(4)]
-        values = stage_finish(*(r[...] for r in ins[:-1]), carried)
-        for ref, value in zip(outs, values):
-            ref[...] = value
-
-    n = pre.shape[1]
+        rows = back.astype(F32).reshape(64, 8, 128)
+        carried = [rows[:, j] + rows[:, 4 + j] for j in range(4)]
+        dinput, grads = stage_finish(
+            *features(parts), in_order(order, weights), *more, carried
+        )
+        wide = jnp.zeros((8, 64, n), BF16).at[order].set(dinput.reshape(8, 64, n))
+        grads = jnp.zeros((8, 64, 512), BF16).at[order].set(grads.reshape(8, 64, 512))
+        return wide.reshape(-1, n), grads.reshape(512, 512)
+
+    def fn(ins, outs, lines):
+        u, q = features([r[...] for r in ins[1 : 1 + count]])
+        rows = in_order(ins[0], ins[1 + count])
+        lines[...] = ins[-1][...].astype(F32)
+        carried = [
+            lines[pl.ds(j, STATE, stride=8), :] + lines[pl.ds(4 + j, STATE, stride=8), :]
+            for j in range(4)
+        ]
+        dinput, grads = stage_finish(
+            u, q, rows, *(r[...] for r in ins[2 + count : -1]), carried
+        )
+        for k in range(8):
+            at = ins[0][k]
+            block = slice(64 * k, 64 * k + 64)
+            outs[0][pl.ds(pl.multiple_of(at * 64, 64), 64), :] = dinput[block]
+            outs[1][pl.ds(pl.multiple_of(at * 64, 64), 64), :] = grads[block]
+
     outs = [((512, n), BF16), ((512, 512), BF16)]
-    return call(fn, outs, (*args, back), 600_000_000)
+    lines = pltpu.VMEM((512, 128), F32)
+    args = (order, *parts, weights, *more, back)
+    return call(fn, outs, args, 600_000_000, (lines,), 1)
 
 
 def carry(blocks):
     count = blocks.shape[0] // 8
-    if PLAIN:
-        parts = blocks.reshape(count, 8, 128)
-        kept, added = parts[:, 4:], parts[:, :4]
-        up, down = [], []
-        run = jnp.zeros((4, 128), F32)
-        for k in range(count):
-            up.append(run)
-            run = kept[k] * run + added[k]
-        run = jnp.zeros((4, 128), F32)
-        for k in reversed(range(count)):
-            down.append(run)
-            run = kept[k] * run + added[k]
-        up, down = jnp.stack(up), jnp.stack(down[::-1])
-        out = jnp.concatenate([up[:, :2], down[:, 2:], jnp.zeros((count, 4, 128), F32)], 1)
-        return out.reshape(-1, 128)
-
-    def fn(ins, outs):
-        src, dst = ins[0], outs[0]
-        dst[...] = jnp.zeros(dst.shape, F32)
+
+    def scan(src, keep):
         up = jnp.zeros((2, 128), F32)
         down = jnp.zeros((2, 128), F32)
         for k in range(count):
             m = count - 1 - k
-            dst[8 * k : 8 * k + 2, :] = up
-            dst[8 * m + 2 : 8 * m + 4, :] = down
+            keep(k, up, m, down)
             up = src[8 * k + 4 : 8 * k + 6, :] * up + src[8 * k : 8 * k + 2, :]
             down = src[8 * m + 6 : 8 * m + 8, :] * down + src[8 * m + 2 : 8 * m + 4, :]
 
-    return call(fn, [((8 * count, 128), F32)], (blocks,), 1_000_000)[0]
+    if PLAIN:
+        ups, downs = [None] * count, [None] * count
+
+        def keep(k, up, m, down):
+            ups[k], downs[m] = up, down
+
+        scan(blocks, keep)
+        full = jnp.concatenate([jnp.stack(ups), jnp.stack(downs)], 1)
+        top = full.astype(BF16)
+        rest = (full - top.astype(F32)).astype(BF16)
+        return jnp.concatenate([top, rest], 1).reshape(-1, 128)
+
+    def fn(ins, outs, sums):
+        def keep(k, up, m, down):
+            sums[8 * k : 8 * k + 2, :] = up
+            sums[8 * m + 2 : 8 * m + 4, :] = down
+
+        scan(ins[0], keep)
+        full = sums[...]
+        top = full.astype(BF16).astype(F32)
+        rest = pltpu.roll(full - top, 4, 0)
+        line = lax.broadcasted_iota(jnp.int32, full.shape, 0)
+        outs[0][...] = jnp.where(line % 8 < 4, top, rest).astype(BF16)
+
+    lines = pltpu.VMEM((8 * count, 128), F32)
+    return call(fn, [((8 * count, 128), BF16)], (blocks,), 1_000_000, (lines,))[0]
 
 
 def exchange(array, axis):
@@ -377,7 +407,15 @@
     heads = dt_weight.shape[1]
     scale = (tok_rows * seq_count) ** (-0.5)
     own = jnp.concatenate([tokens.T, out_grad.T], 0)
-    both = to_all(own, "chan").reshape(-1, tok_rows)
+    across, around = lax.axis_index("chan_0"), lax.axis_index("chan_1")
+    order = jnp.stack(
+        [((across - d) % 4) * 2 + (around ^ e) for d in range(4) for e in range(2)]
+    ).astype(jnp.int32)
+    other = lax.ppermute(own, "chan_1", [(0, 1), (1, 0)])
+    pair = jnp.concatenate([own, other], 0)
+    parts = [pair] + [
+        lax.ppermute(pair, "chan_0", [(k, (k + d) % 4) for k in range(4)]) for d in (1, 2, 3)
+    ]
     packed = jnp.concatenate(
         [
             in_weight,
@@ -394,19 +432,23 @@
         [decay_rate.reshape(-1), dt_bias.reshape(-1), jnp.tile(skip_gain, 2)], 1
     )
     params = jnp.pad(params, ((0, 4), (0, 125)))
-    sums, pre, bc, cot, vec = project(both, weights, params)
+    sums, pre, bc, cot, vec = project(order, parts, weights, params)
     sums = exchange(sums.reshape(64, 8, 128), SEQ).reshape(512, 128)
     mixed, dgated, dbc, extra = within(pre, bc, cot, vec, params)
     back = exchange(carry(sums).reshape(64, 8, 128), SEQ).reshape(512, 128)
-    dinput, grads = finish(
-        both, weights, params, pre, bc, cot, vec, mixed, dgated, dbc, extra, back
+    wide, grads = finish(
+        order, parts, weights, params, pre, bc, cot, vec, mixed, dgated, dbc, extra, back
     )
     grads = exchange(grads.reshape(64, 8, 512), SEQ)
     summed = jnp.sum(grads.astype(F32), axis=0)
-    parts = exchange(dinput.reshape(8, 64, tok_rows), "chan")
-    tokens_grad = jnp.sum(parts.astype(F32), axis=0).astype(BF16).T
+    inside = jnp.concatenate(halves(summed[:, 128:256]), 1)
+    wide = jnp.concatenate(
+        [wide.reshape(8, -1, tok_rows), jnp.broadcast_to(inside[None], (8, *inside.shape))], 1
+    )
+    parts = jnp.sum(exchange(wide, CHAN).astype(F32), axis=0)
+    tokens_grad = parts[:64].astype(BF16).T
+    bc_weight_grad = scale * (parts[64:, :width] + parts[64:, width:])
     in_weight_grad = scale * summed[:, :width]
-    bc_weight_grad = scale * jnp.sum(to_all(summed[:, 128:256], "chan"), axis=0)
     out_weight_grad = scale * summed[:, 256:384].T
     dt_weight_grad = scale * (summed[:, 384:386] + summed[:, 386:388])
     numbers = summed[0, 392:402] + summed[0, 424:434]
@@ -427,31 +469,31 @@
 
 def solution(mesh):
     split = Mesh(
-        mesh.devices.reshape(8, 4, 2, mesh.shape["chan"]), ("seq_0", "seq_1", "seq_2", "chan")
+        mesh.devices.reshape(8, 4, 2, 4, 2), (*SEQ, *CHAN)
     )
     return jax.shard_map(
         body,
         mesh=split,
         in_specs=(
-            P(SEQ, "chan"),
-            P(SEQ, "chan"),
-            P(SEQ, "chan"),
-            P(SEQ, "chan"),
+            P(SEQ, CHAN),
+            P(SEQ, CHAN),
+            P(SEQ, CHAN),
+            P(SEQ, CHAN),
             P(SEQ, None),
-            P("chan", SEQ),
-            P(None, "chan"),
-            P(None, "chan"),
-            P("chan"),
+            P(CHAN, SEQ),
+            P(None, CHAN),
+            P(None, CHAN),
+            P(CHAN),
         ),
         out_specs=(
-            P(SEQ, "chan"),
-            P(SEQ, "chan"),
-            P(SEQ, "chan"),
+            P(SEQ, CHAN),
+            P(SEQ, CHAN),
+            P(SEQ, CHAN),
             P(SEQ, None),
-            P("chan", SEQ),
-            P(None, "chan"),
-            P(None, "chan"),
-            P("chan"),
+            P(CHAN, SEQ),
+            P(None, CHAN),
+            P(None, CHAN),
+            P(CHAN),
         ),
         check_vma=False,
     )

time: 166 us -> 137 us (0.83)
  the two profiles are of different devices: /device:TPU:1 before, /device:TPU:8 now
where the time goes in v2:
time: 137 us
  blocking collectives  50 us (36%)
  starting transfers between devices  39.5 us (29%)
  waiting for transfers between devices  30.3 us (22%)
  local copies, waits for them, and re-layouts  6.52 us (5%)
  Pallas kernels  6.19 us (5%)
  other arithmetic  3.55 us (3%)
    all_to_all x2, blocking collectives, exchange(): return lax.all_to_all(array, axis, 0, 0, tiled=True)  50 us
    all_to_all x3, starting transfers between devices, exchange(): return lax.all_to_all(array, axis, 0, 0, tiled=True)  24.3 us
    all_to_all x3, waiting for transfers between devices, exchange(): return lax.all_to_all(array, axis, 0, 0, tiled=True)  20.7 us
    ppermute x3, starting transfers between devices, body(): lax.ppermute(pair, 'chan_0', [(k, (k + d) % 4) for k in range(4)])  10.2 us
    pallas_call x4, Pallas kernels, call(): pl.pallas_call(kernel, out_shape=[jax.ShapeDtypeStruct(s, d) for s, d in...  6.19 us
    ppermute x1, waiting for transfers between devices, body(): other = lax.ppermute(own, 'chan_1', [(0, 1), (1, 0)])  6.17 us
    ppermute x1, starting transfers between devices, body(): other = lax.ppermute(own, 'chan_1', [(0, 1), (1, 0)])  5.04 us
    unnamed x18, local copies, waits for them, and re-layouts  3.92 us
  transfers between devices with their start and end apart: 7, of which 5 were waited for; matrix products, arithmetic and copies ran while one was open for 2% of the time, Pallas kernels for 1%

profile of v2, /device:TPU:8, one launch (start us, length us, event | category | flops | bytes accessed | tf_op | source)
XLA Modules:
  0.0 136.8 jit_solution(10587781145649295872)
XLA Ops:
  0.6 0.0 copy-start.5
  0.6 0.7 copy.17
  1.4 0.0 copy-start.3
  1.4 0.0 copy-start.4
  1.4 0.0 copy-done.5
  1.4 0.7 copy-done.3
  2.1 0.0 copy-done.4
  2.1 0.1 concatenate.18
  2.2 0.8 broadcast_in_dim.7
  3.0 0.0 copy-start
  3.0 0.0 copy-start.1
  3.0 14.5 %all-to-all-start = ((bf16[64,8,512]{2,1,0:T(8,128)(2,1)}), bf16[64,8,512]{2,1,0:T(8,128)(2,1)S(1)}, u32[]{:S(2)}, u32[]{:S(2)}) async-start(bf16[64,8,512]{2,1,0:T(8,128)(2,1)} %broadcast_in_dim.7), calls=%async_computation | async-start | bytes 1048576 | tf_op jit(solution)/shard_map/all_to_all | solution.py:394
  17.5 0.0 copy-done
  17.5 0.0 copy-done.1
  17.5 5.0 %collective-permute-start = (bf16[128,256]{1,0:T(8,128)(2,1)S(1)}, bf16[128,256]{1,0:T(8,128)(2,1)S(1)}, u32[]{:S(2)}, u32[]{:S(2)}) collective-permute-start(bf16[128,256]{1,0:T(8,128)(2,1)S(1)} %pad_maximum_fusion.2), channel_id=1, source_target_pairs={{0,1},{1,0},{2,3},{3,2},{4,5},{5,4},{6,7},{7,6},{8,9},{9,8},{10,11... | collective-permute-start | bytes 196616 | tf_op jit(solution)/shard_map/ppermute | solution.py:414
  22.6 6.2 %collective-permute-done = bf16[128,256]{1,0:T(8,128)(2,1)S(1)} collective-permute-done((bf16[128,256]{1,0:T(8,128)(2,1)S(1)}, bf16[128,256]{1,0:T(8,128)(2,1)S(1)}, u32[]{:S(2)}, u32[]{:S(2)}) %collective-permute-start) | collective-permute-done | bytes 65568 | tf_op jit(solution)/shard_map/ppermute | solution.py:414
  28.8 4.7 %collective-permute-start.3 = (bf16[256,256]{1,0:T(8,128)(2,1)S(1)}, bf16[256,256]{1,0:T(8,128)(2,1)S(1)}, u32[]{:S(2)}, u32[]{:S(2)}) collective-permute-start(bf16[256,256]{1,0:T(8,128)(2,1)S(1)} %pad_maximum_fusion.1.refs_1_), channel_id=1, source_target_pairs={{0,6},{2,0},{4,2},{6,4},{1,7},{3,1},{5,3},{7,5},{8,14},{10,8},{12,... | collective-permute-start | bytes 393224 | tf_op jit(solution)/shard_map/ppermute | solution.py:417
  33.4 2.7 %collective-permute-start.2 = (bf16[256,256]{1,0:T(8,128)(2,1)S(1)}, bf16[256,256]{1,0:T(8,128)(2,1)S(1)}, u32[]{:S(2)}, u32[]{:S(2)}) collective-permute-start(bf16[256,256]{1,0:T(8,128)(2,1)S(1)} %pad_maximum_fusion.1.refs_1_), channel_id=1, source_target_pairs={{0,4},{2,6},{4,0},{6,2},{1,5},{3,7},{5,1},{7,3},{8,12},{10,14},{12... | collective-permute-start | bytes 393224 | tf_op jit(solution)/shard_map/ppermute | solution.py:417
  36.2 2.8 %collective-permute-start.1 = (bf16[256,256]{1,0:T(8,128)(2,1)S(1)}, bf16[256,256]{1,0:T(8,128)(2,1)S(1)}, u32[]{:S(2)}, u32[]{:S(2)}) collective-permute-start(bf16[256,256]{1,0:T(8,128)(2,1)S(1)} %pad_maximum_fusion.1.refs_1_), channel_id=1, source_target_pairs={{0,2},{2,4},{4,6},{6,0},{1,3},{3,5},{5,7},{7,1},{8,10},{10,12},{12... | collective-permute-start | bytes 393224 | tf_op jit(solution)/shard_map/ppermute | solution.py:417
  39.0 0.0 copy-start.7
  39.0 0.6 copy-done.7
  39.7 0.0 copy-start.6
  39.7 0.1 stack_tile.4
  39.8 0.6 copy-done.6
  40.4 0.0 copy-start.2
  40.4 0.1 stack_reshape.9
  40.5 0.6 copy-done.2
  41.1 0.1 stack_reshape.8
  41.1 0.1 stack.38.refs_0_
  41.2 0.1 select_maximum_fusion.refs_6_.refs_4_
  41.3 0.0 collective-permute-done.3.refs_4_
  41.3 2.0 %collective-permute-done.2.refs_3_ = bf16[256,256]{1,0:T(8,128)(2,1)S(1)} collective-permute-done((bf16[256,256]{1,0:T(8,128)(2,1)S(1)}, bf16[256,256]{1,0:T(8,128)(2,1)S(1)}, u32[]{:S(2)}, u32[]{:S(2)}) %collective-permute-start.2) | collective-permute-done | bytes 131104 | tf_op jit(solution)/shard_map/ppermute | solution.py:417
  43.3 1.4 %collective-permute-done.1.refs_2_ = bf16[256,256]{1,0:T(8,128)(2,1)S(1)} collective-permute-done((bf16[256,256]{1,0:T(8,128)(2,1)S(1)}, bf16[256,256]{1,0:T(8,128)(2,1)S(1)}, u32[]{:S(2)}, u32[]{:S(2)}) %collective-permute-start.1) | collective-permute-done | bytes 131104 | tf_op jit(solution)/shard_map/ppermute | solution.py:417
  44.7 0.0 all-to-all-done
  44.7 1.6 %shard_map.152 = (f32[512,128]{1,0:T(8,128)S(1)}, f32[128,256]{1,0:T(8,128)S(1)}, f32[128,256]{1,0:T(8,128)S(1)}, f32[128,256]{1,0:T(8,128)S(1)}, f32[48,256]{1,0:T(8,128)S(1)}) custom-call(s32[8]{0:T(128)S(1)} %stack.38.refs_0_, bf16[256,256]{1,0:T(8,128)(2,1)S(1)} %pad_maximum_fusion.1.refs_1_, bf16[256,256]{1,0:T(8,128)(2,1)S(1)} %collective-permute-done.1.refs_2_, ...), custom_call_target="tpu_custom_call" | custom-call | flops 300000000 | bytes 1052704 | tf_op jit(solution)/shard_map/pallas_call | solution.py:264
  46.3 27.0 %all_to_all.25 = f32[64,8,128]{2,1,0:T(8,128)S(1)} all-to-all(f32[64,8,128]{2,1,0:T(8,128)S(1)} %bitcast.30), channel_id=1, replica_groups=mesh['seq_0'=8,'seq_1'=4,'seq_2'=2,'chan_0'=4,'chan_1'=2] {'seq_0','seq_..., dimensions={0} | all-to-all | bytes 524288 | tf_op jit(solution)/shard_map/all_to_all | solution.py:394
  73.3 0.9 shard_map.154
  74.2 5.3 %all-to-all-start.2 = ((bf16[64,8,128]{2,1,0:T(8,128)(2,1)}), bf16[64,8,128]{2,1,0:T(8,128)(2,1)S(1)}, u32[]{:S(2)}, u32[]{:S(2)}) async-start(bf16[64,8,128]{2,1,0:T(8,128)(2,1)} %bitcast.14), calls=%async_computation.2 | async-start | bytes 262144 | tf_op jit(solution)/shard_map/all_to_all | solution.py:394
  79.5 1.7 %shard_map.153 = (f32[256,256]{1,0:T(8,128)S(1)}, f32[256,256]{1,0:T(8,128)S(1)}, f32[128,256]{1,0:T(8,128)S(1)}, f32[24,256]{1,0:T(8,128)S(1)}) custom-call(f32[128,256]{1,0:T(8,128)S(1)} %get-tuple-element.19.refs_0_.refs_7_, f32[128,256]{1,0:T(8,128)S(1)} %get-tuple-element.20.refs_1_.refs_8_, f32[128,256]{1,0:T(8,128)S(1)} %get-tuple-element.21.refs_2_.refs_9_, ...), custom_call_target="tpu_custom_call" | custom-call | flops 300000000 | bytes 446464 | tf_op jit(solution)/shard_map/pallas_call | solution.py:264
  81.1 8.3 %all-to-all-done.2 = bf16[64,8,128]{2,1,0:T(8,128)(2,1)S(1)} async-done(((bf16[64,8,128]{2,1,0:T(8,128)(2,1)}), bf16[64,8,128]{2,1,0:T(8,128)(2,1)S(1)}, u32[]{:S(2)}, u32[]{:S(2)}) %all-to-all-start.2) | async-done | bytes 131104 | tf_op jit(solution)/shard_map/all_to_all | solution.py:394
  89.5 2.1 %shard_map.155 = (bf16[512,256]{1,0:T(8,128)(2,1)S(1)}, bf16[512,512]{1,0:T(8,128)(2,1)S(1)}) custom-call(s32[8]{0:T(128)S(1)} %stack.38.refs_0_, bf16[256,256]{1,0:T(8,128)(2,1)S(1)} %pad_maximum_fusion.1.refs_1_, bf16[256,256]{1,0:T(8,128)(2,1)S(1)} %collective-permute-done.1.refs_2_, bf16[256,256]{1,0:T(8,128)(2,1)S(1)} %collective-permute-done.2.refs_3_, ...), custom_call_target="tpu_custom_call" | custom-call | flops 600000000 | bytes 2306080 | tf_op jit(solution)/shard_map/pallas_call | solution.py:264
  91.6 22.9 %all_to_all.26 = bf16[64,8,512]{2,1,0:T(8,128)(2,1)S(1)} all-to-all(bf16[64,8,512]{2,1,0:T(8,128)(2,1)S(1)} %bitcast.28), channel_id=1, replica_groups=mesh['seq_0'=8,'seq_1'=4,'seq_2'=2,'chan_0'=4,'chan_1'=2] {'seq_0','seq_..., dimensions={0} | all-to-all | bytes 1048576 | tf_op jit(solution)/shard_map/all_to_all | solution.py:394
  114.5 0.1 convert_reduce_fusion
  114.6 0.1 slice_add_fusion.2
  114.7 0.1 fusion.3
  114.8 0.6 fusion.1
  115.4 0.7 pad_maximum_fusion
  116.1 4.5 %all-to-all-start.4 = ((bf16[8,72,256]{2,1,0:T(8,128)(2,1)}), bf16[8,72,256]{2,1,0:T(8,128)(2,1)S(1)}, u32[]{:S(2)}, u32[]{:S(2)}) async-start(bf16[8,72,256]{2,1,0:T(8,128)(2,1)} %pad_maximum_fusion), calls=%async_computation.4 | async-start | bytes 589824 | tf_op jit(solution)/shard_map/all_to_all | solution.py:394
  120.6 0.1 multiply_reduce_fusion
  120.7 0.6 mul.62
  121.4 0.1 slice.58
  121.5 0.6 copy.22
  122.1 0.6 multiply_bitcast_fusion
  122.7 0.6 multiply_multiply_fusion
  123.2 12.3 %all-to-all-done.4 = bf16[8,72,256]{2,1,0:T(8,128)(2,1)S(1)} async-done(((bf16[8,72,256]{2,1,0:T(8,128)(2,1)}), bf16[8,72,256]{2,1,0:T(8,128)(2,1)S(1)}, u32[]{:S(2)}, u32[]{:S(2)}) %all-to-all-start.4) | async-done | bytes 294944 | tf_op jit(solution)/shard_map/all_to_all | solution.py:394
  135.6 0.6 fusion.2
  136.2 0.6 fusion
  (7 shorter events, 0.1 us)
Async XLA Ops:
  0.6 0.8 copy-start.5
  1.4 0.7 copy-start.3
  1.4 0.7 copy-start.4
  3.0 14.5 %copy-start = (bf16[256,64]{0,1:T(8,128)(2,1)S(1)}, bf16[256,64]{0,1:T(8,128)(2,1)}, u32[]{:S(2)}) copy-start(bf16[256,64]{0,1:T(8,128)(2,1)} %param.10) | copy-start | bytes 98308
  3.0 14.5 %copy-start.1 = (bf16[256,64]{0,1:T(8,128)(2,1)S(1)}, bf16[256,64]{0,1:T(8,128)(2,1)}, u32[]{:S(2)}) copy-start(bf16[256,64]{0,1:T(8,128)(2,1)} %param.9) | copy-start | bytes 98308
  3.0 41.7 %all-to-all-start = ((bf16[64,8,512]{2,1,0:T(8,128)(2,1)}), bf16[64,8,512]{2,1,0:T(8,128)(2,1)S(1)}, u32[]{:S(2)}, u32[]{:S(2)}) async-start(bf16[64,8,512]{2,1,0:T(8,128)(2,1)} %broadcast_in_dim.7), calls=%async_computation | async-start | bytes 1048576 | tf_op jit(solution)/shard_map/all_to_all | solution.py:394
  17.5 11.2 %collective-permute-start = (bf16[128,256]{1,0:T(8,128)(2,1)S(1)}, bf16[128,256]{1,0:T(8,128)(2,1)S(1)}, u32[]{:S(2)}, u32[]{:S(2)}) collective-permute-start(bf16[128,256]{1,0:T(8,128)(2,1)S(1)} %pad_maximum_fusion.2), channel_id=1, source_target_pairs={{0,1},{1,0},{2,3},{3,2},{4,5},{5,4},{6,7},{7,6},{8,9},{9,8},{10,11... | collective-permute-start | bytes 196616 | tf_op jit(solution)/shard_map/ppermute | solution.py:414
  28.8 12.5 %collective-permute-start.3 = (bf16[256,256]{1,0:T(8,128)(2,1)S(1)}, bf16[256,256]{1,0:T(8,128)(2,1)S(1)}, u32[]{:S(2)}, u32[]{:S(2)}) collective-permute-start(bf16[256,256]{1,0:T(8,128)(2,1)S(1)} %pad_maximum_fusion.1.refs_1_), channel_id=1, source_target_pairs={{0,6},{2,0},{4,2},{6,4},{1,7},{3,1},{5,3},{7,5},{8,14},{10,8},{12,... | collective-permute-start | bytes 393224 | tf_op jit(solution)/shard_map/ppermute | solution.py:417
  33.4 9.8 %collective-permute-start.2 = (bf16[256,256]{1,0:T(8,128)(2,1)S(1)}, bf16[256,256]{1,0:T(8,128)(2,1)S(1)}, u32[]{:S(2)}, u32[]{:S(2)}) collective-permute-start(bf16[256,256]{1,0:T(8,128)(2,1)S(1)} %pad_maximum_fusion.1.refs_1_), channel_id=1, source_target_pairs={{0,4},{2,6},{4,0},{6,2},{1,5},{3,7},{5,1},{7,3},{8,12},{10,14},{12... | collective-permute-start | bytes 393224 | tf_op jit(solution)/shard_map/ppermute | solution.py:417
  36.2 8.5 %collective-permute-start.1 = (bf16[256,256]{1,0:T(8,128)(2,1)S(1)}, bf16[256,256]{1,0:T(8,128)(2,1)S(1)}, u32[]{:S(2)}, u32[]{:S(2)}) collective-permute-start(bf16[256,256]{1,0:T(8,128)(2,1)S(1)} %pad_maximum_fusion.1.refs_1_), channel_id=1, source_target_pairs={{0,2},{2,4},{4,6},{6,0},{1,3},{3,5},{5,7},{7,1},{8,10},{10,12},{12... | collective-permute-start | bytes 393224 | tf_op jit(solution)/shard_map/ppermute | solution.py:417
  39.0 0.7 copy-start.7
  39.7 0.7 copy-start.6
  40.4 0.7 copy-start.2
  74.2 15.3 %all-to-all-start.2 = ((bf16[64,8,128]{2,1,0:T(8,128)(2,1)}), bf16[64,8,128]{2,1,0:T(8,128)(2,1)S(1)}, u32[]{:S(2)}, u32[]{:S(2)}) async-start(bf16[64,8,128]{2,1,0:T(8,128)(2,1)} %bitcast.14), calls=%async_computation.2 | async-start | bytes 262144 | tf_op jit(solution)/shard_map/all_to_all | solution.py:394
  116.1 19.5 %all-to-all-start.4 = ((bf16[8,72,256]{2,1,0:T(8,128)(2,1)}), bf16[8,72,256]{2,1,0:T(8,128)(2,1)S(1)}, u32[]{:S(2)}, u32[]{:S(2)}) async-start(bf16[8,72,256]{2,1,0:T(8,128)(2,1)} %pad_maximum_fusion), calls=%async_computation.4 | async-start | bytes 589824 | tf_op jit(solution)/shard_map/all_to_all | solution.py:394

commit v3 on v2

--- a/solution.py
+++ b/solution.py
@@ -5,6 +5,7 @@
 from jax.experimental.pallas import tpu as pltpu
 from jax.sharding import Mesh
 from jax.sharding import PartitionSpec as P
+
 
 STATE = 64
 HEAD = 64
@@ -239,22 +240,21 @@
     for k in range(2):
         numbers = jnp.where(lane == 16 + k, dskip[k : k + 1], numbers)
     rough = numbers.astype(BF16).astype(F32)
-    fine = pltpu_roll(numbers - rough, 32)
+    fine = rolled(jnp.broadcast_to(numbers - rough, (8, width)), 32)[:1]
     last = rest[:, width:] + jnp.broadcast_to(rough + fine, (u.shape[0], width))
     grads = jnp.concatenate([dfront, dinside, dout, last], 1)
     return dinput.astype(BF16), grads.astype(BF16)
 
 
-def pltpu_roll(x, by):
-    wide = jnp.broadcast_to(x, (8, x.shape[1]))
-    return (jnp.roll(wide, by, 1) if PLAIN else pltpu.roll(wide, by, 1))[:1]
+def rolled(x, by):
+    return jnp.roll(x, by, 1) if PLAIN else pltpu.roll(x, by, 1)
 
 
 PLAIN = False
 FINE = True
 
 
-def call(fn, outs, args, flops, scratch=(), scalars=0):
+def call(fn, outs, args, flops, scratch=(), scalars=0, aliases=None):
     def kernel(*refs):
         k = len(args)
         fn(refs[:k], refs[k : k + len(outs)], *refs[k + len(outs) :])
@@ -266,6 +266,7 @@
         out_shape=[jax.ShapeDtypeStruct(s, d) for s, d in outs],
         in_specs=[pl.BlockSpec(memory_space=m) for m in spaces],
         scratch_shapes=list(scratch),
+        input_output_aliases=aliases or {},
         cost_estimate=pl.CostEstimate(flops=flops, bytes_accessed=size, transcendentals=0),
         compiler_params=pltpu.CompilerParams(vmem_limit_bytes=24 << 20),
         interpret=INTERPRET,
@@ -323,9 +324,9 @@
         dinput, grads = stage_finish(
             *features(parts), in_order(order, weights), *more, carried
         )
-        wide = jnp.zeros((8, 64, n), BF16).at[order].set(dinput.reshape(8, 64, n))
+        wide = jnp.zeros((8, 72, n), BF16).at[order, :64].set(dinput.reshape(8, 64, n))
         grads = jnp.zeros((8, 64, 512), BF16).at[order].set(grads.reshape(8, 64, 512))
-        return wide.reshape(-1, n), grads.reshape(512, 512)
+        return wide, grads.reshape(512, 512)
 
     def fn(ins, outs, lines):
         u, q = features([r[...] for r in ins[1 : 1 + count]])
@@ -341,10 +342,11 @@
         for k in range(8):
             at = ins[0][k]
             block = slice(64 * k, 64 * k + 64)
-            outs[0][pl.ds(pl.multiple_of(at * 64, 64), 64), :] = dinput[block]
+            outs[0][at, :64, :] = dinput[block]
+            outs[0][at, 64:, :] = jnp.zeros((8, n), BF16)
             outs[1][pl.ds(pl.multiple_of(at * 64, 64), 64), :] = grads[block]
 
-    outs = [((512, n), BF16), ((512, 512), BF16)]
+    outs = [((8, 72, n), BF16), ((512, 512), BF16)]
     lines = pltpu.VMEM((512, 128), F32)
     args = (order, *parts, weights, *more, back)
     return call(fn, outs, args, 600_000_000, (lines,), 1)
@@ -390,12 +392,101 @@
     return call(fn, [((8 * count, 128), BF16)], (blocks,), 1_000_000, (lines,))[0]
 
 
+def send_rows(in_weight, bc_weight, out_rows, dt_rows):
+    def fill(inw, bcw, outw, dtw):
+        lane = lax.broadcasted_iota(jnp.int32, (8, 128), 1)
+        square = lax.broadcasted_iota(jnp.int32, (8, 8), 0) == lax.broadcasted_iota(
+            jnp.int32, (8, 8), 1
+        )
+        last = jnp.zeros((8, 128), F32)
+        for k in range(4):
+            row = jnp.broadcast_to(dtw[k % 2 : k % 2 + 1].astype(F32), (8, 8))
+            column = jnp.sum(jnp.where(square, row, 0.0), axis=1, keepdims=True)
+            last = jnp.where(lane == k, column, last)
+        return jnp.concatenate([inw, bcw, outw, last.astype(BF16)], 1)
+
+    args = (in_weight, bc_weight, out_rows, dt_rows)
+    if PLAIN:
+        return jnp.broadcast_to(fill(*args)[None], (64, 8, 512))
+
+    def fn(ins, outs):
+        rows = fill(*(r[...] for r in ins))
+        outs[0][...] = jnp.broadcast_to(rows[None], (64, 8, 512))
+
+    return call(fn, [((64, 8, 512), BF16)], args, 1_000_000)[0]
+
+
+def add_rows(grads, wide, decay_rate, scale):
+    def add(pieces, rates):
+        total = jnp.sum(pieces.astype(F32), axis=0)
+        inside = jnp.concatenate(halves(total[:, 128:256]), 1)
+        last = total[:, 384:512]
+        numbers = scale * (last + rolled(last, 96))[:1]
+        lane = lax.broadcasted_iota(jnp.int32, (1, 128), 1)
+
+        def pick(k):
+            return jnp.sum(jnp.where(lane == k, numbers, 0.0), axis=1, keepdims=True)
+
+        def table(shape, at):
+            i = lax.broadcasted_iota(jnp.int32, shape, 0)
+            j = lax.broadcasted_iota(jnp.int32, shape, 1)
+            out = jnp.zeros(shape, F32)
+            for k in range(shape[0] * shape[1]):
+                out = jnp.where(i * shape[1] + j == k, pick(at + k), out)
+            return out
+
+        square = lax.broadcasted_iota(jnp.int32, (8, 8), 0) == lax.broadcasted_iota(
+            jnp.int32, (8, 8), 1
+        )
+        steps = [
+            jnp.sum(
+                jnp.where(square, last[:, k : k + 1] + last[:, k + 2 : k + 3], 0.0),
+                axis=0,
+                keepdims=True,
+            )
+            for k in (0, 1)
+        ]
+        return (
+            jnp.broadcast_to(inside[None], (8, *inside.shape)),
+            scale * total[:, :128],
+            scale * total[:, 256:384],
+            scale * jnp.concatenate(steps, 0),
+            table((2, 2), 8) * rates,
+            table((2, 2), 12),
+            table((1, 2), 16),
+        )
+
+    if PLAIN:
+        inside, *rest = add(grads, decay_rate)
+    else:
+
+        def fn(ins, outs):
+            for ref, value in zip(outs, add(ins[0][...], ins[1][...])):
+                ref[...] = value
+
+        shapes = [(8, 128), (8, 128), (2, 8), (2, 2), (2, 2), (1, 2)]
+        outs = [((8, 8, 256), BF16)] + [(shape, F32) for shape in shapes]
+        inside, *rest = call(fn, outs, (grads, decay_rate), 1_000_000)
+    return wide.at[:, 64:].set(inside), *rest
+
+
+def add_parts(parts, scale):
+    def add(pieces):
+        total = jnp.sum(pieces.astype(F32), axis=0)
+        return total[:64].astype(BF16), scale * (total[64:, :128] + total[64:, 128:])
+
+    if PLAIN:
+        return add(parts)
+
+    def fn(ins, outs):
+        outs[0][...], outs[1][...] = add(ins[0][...])
+
+    n = parts.shape[2]
+    return call(fn, [((64, n), BF16), ((8, 128), F32)], (parts,), 1_000_000)
+
+
 def exchange(array, axis):
     return lax.all_to_all(array, axis, 0, 0, tiled=True)
-
-
-def to_all(array, axis):
-    return exchange(jnp.broadcast_to(array[None], (lax.axis_size(axis), *array.shape)), axis)
 
 
 def body(
@@ -403,8 +494,6 @@
 ):
     seq_count = lax.axis_size(SEQ)
     tok_rows = tokens.shape[0]
-    width = in_weight.shape[1]
-    heads = dt_weight.shape[1]
     scale = (tok_rows * seq_count) ** (-0.5)
     own = jnp.concatenate([tokens.T, out_grad.T], 0)
     across, around = lax.axis_index("chan_0"), lax.axis_index("chan_1")
@@ -416,18 +505,8 @@
     parts = [pair] + [
         lax.ppermute(pair, "chan_0", [(k, (k + d) % 4) for k in range(4)]) for d in (1, 2, 3)
     ]
-    packed = jnp.concatenate(
-        [
-            in_weight,
-            bc_weight,
-            out_weight.T,
-            dt_weight,
-            dt_weight,
-            jnp.zeros((in_weight.shape[0], 128 - 2 * heads), BF16),
-        ],
-        1,
-    )
-    weights = to_all(packed, SEQ).reshape(-1, 512)
+    rows = send_rows(in_weight, bc_weight, out_weight.T, dt_weight.T)
+    weights = exchange(rows, SEQ).reshape(-1, 512)
     params = jnp.stack(
         [decay_rate.reshape(-1), dt_bias.reshape(-1), jnp.tile(skip_gain, 2)], 1
     )
@@ -440,21 +519,14 @@
         order, parts, weights, params, pre, bc, cot, vec, mixed, dgated, dbc, extra, back
     )
     grads = exchange(grads.reshape(64, 8, 512), SEQ)
-    summed = jnp.sum(grads.astype(F32), axis=0)
-    inside = jnp.concatenate(halves(summed[:, 128:256]), 1)
-    wide = jnp.concatenate(
-        [wide.reshape(8, -1, tok_rows), jnp.broadcast_to(inside[None], (8, *inside.shape))], 1
-    )
-    parts = jnp.sum(exchange(wide, CHAN).astype(F32), axis=0)
-    tokens_grad = parts[:64].astype(BF16).T
-    bc_weight_grad = scale * (parts[64:, :width] + parts[64:, width:])
-    in_weight_grad = scale * summed[:, :width]
-    out_weight_grad = scale * summed[:, 256:384].T
-    dt_weight_grad = scale * (summed[:, 384:386] + summed[:, 386:388])
-    numbers = summed[0, 392:402] + summed[0, 424:434]
-    rate_grad = scale * decay_rate * numbers[:4].reshape(2, 2)
-    bias_grad = scale * numbers[4:8].reshape(2, 2)
-    skip_grad = scale * numbers[8:10]
+    wide, in_weight_grad, out_rows, dt_rows, rate_grad, bias_grad, skip_grad = add_rows(
+        grads, wide, decay_rate, scale
+    )
+    tokens_grad, bc_weight_grad = add_parts(exchange(wide, CHAN), scale)
+    tokens_grad = tokens_grad.T
+    out_weight_grad = out_rows.T
+    dt_weight_grad = dt_rows.T
+    skip_grad = skip_grad.reshape(-1)
     return (
         tokens_grad,
         in_weight_grad,

time: 137 us -> 137 us (level)
  blocking collectives: 50 us -> 69.4 us
  waiting for transfers between devices: 30.3 us -> 17.9 us
  starting transfers between devices: 39.5 us -> 35 us
  other arithmetic: 3.55 us -> 0.09 us
  Pallas kernels: 6.19 us -> 8.57 us
  local copies, waits for them, and re-layouts: 6.52 us -> 4.21 us
    all_to_all x2 -> x3, blocking collectives: 50 us -> 69.4 us  [exchange(): return lax.all_to_all(array, axis, 0, 0, tiled=True)]
    all_to_all x3 -> x2, waiting for transfers between devices: 20.7 us -> 8.35 us  [exchange(): return lax.all_to_all(array, axis, 0, 0, tiled=True)]
    all_to_all x3 -> x2, starting transfers between devices: 24.3 us -> 19.8 us  [exchange(): return lax.all_to_all(array, axis, 0, 0, tiled=True)]
    mul x6 -> x0, other arithmetic: 2.51 us -> none  [the longest x1 0.6 us: body(): out_weight_grad = scale * summed[:, 256:384].T]
    pallas_call x4 -> x7, Pallas kernels: 6.19 us -> 8.57 us  [call(): pl.pallas_call(kernel, out_shape=[jax.ShapeDtypeStruct(s, d) for s, d in...]
  transfers between devices with their start and end apart: 7 -> 6, of which waited for: 5 -> 4; matrix products, arithmetic and copies ran while one was open for 2% -> 0% of each run, Pallas kernels for 1% -> 1%
where the time goes in v3:
time: 137 us; the launch traced here: 136 us
  blocking collectives  69.4 us (51%)
  starting transfers between devices  35 us (26%)
  waiting for transfers between devices  17.9 us (13%)
  Pallas kernels  8.57 us (6%)
  local copies, waits for them, and re-layouts  4.21 us (3%)
    all_to_all x3, blocking collectives, exchange(): return lax.all_to_all(array, axis, 0, 0, tiled=True)  69.4 us
    all_to_all x2, starting transfers between devices, exchange(): return lax.all_to_all(array, axis, 0, 0, tiled=True)  19.8 us
    ppermute x3, starting transfers between devices, body(): lax.ppermute(pair, 'chan_0', [(k, (k + d) % 4) for k in range(4)])  10.2 us
    pallas_call x7, Pallas kernels, call(): pl.pallas_call(kernel, out_shape=[jax.ShapeDtypeStruct(s, d) for s, d in...  8.57 us
    all_to_all x2, waiting for transfers between devices, exchange(): return lax.all_to_all(array, axis, 0, 0, tiled=True)  8.35 us
    ppermute x1, waiting for transfers between devices, body(): other = lax.ppermute(own, 'chan_1', [(0, 1), (1, 0)])  6.17 us
    ppermute x1, starting transfers between devices, body(): other = lax.ppermute(own, 'chan_1', [(0, 1), (1, 0)])  5.04 us
    unnamed x18, local copies, waits for them, and re-layouts  3.88 us
  transfers between devices with their start and end apart: 6, of which 4 were waited for; matrix products, arithmetic and copies ran while one was open for 0% of the time, Pallas kernels for 1%

profile of v3, /device:TPU:8, one launch (start us, length us, event | category | flops | bytes accessed | tf_op | source)
XLA Modules:
  0.0 136.0 jit_solution(7369265448651239161)
XLA Ops:
  0.6 0.0 copy-start.1
  0.6 0.0 copy-start.4
  0.7 0.7 copy-done.1
  1.3 0.0 copy-done.4
  1.3 0.0 copy-start.2
  1.3 0.7 copy-done.2
  2.0 0.0 copy-start.3
  2.0 0.7 copy-done.3
  2.7 0.9 shard_map.152
  3.6 0.0 copy-start.5
  3.6 0.0 copy-start.6
  3.6 14.5 %all-to-all-start = ((bf16[64,8,512]{2,1,0:T(8,128)(2,1)}), bf16[64,8,512]{2,1,0:T(8,128)(2,1)S(1)}, u32[]{:S(2)}, u32[]{:S(2)}) async-start(bf16[64,8,512]{2,1,0:T(8,128)(2,1)} %shard_map.152), calls=%async_computation | async-start | bytes 1048576 | tf_op jit(solution)/shard_map/all_to_all | solution.py:489
  18.1 0.0 copy-done.5
  18.1 0.0 copy-done.6
  18.1 5.0 %collective-permute-start = (bf16[128,256]{1,0:T(8,128)(2,1)S(1)}, bf16[128,256]{1,0:T(8,128)(2,1)S(1)}, u32[]{:S(2)}, u32[]{:S(2)}) collective-permute-start(bf16[128,256]{1,0:T(8,128)(2,1)S(1)} %pad_maximum_fusion.1), channel_id=1, source_target_pairs={{0,1},{1,0},{2,3},{3,2},{4,5},{5,4},{6,7},{7,6},{8,9},{9,8},{10,11... | collective-permute-start | bytes 196616 | tf_op jit(solution)/shard_map/ppermute | solution.py:503
  23.2 6.2 %collective-permute-done = bf16[128,256]{1,0:T(8,128)(2,1)S(1)} collective-permute-done((bf16[128,256]{1,0:T(8,128)(2,1)S(1)}, bf16[128,256]{1,0:T(8,128)(2,1)S(1)}, u32[]{:S(2)}, u32[]{:S(2)}) %collective-permute-start) | collective-permute-done | bytes 65568 | tf_op jit(solution)/shard_map/ppermute | solution.py:503
  29.4 4.7 %collective-permute-start.3 = (bf16[256,256]{1,0:T(8,128)(2,1)S(1)}, bf16[256,256]{1,0:T(8,128)(2,1)S(1)}, u32[]{:S(2)}, u32[]{:S(2)}) collective-permute-start(bf16[256,256]{1,0:T(8,128)(2,1)S(1)} %pad_maximum_fusion.refs_1_), channel_id=1, source_target_pairs={{0,6},{2,0},{4,2},{6,4},{1,7},{3,1},{5,3},{7,5},{8,14},{10,8},{12,... | collective-permute-start | bytes 393224 | tf_op jit(solution)/shard_map/ppermute | solution.py:506
  34.0 2.7 %collective-permute-start.2 = (bf16[256,256]{1,0:T(8,128)(2,1)S(1)}, bf16[256,256]{1,0:T(8,128)(2,1)S(1)}, u32[]{:S(2)}, u32[]{:S(2)}) collective-permute-start(bf16[256,256]{1,0:T(8,128)(2,1)S(1)} %pad_maximum_fusion.refs_1_), channel_id=1, source_target_pairs={{0,4},{2,6},{4,0},{6,2},{1,5},{3,7},{5,1},{7,3},{8,12},{10,14},{12... | collective-permute-start | bytes 393224 | tf_op jit(solution)/shard_map/ppermute | solution.py:506
  36.7 2.8 %collective-permute-start.1 = (bf16[256,256]{1,0:T(8,128)(2,1)S(1)}, bf16[256,256]{1,0:T(8,128)(2,1)S(1)}, u32[]{:S(2)}, u32[]{:S(2)}) collective-permute-start(bf16[256,256]{1,0:T(8,128)(2,1)S(1)} %pad_maximum_fusion.refs_1_), channel_id=1, source_target_pairs={{0,2},{2,4},{4,6},{6,0},{1,3},{3,5},{5,7},{7,1},{8,10},{10,12},{12... | collective-permute-start | bytes 393224 | tf_op jit(solution)/shard_map/ppermute | solution.py:506
  39.6 0.0 copy-start.8
  39.6 0.6 copy-done.8
  40.3 0.0 copy-start.7
  40.3 0.1 stack_tile.4
  40.4 0.6 copy-done.7
  41.0 0.0 copy-start
  41.0 0.1 stack_reshape.9
  41.0 0.6 copy-done
  41.6 0.1 stack_reshape.8
  41.7 0.1 stack.38.refs_0_
  41.8 0.1 select_maximum_fusion.refs_6_.refs_4_
  41.9 0.0 collective-permute-done.3.refs_4_
  41.9 2.0 %collective-permute-done.2.refs_3_ = bf16[256,256]{1,0:T(8,128)(2,1)S(1)} collective-permute-done((bf16[256,256]{1,0:T(8,128)(2,1)S(1)}, bf16[256,256]{1,0:T(8,128)(2,1)S(1)}, u32[]{:S(2)}, u32[]{:S(2)}) %collective-permute-start.2) | collective-permute-done | bytes 131104 | tf_op jit(solution)/shard_map/ppermute | solution.py:506
  43.9 1.4 %collective-permute-done.1.refs_2_ = bf16[256,256]{1,0:T(8,128)(2,1)S(1)} collective-permute-done((bf16[256,256]{1,0:T(8,128)(2,1)S(1)}, bf16[256,256]{1,0:T(8,128)(2,1)S(1)}, u32[]{:S(2)}, u32[]{:S(2)}) %collective-permute-start.1) | collective-permute-done | bytes 131104 | tf_op jit(solution)/shard_map/ppermute | solution.py:506
  45.3 0.0 all-to-all-done
  45.3 1.6 %shard_map.153 = (f32[512,128]{1,0:T(8,128)S(1)}, f32[128,256]{1,0:T(8,128)S(1)}, f32[128,256]{1,0:T(8,128)S(1)}, f32[128,256]{1,0:T(8,128)S(1)}, f32[48,256]{1,0:T(8,128)S(1)}) custom-call(s32[8]{0:T(128)S(1)} %stack.38.refs_0_, bf16[256,256]{1,0:T(8,128)(2,1)S(1)} %pad_maximum_fusion.refs_1_, bf16[256,256]{1,0:T(8,128)(2,1)S(1)} %collective-permute-done.1.refs_2_, ...), custom_call_target="tpu_custom_call" | custom-call | flops 300000000 | bytes 1052704 | tf_op jit(solution)/shard_map/pallas_call | solution.py:264
  46.9 27.0 %all_to_all.25 = f32[64,8,128]{2,1,0:T(8,128)S(1)} all-to-all(f32[64,8,128]{2,1,0:T(8,128)S(1)} %bitcast.27), channel_id=1, replica_groups=mesh['seq_0'=8,'seq_1'=4,'seq_2'=2,'chan_0'=4,'chan_1'=2] {'seq_0','seq_..., dimensions={0} | all-to-all | bytes 524288 | tf_op jit(solution)/shard_map/all_to_all | solution.py:489
  73.9 0.9 shard_map.155
  74.8 5.3 %all-to-all-start.2 = ((bf16[64,8,128]{2,1,0:T(8,128)(2,1)}), bf16[64,8,128]{2,1,0:T(8,128)(2,1)S(1)}, u32[]{:S(2)}, u32[]{:S(2)}) async-start(bf16[64,8,128]{2,1,0:T(8,128)(2,1)} %bitcast.15), calls=%async_computation.2 | async-start | bytes 262144 | tf_op jit(solution)/shard_map/all_to_all | solution.py:489
  80.0 1.7 %shard_map.154 = (f32[256,256]{1,0:T(8,128)S(1)}, f32[256,256]{1,0:T(8,128)S(1)}, f32[128,256]{1,0:T(8,128)S(1)}, f32[24,256]{1,0:T(8,128)S(1)}) custom-call(f32[128,256]{1,0:T(8,128)S(1)} %get-tuple-element.40.refs_0_.refs_7_, f32[128,256]{1,0:T(8,128)S(1)} %get-tuple-element.41.refs_1_.refs_8_, f32[128,256]{1,0:T(8,128)S(1)} %get-tuple-element.42.refs_2_.refs_9_, ...), custom_call_target="tpu_custom_call" | custom-call | flops 300000000 | bytes 446464 | tf_op jit(solution)/shard_map/pallas_call | solution.py:264
  81.7 8.3 %all-to-all-done.2 = bf16[64,8,128]{2,1,0:T(8,128)(2,1)S(1)} async-done(((bf16[64,8,128]{2,1,0:T(8,128)(2,1)}), bf16[64,8,128]{2,1,0:T(8,128)(2,1)S(1)}, u32[]{:S(2)}, u32[]{:S(2)}) %all-to-all-start.2) | async-done | bytes 131104 | tf_op jit(solution)/shard_map/all_to_all | solution.py:489
  90.1 2.1 %shard_map.156 = (bf16[8,72,256]{2,1,0:T(8,128)(2,1)S(1)}, bf16[512,512]{1,0:T(8,128)(2,1)S(1)}) custom-call(s32[8]{0:T(128)S(1)} %stack.38.refs_0_, bf16[256,256]{1,0:T(8,128)(2,1)S(1)} %pad_maximum_fusion.refs_1_, bf16[256,256]{1,0:T(8,128)(2,1)S(1)} %collective-permute-done.1.refs_2_, bf16[256,256]{1,0:T(8,128)(2,1)S(1)} %collective-permute-done.2.refs_3_, ...), custom_call_target="tpu_custom_call" | custom-call | flops 600000000 | bytes 2306080 | tf_op jit(solution)/shard_map/pallas_call | solution.py:264
  92.2 22.9 %all_to_all.26.refs_0_ = bf16[64,8,512]{2,1,0:T(8,128)(2,1)S(1)} all-to-all(bf16[64,8,512]{2,1,0:T(8,128)(2,1)S(1)} %bitcast.26), channel_id=1, replica_groups=mesh['seq_0'=8,'seq_1'=4,'seq_2'=2,'chan_0'=4,'chan_1'=2] {'seq_0','seq_..., dimensions={0} | all-to-all | bytes 1048576 | tf_op jit(solution)/shard_map/all_to_all | solution.py:489
  115.1 0.8 shard_map.157
  115.9 19.5 %all_to_all.27.refs_0_ = bf16[8,72,256]{2,1,0:T(8,128)(2,1)S(1)} all-to-all(bf16[8,72,256]{2,1,0:T(8,128)(2,1)S(1)} %constant_dynamic-update-slice_fusion), channel_id=1, replica_groups=mesh['seq_0'=8,'seq_1'=4,'seq_2'=2,'chan_0'=4,'chan_1'=2] {'chan_0','cha..., dimensions={0} | all-to-all | bytes 589824 | tf_op jit(solution)/shard_map/all_to_all | solution.py:489
  135.4 0.7 shard_map.158
  (4 shorter events, 0.0 us)
Async XLA Ops:
  0.6 0.7 copy-start.1
  0.6 0.7 copy-start.4
  1.3 0.7 copy-start.2
  2.0 0.7 copy-start.3
  3.6 14.5 %copy-start.5 = (bf16[256,64]{0,1:T(8,128)(2,1)S(1)}, bf16[256,64]{0,1:T(8,128)(2,1)}, u32[]{:S(2)}) copy-start(bf16[256,64]{0,1:T(8,128)(2,1)} %param.12) | copy-start | bytes 98308
  3.6 14.5 %copy-start.6 = (bf16[256,64]{0,1:T(8,128)(2,1)S(1)}, bf16[256,64]{0,1:T(8,128)(2,1)}, u32[]{:S(2)}) copy-start(bf16[256,64]{0,1:T(8,128)(2,1)} %param.11) | copy-start | bytes 98308
  3.6 41.7 %all-to-all-start = ((bf16[64,8,512]{2,1,0:T(8,128)(2,1)}), bf16[64,8,512]{2,1,0:T(8,128)(2,1)S(1)}, u32[]{:S(2)}, u32[]{:S(2)}) async-start(bf16[64,8,512]{2,1,0:T(8,128)(2,1)} %shard_map.152), calls=%async_computation | async-start | bytes 1048576 | tf_op jit(solution)/shard_map/all_to_all | solution.py:489
  18.1 11.2 %collective-permute-start = (bf16[128,256]{1,0:T(8,128)(2,1)S(1)}, bf16[128,256]{1,0:T(8,128)(2,1)S(1)}, u32[]{:S(2)}, u32[]{:S(2)}) collective-permute-start(bf16[128,256]{1,0:T(8,128)(2,1)S(1)} %pad_maximum_fusion.1), channel_id=1, source_target_pairs={{0,1},{1,0},{2,3},{3,2},{4,5},{5,4},{6,7},{7,6},{8,9},{9,8},{10,11... | collective-permute-start | bytes 196616 | tf_op jit(solution)/shard_map/ppermute | solution.py:503
  29.4 12.5 %collective-permute-start.3 = (bf16[256,256]{1,0:T(8,128)(2,1)S(1)}, bf16[256,256]{1,0:T(8,128)(2,1)S(1)}, u32[]{:S(2)}, u32[]{:S(2)}) collective-permute-start(bf16[256,256]{1,0:T(8,128)(2,1)S(1)} %pad_maximum_fusion.refs_1_), channel_id=1, source_target_pairs={{0,6},{2,0},{4,2},{6,4},{1,7},{3,1},{5,3},{7,5},{8,14},{10,8},{12,... | collective-permute-start | bytes 393224 | tf_op jit(solution)/shard_map/ppermute | solution.py:506
  34.0 9.8 %collective-permute-start.2 = (bf16[256,256]{1,0:T(8,128)(2,1)S(1)}, bf16[256,256]{1,0:T(8,128)(2,1)S(1)}, u32[]{:S(2)}, u32[]{:S(2)}) collective-permute-start(bf16[256,256]{1,0:T(8,128)(2,1)S(1)} %pad_maximum_fusion.refs_1_), channel_id=1, source_target_pairs={{0,4},{2,6},{4,0},{6,2},{1,5},{3,7},{5,1},{7,3},{8,12},{10,14},{12... | collective-permute-start | bytes 393224 | tf_op jit(solution)/shard_map/ppermute | solution.py:506
  36.7 8.5 %collective-permute-start.1 = (bf16[256,256]{1,0:T(8,128)(2,1)S(1)}, bf16[256,256]{1,0:T(8,128)(2,1)S(1)}, u32[]{:S(2)}, u32[]{:S(2)}) collective-permute-start(bf16[256,256]{1,0:T(8,128)(2,1)S(1)} %pad_maximum_fusion.refs_1_), channel_id=1, source_target_pairs={{0,2},{2,4},{4,6},{6,0},{1,3},{3,5},{5,7},{7,1},{8,10},{10,12},{12... | collective-permute-start | bytes 393224 | tf_op jit(solution)/shard_map/ppermute | solution.py:506
  39.6 0.7 copy-start.8
  40.3 0.7 copy-start.7
  41.0 0.7 copy-start
  74.8 15.3 %all-to-all-start.2 = ((bf16[64,8,128]{2,1,0:T(8,128)(2,1)}), bf16[64,8,128]{2,1,0:T(8,128)(2,1)S(1)}, u32[]{:S(2)}, u32[]{:S(2)}) async-start(bf16[64,8,128]{2,1,0:T(8,128)(2,1)} %bitcast.15), calls=%async_computation.2 | async-start | bytes 262144 | tf_op jit(solution)/shard_map/all_to_all | solution.py:489

commit v4 on v3

--- a/solution.py
+++ b/solution.py
@@ -10,6 +10,8 @@
 STATE = 64
 HEAD = 64
 SEQ = ("seq_0", "seq_1", "seq_2")
+ZY = ("seq_0", "seq_1")
+CORE = "seq_2"
 CHAN = ("chan_0", "chan_1")
 NN = (((1,), (0,)), ((), ()))
 NT = (((1,), (1,)), ((), ()))
@@ -63,15 +65,6 @@
 
 def sigmoid(x):
     return 1.0 / (1.0 + jnp.exp(-x))
-
-
-def features(parts):
-    up, down = [], []
-    for part in parts:
-        for k in range(part.shape[0] // 128):
-            up.append(part[128 * k : 128 * k + 64])
-            down.append(part[128 * k + 64 : 128 * k + 128])
-    return jnp.concatenate(up, 0), jnp.concatenate(down, 0)
 
 
 def stage_project(u, q, weights, params):
@@ -102,9 +95,13 @@
     kept = jnp.broadcast_to(jnp.exp(total), (8, width))
     lane = lax.broadcasted_iota(jnp.int32, (1, width), 1)
     sends = [ps[:, :width], pl_[:, width:], pl_[:, :width], ps[:, width:]]
-    for r in (0, 1, 0, 1):
-        row = jnp.where(lane < HEAD, kept[2 * r : 2 * r + 1], kept[2 * r + 1 : 2 * r + 2])
-        sends.append(jnp.broadcast_to(row, (STATE, width)))
+    tops = [part.astype(BF16).astype(F32) for part in sends]
+    rests = [part - top for part, top in zip(sends, tops)]
+    for k in range(4):
+        top = kept[k : k + 1].astype(BF16).astype(F32)
+        rests[3] = jnp.where(lane == 120 + 2 * k, top, rests[3])
+        rests[3] = jnp.where(lane == 121 + 2 * k, kept[k : k + 1] - top, rests[3])
+    sends = tops + rests
     vec = jnp.concatenate(
         [step, run, grown, tail, slope, jnp.broadcast_to(jnp.exp(total), (8, n))], 0
     )
@@ -243,7 +240,7 @@
     fine = rolled(jnp.broadcast_to(numbers - rough, (8, width)), 32)[:1]
     last = rest[:, width:] + jnp.broadcast_to(rough + fine, (u.shape[0], width))
     grads = jnp.concatenate([dfront, dinside, dout, last], 1)
-    return dinput.astype(BF16), grads.astype(BF16)
+    return dinput, grads
 
 
 def rolled(x, by):
@@ -251,10 +248,11 @@
 
 
 PLAIN = False
+SWAP = [(0, 1), (1, 0)]
 FINE = True
 
 
-def call(fn, outs, args, flops, scratch=(), scalars=0, aliases=None):
+def call(fn, outs, args, flops, scratch=(), scalars=0, grant=24 << 20):
     def kernel(*refs):
         k = len(args)
         fn(refs[:k], refs[k : k + len(outs)], *refs[k + len(outs) :])
@@ -266,39 +264,51 @@
         out_shape=[jax.ShapeDtypeStruct(s, d) for s, d in outs],
         in_specs=[pl.BlockSpec(memory_space=m) for m in spaces],
         scratch_shapes=list(scratch),
-        input_output_aliases=aliases or {},
         cost_estimate=pl.CostEstimate(flops=flops, bytes_accessed=size, transcendentals=0),
-        compiler_params=pltpu.CompilerParams(vmem_limit_bytes=24 << 20),
+        compiler_params=pltpu.CompilerParams(vmem_limit_bytes=grant),
         interpret=INTERPRET,
     )(*args)
 
 
-def in_order(order, weights):
-    if PLAIN:
-        return weights.reshape(8, 64, -1)[order].reshape(weights.shape)
-    rows = [weights[pl.ds(pl.multiple_of(order[k] * 64, 64), 64), :] for k in range(8)]
-    return jnp.concatenate(rows, 0)
-
-
-def project(order, parts, weights, params):
-    if PLAIN:
-        sends, *rest = stage_project(*features(parts), in_order(order, weights), params)
-        return (jnp.stack(sends, 1).reshape(512, 128), *rest)
-
-    count = len(parts)
-
-    def fn(ins, outs):
-        u, q = features([r[...] for r in ins[1 : 1 + count]])
-        rows = in_order(ins[0], ins[1 + count])
-        sends, *rest = stage_project(u, q, rows, ins[2 + count][...])
+def gathered(order, parts, own, other):
+    if PLAIN:
+        n = parts[0].shape[1]
+        blocks = jnp.concatenate(parts, 0).reshape(8, 2, 2, 32, n)
+        mine = order[8]
+        u, q = (
+            jnp.concatenate([blocks[:, k, mine], blocks[:, k, 1 - mine]], 0).reshape(512, n)
+            for k in (0, 1)
+        )
+        halves_ = [w.reshape(8, 32, -1)[order[:8]] for w in (own, other)]
+        return u, q, jnp.concatenate(halves_, 0).reshape(512, -1)
+    mine = order[8] * 32
+    up, down, rows = [], [], []
+    for at, weights in ((mine, own), (32 - mine, other)):
+        for k in range(8):
+            part, base = parts[k // 2], 128 * (k % 2)
+            up.append(part[pl.ds(pl.multiple_of(base + at, 32), 32), :])
+            down.append(part[pl.ds(pl.multiple_of(base + 64 + at, 32), 32), :])
+            rows.append(weights[pl.ds(pl.multiple_of(order[k] * 32, 32), 32), :])
+    return jnp.concatenate(up, 0), jnp.concatenate(down, 0), jnp.concatenate(rows, 0)
+
+
+def project(order, parts, own, other, params):
+    if PLAIN:
+        sends, *rest = stage_project(*gathered(order, parts, own, other), params)
+        return (jnp.stack(sends, 1).reshape(512, 128).astype(BF16), *rest)
+
+    def fn(ins, outs, lines):
+        sends, *rest = stage_project(*gathered(ins[0], ins[1:5], ins[5], ins[6]), ins[7][...])
         for j, part in enumerate(sends):
-            outs[0][pl.ds(j, STATE, stride=8), :] = part
+            lines[pl.ds(j, STATE, stride=8), :] = part
+        outs[0][...] = lines[...].astype(BF16)
         for ref, value in zip(outs[1:], rest):
             ref[...] = value
 
     n = parts[0].shape[1]
-    outs = [((512, 128), F32), ((128, n), F32), ((128, n), F32), ((128, n), F32), ((48, n), F32)]
-    return call(fn, outs, (order, *parts, weights, params), 300_000_000, (), 1)
+    outs = [((512, 128), BF16), ((128, n), F32), ((128, n), F32), ((128, n), F32), ((48, n), F32)]
+    lines = pltpu.VMEM((512, 128), F32)
+    return call(fn, outs, (order, *parts, own, other, params), 300_000_000, (lines,), 1)
 
 
 def within(pre, bc, cot, vec, params):
@@ -314,86 +324,134 @@
     return call(fn, outs, (pre, bc, cot, vec, params), 300_000_000)
 
 
-def finish(order, parts, weights, params, pre, bc, cot, vec, mixed, dgated, dbc, extra, back):
+def finish(order, parts, own, other, params, pre, bc, cot, vec, mixed, dgated, dbc, extra, back):
     more = (params, pre, bc, cot, vec, mixed, dgated, dbc, extra)
     n = pre.shape[1]
-    count = len(parts)
     if PLAIN:
         rows = back.astype(F32).reshape(64, 8, 128)
         carried = [rows[:, j] + rows[:, 4 + j] for j in range(4)]
-        dinput, grads = stage_finish(
-            *features(parts), in_order(order, weights), *more, carried
-        )
-        wide = jnp.zeros((8, 72, n), BF16).at[order, :64].set(dinput.reshape(8, 64, n))
-        grads = jnp.zeros((8, 64, 512), BF16).at[order].set(grads.reshape(8, 64, 512))
-        return wide, grads.reshape(512, 512)
+        dinput, grads = stage_finish(*gathered(order, parts, own, other), *more, carried)
+        at, mine = order[:8], order[8]
+        dinput = dinput.astype(BF16).reshape(2, 8, 32, n)
+        dinput = jnp.where(mine == 0, dinput, dinput[::-1]).transpose(1, 0, 2, 3)
+        wide = jnp.zeros((8, 72, n), BF16).at[at, :64].set(dinput.reshape(8, 64, n))
+        grads = grads.reshape(2, 8, 32, 512)
+        keep = jnp.zeros((8, 32, 512), F32).at[at].set(grads[0]).reshape(256, 512)
+        give = jnp.zeros((8, 32, 512), F32).at[at].set(grads[1]).reshape(256, 512)
+        return wide, keep, give.astype(BF16)
 
     def fn(ins, outs, lines):
-        u, q = features([r[...] for r in ins[1 : 1 + count]])
-        rows = in_order(ins[0], ins[1 + count])
+        order = ins[0]
         lines[...] = ins[-1][...].astype(F32)
         carried = [
             lines[pl.ds(j, STATE, stride=8), :] + lines[pl.ds(4 + j, STATE, stride=8), :]
             for j in range(4)
         ]
         dinput, grads = stage_finish(
-            u, q, rows, *(r[...] for r in ins[2 + count : -1]), carried
+            *gathered(order, ins[1:5], ins[5], ins[6]), *(r[...] for r in ins[7:-1]), carried
         )
+        dinput = dinput.astype(BF16)
+        give = grads[256:].astype(BF16)
+        mine = order[8] * 32
         for k in range(8):
-            at = ins[0][k]
-            block = slice(64 * k, 64 * k + 64)
-            outs[0][at, :64, :] = dinput[block]
+            at = order[k]
+            block = slice(32 * k, 32 * k + 32)
+            rows = pl.ds(pl.multiple_of(at * 32, 32), 32)
+            outs[0][at, pl.ds(pl.multiple_of(mine, 32), 32), :] = dinput[block]
+            outs[0][at, pl.ds(pl.multiple_of(32 - mine, 32), 32), :] = dinput[256:][block]
             outs[0][at, 64:, :] = jnp.zeros((8, n), BF16)
-            outs[1][pl.ds(pl.multiple_of(at * 64, 64), 64), :] = grads[block]
-
-    outs = [((8, 72, n), BF16), ((512, 512), BF16)]
+            outs[1][rows, :] = grads[block]
+            outs[2][rows, :] = give[block]
+
+    outs = [((8, 72, n), BF16), ((256, 512), F32), ((256, 512), BF16)]
     lines = pltpu.VMEM((512, 128), F32)
-    args = (order, *parts, weights, *more, back)
+    args = (order, *parts, own, other, *more, back)
     return call(fn, outs, args, 600_000_000, (lines,), 1)
+
+
+def join(keep, got):
+    def add(mine, theirs):
+        total = mine + theirs.astype(F32)
+        last = total[:, 384:]
+        lane = lax.broadcasted_iota(jnp.int32, last.shape, 1)
+        numbers = last + rolled(last, 96)
+        rough = numbers.astype(BF16).astype(F32)
+        fine = rolled(numbers - rough, 32)
+        last = jnp.where(lane < 8, last, jnp.where(lane < 32, rough, fine))
+        return jnp.concatenate([total[:, :384], last], 1).astype(BF16)
+
+    if PLAIN:
+        return add(keep, got)
+
+    def fn(ins, outs):
+        outs[0][...] = add(ins[0][...], ins[1][...])
+
+    return call(fn, [(keep.shape, BF16)], (keep, got), 1_000_000)[0]
 
 
 def carry(blocks):
     count = blocks.shape[0] // 8
 
-    def scan(src, keep):
+    def unpack(take):
+        lane = lax.broadcasted_iota(jnp.int32, (1, 128), 1)
+        last = take(7)
+        rests = [take(4), take(5), take(6), jnp.where(lane < 120, last, 0.0)]
+        sums = [take(j) + rests[j] for j in range(4)]
+        kept = [last[:, k : k + 1] + last[:, k + 1 : k + 2] for k in range(120, 128, 2)]
+        return sums, [jnp.where(lane < HEAD, kept[2 * r], kept[2 * r + 1]) for r in (0, 1)]
+
+    def scan(added, kept, keep):
         up = jnp.zeros((2, 128), F32)
         down = jnp.zeros((2, 128), F32)
         for k in range(count):
             m = count - 1 - k
             keep(k, up, m, down)
-            up = src[8 * k + 4 : 8 * k + 6, :] * up + src[8 * k : 8 * k + 2, :]
-            down = src[8 * m + 6 : 8 * m + 8, :] * down + src[8 * m + 2 : 8 * m + 4, :]
-
-    if PLAIN:
+            up = kept[2 * k : 2 * k + 2, :] * up + added[4 * k : 4 * k + 2, :]
+            down = kept[2 * m : 2 * m + 2, :] * down + added[4 * m + 2 : 4 * m + 4, :]
+
+    if PLAIN:
+        lines = blocks.astype(F32).reshape(count, 8, 128)
+        sums, kept = unpack(lambda j: lines[:, j])
         ups, downs = [None] * count, [None] * count
 
         def keep(k, up, m, down):
             ups[k], downs[m] = up, down
 
-        scan(blocks, keep)
+        scan(jnp.stack(sums, 1).reshape(-1, 128), jnp.stack(kept, 1).reshape(-1, 128), keep)
         full = jnp.concatenate([jnp.stack(ups), jnp.stack(downs)], 1)
         top = full.astype(BF16)
         rest = (full - top.astype(F32)).astype(BF16)
         return jnp.concatenate([top, rest], 1).reshape(-1, 128)
 
-    def fn(ins, outs, sums):
+    def fn(ins, outs, lines, added, factors, done):
+        lines[...] = ins[0][...].astype(F32)
+        sums, kept = unpack(lambda j: lines[pl.ds(j, count, stride=8), :])
+        for j in range(4):
+            added[pl.ds(j, count, stride=4), :] = sums[j]
+        for r in (0, 1):
+            factors[pl.ds(r, count, stride=2), :] = kept[r]
+
         def keep(k, up, m, down):
-            sums[8 * k : 8 * k + 2, :] = up
-            sums[8 * m + 2 : 8 * m + 4, :] = down
-
-        scan(ins[0], keep)
-        full = sums[...]
+            done[8 * k : 8 * k + 2, :] = up
+            done[8 * m + 2 : 8 * m + 4, :] = down
+
+        scan(added, factors, keep)
+        full = done[...]
         top = full.astype(BF16).astype(F32)
         rest = pltpu.roll(full - top, 4, 0)
         line = lax.broadcasted_iota(jnp.int32, full.shape, 0)
         outs[0][...] = jnp.where(line % 8 < 4, top, rest).astype(BF16)
 
-    lines = pltpu.VMEM((8 * count, 128), F32)
-    return call(fn, [((8 * count, 128), BF16)], (blocks,), 1_000_000, (lines,))[0]
-
-
-def send_rows(in_weight, bc_weight, out_rows, dt_rows):
-    def fill(inw, bcw, outw, dtw):
+    scratch = [pltpu.VMEM((rows * count, 128), F32) for rows in (8, 4, 2, 8)]
+    return call(fn, [((8 * count, 128), BF16)], (blocks,), 1_000_000, scratch)[0]
+
+
+def pack(tokens, cotangents, in_weight, bc_weight, out_rows, dt_rows):
+    def fill(tok, cot, inw, bcw, outw, dtw):
+        blocks = []
+        for x in (tok.astype(F32), cot.astype(F32)):
+            for odd in (0, 8):
+                blocks += [x[k + odd : k + odd + 8] for k in range(0, 64, 16)]
         lane = lax.broadcasted_iota(jnp.int32, (8, 128), 1)
         square = lax.broadcasted_iota(jnp.int32, (8, 8), 0) == lax.broadcasted_iota(
             jnp.int32, (8, 8), 1
@@ -403,17 +461,18 @@
             row = jnp.broadcast_to(dtw[k % 2 : k % 2 + 1].astype(F32), (8, 8))
             column = jnp.sum(jnp.where(square, row, 0.0), axis=1, keepdims=True)
             last = jnp.where(lane == k, column, last)
-        return jnp.concatenate([inw, bcw, outw, last.astype(BF16)], 1)
-
-    args = (in_weight, bc_weight, out_rows, dt_rows)
-    if PLAIN:
-        return jnp.broadcast_to(fill(*args)[None], (64, 8, 512))
+        rows = jnp.concatenate([inw, bcw, outw, last.astype(BF16)], 1)
+        return jnp.concatenate(blocks, 0).astype(BF16), jnp.broadcast_to(rows[None], (32, 8, 512))
+
+    args = (tokens, cotangents, in_weight, bc_weight, out_rows, dt_rows)
+    if PLAIN:
+        return fill(*args)
 
     def fn(ins, outs):
-        rows = fill(*(r[...] for r in ins))
-        outs[0][...] = jnp.broadcast_to(rows[None], (64, 8, 512))
-
-    return call(fn, [((64, 8, 512), BF16)], args, 1_000_000)[0]
+        outs[0][...], outs[1][...] = fill(*(r[...] for r in ins))
+
+    n = tokens.shape[1]
+    return call(fn, [((128, n), BF16), ((32, 8, 512), BF16)], args, 1_000_000, grant=None)
 
 
 def add_rows(grads, wide, decay_rate, scale):
@@ -473,7 +532,8 @@
 def add_parts(parts, scale):
     def add(pieces):
         total = jnp.sum(pieces.astype(F32), axis=0)
-        return total[:64].astype(BF16), scale * (total[64:, :128] + total[64:, 128:])
+        blocks = [total[8 * (k // 2) + 32 * (k % 2) :][:8] for k in range(8)]
+        return jnp.concatenate(blocks, 0).astype(BF16), scale * (total[64:, :128] + total[64:, 128:])
 
     if PLAIN:
         return add(parts)
@@ -495,30 +555,33 @@
     seq_count = lax.axis_size(SEQ)
     tok_rows = tokens.shape[0]
     scale = (tok_rows * seq_count) ** (-0.5)
-    own = jnp.concatenate([tokens.T, out_grad.T], 0)
+    own, rows = pack(
+        tokens.T, out_grad.T, in_weight, bc_weight, out_weight.T, dt_weight.T
+    )
     across, around = lax.axis_index("chan_0"), lax.axis_index("chan_1")
     order = jnp.stack(
         [((across - d) % 4) * 2 + (around ^ e) for d in range(4) for e in range(2)]
+        + [lax.axis_index(CORE)]
     ).astype(jnp.int32)
-    other = lax.ppermute(own, "chan_1", [(0, 1), (1, 0)])
+    other = lax.ppermute(own, "chan_1", SWAP)
     pair = jnp.concatenate([own, other], 0)
     parts = [pair] + [
-        lax.ppermute(pair, "chan_0", [(k, (k + d) % 4) for k in range(4)]) for d in (1, 2, 3)
+        lax.ppermute(pair, "chan_0", [(k, (k + d) % 4) for k in range(4)])
+        for d in (1, 2, 3)
     ]
-    rows = send_rows(in_weight, bc_weight, out_weight.T, dt_weight.T)
-    weights = exchange(rows, SEQ).reshape(-1, 512)
-    params = jnp.stack(
-        [decay_rate.reshape(-1), dt_bias.reshape(-1), jnp.tile(skip_gain, 2)], 1
-    )
+    here = exchange(rows, ZY).reshape(-1, 512)
+    there = lax.ppermute(here, CORE, SWAP)
+    params = jnp.stack([decay_rate.reshape(-1), dt_bias.reshape(-1), jnp.tile(skip_gain, 2)], 1)
     params = jnp.pad(params, ((0, 4), (0, 125)))
-    sums, pre, bc, cot, vec = project(order, parts, weights, params)
+    sums, pre, bc, cot, vec = project(order, parts, here, there, params)
     sums = exchange(sums.reshape(64, 8, 128), SEQ).reshape(512, 128)
     mixed, dgated, dbc, extra = within(pre, bc, cot, vec, params)
     back = exchange(carry(sums).reshape(64, 8, 128), SEQ).reshape(512, 128)
-    wide, grads = finish(
-        order, parts, weights, params, pre, bc, cot, vec, mixed, dgated, dbc, extra, back
-    )
-    grads = exchange(grads.reshape(64, 8, 512), SEQ)
+    wide, keep, give = finish(
+        order, parts, here, there, params, pre, bc, cot, vec, mixed, dgated, dbc, extra, back
+    )
+    grads = join(keep, lax.ppermute(give, CORE, SWAP))
+    grads = exchange(grads.reshape(32, 8, 512), ZY)
     wide, in_weight_grad, out_rows, dt_rows, rate_grad, bias_grad, skip_grad = add_rows(
         grads, wide, decay_rate, scale
     )

time: 137 us -> 122 us (0.89)
  the two profiles are of different devices: /device:TPU:8 before, /device:TPU:16 now
where the time goes in v4:
time: 122 us; the launch traced here: 121 us
  blocking collectives  50.6 us (41%)
  starting transfers between devices  39.2 us (32%)
  waiting for transfers between devices  18.8 us (15%)
  Pallas kernels  9.63 us (8%)
  local copies, waits for them, and re-layouts  2.19 us (2%)
    all_to_all x3, blocking collectives, exchange(): return lax.all_to_all(array, axis, 0, 0, tiled=True)  50.6 us
    all_to_all x2, starting transfers between devices, exchange(): return lax.all_to_all(array, axis, 0, 0, tiled=True)  20.1 us
    all_to_all x2, waiting for transfers between devices, exchange(): return lax.all_to_all(array, axis, 0, 0, tiled=True)  13.4 us
    ppermute x3, starting transfers between devices, body(): lax.ppermute(pair, 'chan_0', [(k, (k + d) % 4) for k in range(4)])  10.2 us
    pallas_call x8, Pallas kernels, call(): pl.pallas_call(kernel, out_shape=[jax.ShapeDtypeStruct(s, d) for s, d in...  9.63 us
    ppermute x1, starting transfers between devices, body(): other = lax.ppermute(own, 'chan_1', SWAP)  5.04 us
    ppermute x3, waiting for transfers between devices, body(): lax.ppermute(pair, 'chan_0', [(k, (k + d) % 4) for k in range(4)])  4.02 us
  transfers between devices with their start and end apart: 8, of which 5 were waited for; matrix products, arithmetic and copies ran while one was open for 0% of the time, Pallas kernels for 1%

profile of v4, /device:TPU:16, one launch (start us, length us, event | category | flops | bytes accessed | tf_op | source)
XLA Modules:
  0.0 121.4 jit_solution(4940152687248563842)
XLA Ops:
  0.6 1.6 %shard_map.152 = (bf16[128,256]{1,0:T(8,128)(2,1)}, bf16[32,8,512]{2,1,0:T(8,128)(2,1)}) custom-call(bf16[64,256]{1,0:T(8,128)(2,1)} %bitcast.30, bf16[64,256]{1,0:T(8,128)(2,1)} %bitcast.31, bf16[8,128]{1,0:T(8,128)(2,1)} %refs_2_.1, bf16[8,128]{1,0:T(8,128)(2,1)} %refs_3_.1, bf16[8,128]{1,0:T(8,128)(2,1)} %bitcast.32, bf16[2,8]{1,0:T(2,128)(2,1)} %bitcast.33), custom_call_target="tpu_custom_call" | custom-call | flops 1000000 | bytes 71712 | tf_op jit(solution)/shard_map/pallas_call | solution.py:262
  2.2 0.0 copy-start.1
  2.2 14.0 %all-to-all-start = ((bf16[32,8,512]{2,1,0:T(8,128)(2,1)}), bf16[32,8,512]{2,1,0:T(8,128)(2,1)S(1)}, u32[]{:S(2)}, u32[]{:S(2)}) async-start(bf16[32,8,512]{2,1,0:T(8,128)(2,1)} %get-tuple-element.44), calls=%async_computation | async-start | bytes 524288 | tf_op jit(solution)/shard_map/all_to_all | solution.py:549
  16.2 0.0 copy-done.1
  16.2 5.0 %collective-permute-start = (bf16[128,256]{1,0:T(8,128)(2,1)S(1)}, bf16[128,256]{1,0:T(8,128)(2,1)S(1)}, u32[]{:S(2)}, u32[]{:S(2)}) collective-permute-start(bf16[128,256]{1,0:T(8,128)(2,1)S(1)} %copy-done.1), channel_id=1, source_target_pairs={{0,1},{1,0},{2,3},{3,2},{4,5},{5,4},{6,7},{7,6},{8,9},{9,8},{10,11... | collective-permute-start | bytes 196616 | tf_op jit(solution)/shard_map/ppermute | solution.py:566
  21.3 5.8 %all-to-all-done = bf16[32,8,512]{2,1,0:T(8,128)(2,1)S(1)} async-done(((bf16[32,8,512]{2,1,0:T(8,128)(2,1)}), bf16[32,8,512]{2,1,0:T(8,128)(2,1)S(1)}, u32[]{:S(2)}, u32[]{:S(2)}) %all-to-all-start) | async-done | bytes 262176 | tf_op jit(solution)/shard_map/all_to_all | solution.py:549
  27.1 1.9 %collective-permute-start.4 = (bf16[256,512]{1,0:T(8,128)(2,1)S(1)}, bf16[256,512]{1,0:T(8,128)(2,1)S(1)}, u32[]{:S(2)}, u32[]{:S(2)}) collective-permute-start(bf16[256,512]{1,0:T(8,128)(2,1)S(1)} %bitcast.23), channel_id=1, source_target_pairs={{0,8},{8,0},{1,9},{9,1},{2,10},{10,2},{3,11},{11,3},{4,12},{12,4},... | collective-permute-start | bytes 786440 | tf_op jit(solution)/shard_map/ppermute | solution.py:573
  29.0 0.0 collective-permute-done
  29.0 4.7 %collective-permute-start.3 = (bf16[256,256]{1,0:T(8,128)(2,1)S(1)}, bf16[256,256]{1,0:T(8,128)(2,1)S(1)}, u32[]{:S(2)}, u32[]{:S(2)}) collective-permute-start(bf16[256,256]{1,0:T(8,128)(2,1)S(1)} %constant_dynamic-update-slice_fusion.refs_1_), channel_id=1, source_target_pairs={{0,6},{2,0},{4,2},{6,4},{1,7},{3,1},{5,3},{7,5},{8,14},{10,8},{12,... | collective-permute-start | bytes 393224 | tf_op jit(solution)/shard_map/ppermute | solution.py:569
  33.7 2.7 %collective-permute-start.2 = (bf16[256,256]{1,0:T(8,128)(2,1)S(1)}, bf16[256,256]{1,0:T(8,128)(2,1)S(1)}, u32[]{:S(2)}, u32[]{:S(2)}) collective-permute-start(bf16[256,256]{1,0:T(8,128)(2,1)S(1)} %constant_dynamic-update-slice_fusion.refs_1_), channel_id=1, source_target_pairs={{0,4},{2,6},{4,0},{6,2},{1,5},{3,7},{5,1},{7,3},{8,12},{10,14},{12... | collective-permute-start | bytes 393224 | tf_op jit(solution)/shard_map/ppermute | solution.py:569
  36.4 2.8 %collective-permute-start.1 = (bf16[256,256]{1,0:T(8,128)(2,1)S(1)}, bf16[256,256]{1,0:T(8,128)(2,1)S(1)}, u32[]{:S(2)}, u32[]{:S(2)}) collective-permute-start(bf16[256,256]{1,0:T(8,128)(2,1)S(1)} %constant_dynamic-update-slice_fusion.refs_1_), channel_id=1, source_target_pairs={{0,2},{2,4},{4,6},{6,0},{1,3},{3,5},{5,7},{7,1},{8,10},{10,12},{12... | collective-permute-start | bytes 393224 | tf_op jit(solution)/shard_map/ppermute | solution.py:569
  39.3 0.0 copy-start.3
  39.3 0.6 copy-done.3
  39.9 0.0 copy-start.2
  39.9 0.1 stack_tile.4
  40.0 0.6 copy-done.2
  40.6 0.0 copy-start
  40.6 0.1 stack_reshape.9
  40.7 0.6 copy-done
  41.3 0.1 stack_reshape.8
  41.4 0.1 stack.42.refs_0_
  41.5 0.1 select_maximum_fusion.refs_7_.refs_4_
  41.5 0.0 collective-permute-done.3.refs_4_
  41.5 1.9 %collective-permute-done.2.refs_3_ = bf16[256,256]{1,0:T(8,128)(2,1)S(1)} collective-permute-done((bf16[256,256]{1,0:T(8,128)(2,1)S(1)}, bf16[256,256]{1,0:T(8,128)(2,1)S(1)}, u32[]{:S(2)}, u32[]{:S(2)}) %collective-permute-start.2) | collective-permute-done | bytes 131104 | tf_op jit(solution)/shard_map/ppermute | solution.py:569
  43.5 2.1 %collective-permute-done.1.refs_2_ = bf16[256,256]{1,0:T(8,128)(2,1)S(1)} collective-permute-done((bf16[256,256]{1,0:T(8,128)(2,1)S(1)}, bf16[256,256]{1,0:T(8,128)(2,1)S(1)}, u32[]{:S(2)}, u32[]{:S(2)}) %collective-permute-start.1) | collective-permute-done | bytes 131104 | tf_op jit(solution)/shard_map/ppermute | solution.py:569
  45.6 0.0 collective-permute-done.4.refs_6_
  45.6 1.6 %shard_map.153 = (bf16[512,128]{1,0:T(8,128)(2,1)S(1)}, f32[128,256]{1,0:T(8,128)S(1)}, f32[128,256]{1,0:T(8,128)S(1)}, f32[128,256]{1,0:T(8,128)S(1)}, f32[48,256]{1,0:T(8,128)S(1)}) custom-call(s32[9]{0:T(128)S(1)} %stack.42.refs_0_, bf16[256,256]{1,0:T(8,128)(2,1)S(1)} %constant_dynamic-update-slice_fusion.refs_1_, ...), custom_call_target="tpu_custom_call" | custom-call | flops 300000000 | bytes 1052708 | tf_op jit(solution)/shard_map/pallas_call | solution.py:262
  47.1 16.4 %all_to_all.25 = bf16[64,8,128]{2,1,0:T(8,128)(2,1)S(1)} all-to-all(bf16[64,8,128]{2,1,0:T(8,128)(2,1)S(1)} %bitcast.29), channel_id=1, replica_groups=mesh['seq_0'=8,'seq_1'=4,'seq_2'=2,'chan_0'=4,'chan_1'=2] {'seq_0','seq_..., dimensions={0} | all-to-all | bytes 262144 | tf_op jit(solution)/shard_map/all_to_all | solution.py:549
  63.5 1.0 shard_map.155
  64.5 6.1 %all-to-all-start.2 = ((bf16[64,8,128]{2,1,0:T(8,128)(2,1)}), bf16[64,8,128]{2,1,0:T(8,128)(2,1)S(1)}, u32[]{:S(2)}, u32[]{:S(2)}) async-start(bf16[64,8,128]{2,1,0:T(8,128)(2,1)} %bitcast.16), calls=%async_computation.2 | async-start | bytes 262144 | tf_op jit(solution)/shard_map/all_to_all | solution.py:549
  70.6 1.7 %shard_map.154 = (f32[256,256]{1,0:T(8,128)S(1)}, f32[256,256]{1,0:T(8,128)S(1)}, f32[128,256]{1,0:T(8,128)S(1)}, f32[24,256]{1,0:T(8,128)S(1)}) custom-call(f32[128,256]{1,0:T(8,128)S(1)} %get-tuple-element.45.refs_0_.refs_8_, f32[128,256]{1,0:T(8,128)S(1)} %get-tuple-element.46.refs_1_.refs_9_, f32[128,256]{1,0:T(8,128)S(1)} %get-tuple-element.47.refs_2_.refs_10_, ...), custom_call_target="tpu_custom_call" | custom-call | flops 300000000 | bytes 446464 | tf_op jit(solution)/shard_map/pallas_call | solution.py:262
  72.3 7.6 %all-to-all-done.2 = bf16[64,8,128]{2,1,0:T(8,128)(2,1)S(1)} async-done(((bf16[64,8,128]{2,1,0:T(8,128)(2,1)}), bf16[64,8,128]{2,1,0:T(8,128)(2,1)S(1)}, u32[]{:S(2)}, u32[]{:S(2)}) %all-to-all-start.2) | async-done | bytes 131104 | tf_op jit(solution)/shard_map/all_to_all | solution.py:549
  79.9 2.1 %shard_map.156 = (bf16[8,72,256]{2,1,0:T(8,128)(2,1)S(1)}, f32[256,512]{1,0:T(8,128)S(1)}, bf16[256,512]{1,0:T(8,128)(2,1)S(1)}) custom-call(s32[9]{0:T(128)S(1)} %stack.42.refs_0_, bf16[256,256]{1,0:T(8,128)(2,1)S(1)} %constant_dynamic-update-slice_fusion.refs_1_, bf16[256,256]{1,0:T(8,128)(2,1)S(1)} %collective-permute-done.1.refs_2_, ...), custom_call_target="tpu_custom_call" | custom-call | flops 600000000 | bytes 2306084 | tf_op jit(solution)/shard_map/pallas_call | solution.py:262
  82.1 2.0 %collective-permute-start.5 = (bf16[256,512]{1,0:T(8,128)(2,1)S(1)}, bf16[256,512]{1,0:T(8,128)(2,1)S(1)}, u32[]{:S(2)}, u32[]{:S(2)}) collective-permute-start(bf16[256,512]{1,0:T(8,128)(2,1)S(1)} %get-tuple-element.56), channel_id=1, source_target_pairs={{0,8},{8,0},{1,9},{9,1},{2,10},{10,2},{3,11},{11,3},{4,12},{12,4},... | collective-permute-start | bytes 786440 | tf_op jit(solution)/shard_map/ppermute | solution.py:583
  84.1 1.4 %collective-permute-done.5.refs_1_ = bf16[256,512]{1,0:T(8,128)(2,1)S(1)} collective-permute-done((bf16[256,512]{1,0:T(8,128)(2,1)S(1)}, bf16[256,512]{1,0:T(8,128)(2,1)S(1)}, u32[]{:S(2)}, u32[]{:S(2)}) %collective-permute-start.5) | collective-permute-done | bytes 262176 | tf_op jit(solution)/shard_map/ppermute | solution.py:583
  85.5 0.2 shard_map.157
  85.7 16.3 %all_to_all.26.refs_0_ = bf16[32,8,512]{2,1,0:T(8,128)(2,1)S(1)} all-to-all(bf16[32,8,512]{2,1,0:T(8,128)(2,1)S(1)} %bitcast.26), channel_id=1, replica_groups=mesh['seq_0'=8,'seq_1'=4,'seq_2'=2,'chan_0'=4,'chan_1'=2] {'seq_0','seq_1'}, dimensions={0} | all-to-all | bytes 524288 | tf_op jit(solution)/shard_map/all_to_all | solution.py:549
  101.9 0.8 shard_map.158
  102.7 18.0 %all_to_all.27.refs_0_ = bf16[8,72,256]{2,1,0:T(8,128)(2,1)S(1)} all-to-all(bf16[8,72,256]{2,1,0:T(8,128)(2,1)S(1)} %constant_dynamic-update-slice_fusion.2), channel_id=1, replica_groups=mesh['seq_0'=8,'seq_1'=4,'seq_2'=2,'chan_0'=4,'chan_1'=2] {'chan_0','cha..., dimensions={0} | all-to-all | bytes 589824 | tf_op jit(solution)/shard_map/all_to_all | solution.py:549
  120.7 0.7 shard_map.159
  (4 shorter events, 0.0 us)
Async XLA Ops:
  2.2 14.0 %copy-start.1 = (bf16[128,256]{1,0:T(8,128)(2,1)S(1)}, bf16[128,256]{1,0:T(8,128)(2,1)}, u32[]{:S(2)}) copy-start(bf16[128,256]{1,0:T(8,128)(2,1)} %get-tuple-element.43) | copy-start | bytes 196612
  2.2 24.8 %all-to-all-start = ((bf16[32,8,512]{2,1,0:T(8,128)(2,1)}), bf16[32,8,512]{2,1,0:T(8,128)(2,1)S(1)}, u32[]{:S(2)}, u32[]{:S(2)}) async-start(bf16[32,8,512]{2,1,0:T(8,128)(2,1)} %get-tuple-element.44), calls=%async_computation | async-start | bytes 524288 | tf_op jit(solution)/shard_map/all_to_all | solution.py:549
  16.2 12.8 %collective-permute-start = (bf16[128,256]{1,0:T(8,128)(2,1)S(1)}, bf16[128,256]{1,0:T(8,128)(2,1)S(1)}, u32[]{:S(2)}, u32[]{:S(2)}) collective-permute-start(bf16[128,256]{1,0:T(8,128)(2,1)S(1)} %copy-done.1), channel_id=1, source_target_pairs={{0,1},{1,0},{2,3},{3,2},{4,5},{5,4},{6,7},{7,6},{8,9},{9,8},{10,11... | collective-permute-start | bytes 196616 | tf_op jit(solution)/shard_map/ppermute | solution.py:566
  27.1 18.5 %collective-permute-start.4 = (bf16[256,512]{1,0:T(8,128)(2,1)S(1)}, bf16[256,512]{1,0:T(8,128)(2,1)S(1)}, u32[]{:S(2)}, u32[]{:S(2)}) collective-permute-start(bf16[256,512]{1,0:T(8,128)(2,1)S(1)} %bitcast.23), channel_id=1, source_target_pairs={{0,8},{8,0},{1,9},{9,1},{2,10},{10,2},{3,11},{11,3},{4,12},{12,4},... | collective-permute-start | bytes 786440 | tf_op jit(solution)/shard_map/ppermute | solution.py:573
  29.0 12.5 %collective-permute-start.3 = (bf16[256,256]{1,0:T(8,128)(2,1)S(1)}, bf16[256,256]{1,0:T(8,128)(2,1)S(1)}, u32[]{:S(2)}, u32[]{:S(2)}) collective-permute-start(bf16[256,256]{1,0:T(8,128)(2,1)S(1)} %constant_dynamic-update-slice_fusion.refs_1_), channel_id=1, source_target_pairs={{0,6},{2,0},{4,2},{6,4},{1,7},{3,1},{5,3},{7,5},{8,14},{10,8},{12,... | collective-permute-start | bytes 393224 | tf_op jit(solution)/shard_map/ppermute | solution.py:569
  33.7 9.8 %collective-permute-start.2 = (bf16[256,256]{1,0:T(8,128)(2,1)S(1)}, bf16[256,256]{1,0:T(8,128)(2,1)S(1)}, u32[]{:S(2)}, u32[]{:S(2)}) collective-permute-start(bf16[256,256]{1,0:T(8,128)(2,1)S(1)} %constant_dynamic-update-slice_fusion.refs_1_), channel_id=1, source_target_pairs={{0,4},{2,6},{4,0},{6,2},{1,5},{3,7},{5,1},{7,3},{8,12},{10,14},{12... | collective-permute-start | bytes 393224 | tf_op jit(solution)/shard_map/ppermute | solution.py:569
  36.4 9.2 %collective-permute-start.1 = (bf16[256,256]{1,0:T(8,128)(2,1)S(1)}, bf16[256,256]{1,0:T(8,128)(2,1)S(1)}, u32[]{:S(2)}, u32[]{:S(2)}) collective-permute-start(bf16[256,256]{1,0:T(8,128)(2,1)S(1)} %constant_dynamic-update-slice_fusion.refs_1_), channel_id=1, source_target_pairs={{0,2},{2,4},{4,6},{6,0},{1,3},{3,5},{5,7},{7,1},{8,10},{10,12},{12... | collective-permute-start | bytes 393224 | tf_op jit(solution)/shard_map/ppermute | solution.py:569
  39.3 0.7 copy-start.3
  39.9 0.7 copy-start.2
  40.6 0.7 copy-start
  64.5 15.4 %all-to-all-start.2 = ((bf16[64,8,128]{2,1,0:T(8,128)(2,1)}), bf16[64,8,128]{2,1,0:T(8,128)(2,1)S(1)}, u32[]{:S(2)}, u32[]{:S(2)}) async-start(bf16[64,8,128]{2,1,0:T(8,128)(2,1)} %bitcast.16), calls=%async_computation.2 | async-start | bytes 262144 | tf_op jit(solution)/shard_map/all_to_all | solution.py:549
  82.1 3.4 %collective-permute-start.5 = (bf16[256,512]{1,0:T(8,128)(2,1)S(1)}, bf16[256,512]{1,0:T(8,128)(2,1)S(1)}, u32[]{:S(2)}, u32[]{:S(2)}) collective-permute-start(bf16[256,512]{1,0:T(8,128)(2,1)S(1)} %get-tuple-element.56), channel_id=1, source_target_pairs={{0,8},{8,0},{1,9},{9,1},{2,10},{10,2},{3,11},{11,3},{4,12},{12,4},... | collective-permute-start | bytes 786440 | tf_op jit(solution)/shard_map/ppermute | solution.py:583

commit v5 on v4

--- a/solution.py
+++ b/solution.py
@@ -36,10 +36,15 @@
     return low(xt, yt, dims) + (low(xt, yl, dims) + low(xl, yt, dims))
 
 
-def exact(x, y, dims):
-    return lax.dot_general(
-        x, y, dims, precision=lax.Precision.HIGHEST, preferred_element_type=F32
-    )
+def running(x):
+    n = x.shape[1]
+    top, rest = halves(x)
+    low_ = (x - top.astype(F32) - rest.astype(F32)).astype(BF16)
+    parts = jnp.concatenate([top.astype(F32), rest.astype(F32), low_.astype(F32)], 0)
+    both = jnp.concatenate([before(n), before(n, True)], 1)
+    sums = low(parts, both, NN)
+    sums = sums[:8] + (sums[8:16] + sums[16:24])
+    return sums[:, :n], sums[:, n:]
 
 
 def before(n, flip=False):
@@ -79,9 +84,8 @@
     step = jnp.maximum(v, 0.0) + jnp.log1p(jnp.exp(-jnp.abs(v)))
     slope = sigmoid(v)
     decay = -rate * step
-    run = jnp.where(
-        forward_rows(n), exact(decay, before(n), NN), exact(decay, before(n, True), NN)
-    )
+    from_start, from_end = running(decay)
+    run = jnp.where(forward_rows(n), from_start, from_end)
     total = jnp.sum(decay, axis=1, keepdims=True)
     grown = jnp.exp(run)
     tail = jnp.exp(total - run)
@@ -207,9 +211,8 @@
     ]
     ends = jnp.concatenate(ends + [jnp.zeros((4, 1), F32)], 0)
     ends = kept * ends + jnp.sum(lost, axis=1, keepdims=True)
-    ddecay = ends + jnp.where(
-        forward_rows(n), exact(drun, before(n, True), NN), exact(drun, before(n), NN)
-    )
+    from_start, from_end = running(drun)
+    ddecay = ends + jnp.where(forward_rows(n), from_end, from_start)
     dstep = extra[0:8] + falls - rate * ddecay
     valid = lax.broadcasted_iota(jnp.int32, (8, n), 0) < 4
     dz = jnp.where(valid, dstep * slope, 0.0)
@@ -272,8 +275,8 @@
 
 def gathered(order, parts, own, other):
     if PLAIN:
-        n = parts[0].shape[1]
-        blocks = jnp.concatenate(parts, 0).reshape(8, 2, 2, 32, n)
+        n = parts.shape[1]
+        blocks = parts.reshape(8, 2, 2, 32, n)
         mine = order[8]
         u, q = (
             jnp.concatenate([blocks[:, k, mine], blocks[:, k, 1 - mine]], 0).reshape(512, n)
@@ -285,9 +288,9 @@
     up, down, rows = [], [], []
     for at, weights in ((mine, own), (32 - mine, other)):
         for k in range(8):
-            part, base = parts[k // 2], 128 * (k % 2)
-            up.append(part[pl.ds(pl.multiple_of(base + at, 32), 32), :])
-            down.append(part[pl.ds(pl.multiple_of(base + 64 + at, 32), 32), :])
+            base = 128 * k
+            up.append(parts[pl.ds(pl.multiple_of(base + at, 32), 32), :])
+            down.append(parts[pl.ds(pl.multiple_of(base + 64 + at, 32), 32), :])
             rows.append(weights[pl.ds(pl.multiple_of(order[k] * 32, 32), 32), :])
     return jnp.concatenate(up, 0), jnp.concatenate(down, 0), jnp.concatenate(rows, 0)
 
@@ -298,17 +301,17 @@
         return (jnp.stack(sends, 1).reshape(512, 128).astype(BF16), *rest)
 
     def fn(ins, outs, lines):
-        sends, *rest = stage_project(*gathered(ins[0], ins[1:5], ins[5], ins[6]), ins[7][...])
+        sends, *rest = stage_project(*gathered(*ins[:4]), ins[4][...])
         for j, part in enumerate(sends):
             lines[pl.ds(j, STATE, stride=8), :] = part
         outs[0][...] = lines[...].astype(BF16)
         for ref, value in zip(outs[1:], rest):
             ref[...] = value
 
-    n = parts[0].shape[1]
+    n = parts.shape[1]
     outs = [((512, 128), BF16), ((128, n), F32), ((128, n), F32), ((128, n), F32), ((48, n), F32)]
     lines = pltpu.VMEM((512, 128), F32)
-    return call(fn, outs, (order, *parts, own, other, params), 300_000_000, (lines,), 1)
+    return call(fn, outs, (order, parts, own, other, params), 300_000_000, (lines,), 1)
 
 
 def within(pre, bc, cot, vec, params):
@@ -348,7 +351,7 @@
             for j in range(4)
         ]
         dinput, grads = stage_finish(
-            *gathered(order, ins[1:5], ins[5], ins[6]), *(r[...] for r in ins[7:-1]), carried
+            *gathered(*ins[:4]), *(r[...] for r in ins[4:-1]), carried
         )
         dinput = dinput.astype(BF16)
         give = grads[256:].astype(BF16)
@@ -365,7 +368,7 @@
 
     outs = [((8, 72, n), BF16), ((256, 512), F32), ((256, 512), BF16)]
     lines = pltpu.VMEM((512, 128), F32)
-    args = (order, *parts, own, other, *more, back)
+    args = (order, parts, own, other, *more, back)
     return call(fn, outs, args, 600_000_000, (lines,), 1)
 
 
@@ -446,8 +449,8 @@
     return call(fn, [((8 * count, 128), BF16)], (blocks,), 1_000_000, scratch)[0]
 
 
-def pack(tokens, cotangents, in_weight, bc_weight, out_rows, dt_rows):
-    def fill(tok, cot, inw, bcw, outw, dtw):
+def pack(*args):
+    def fill(tok, cot, inw, bcw, outw, dtw, rates, biases, gains):
         blocks = []
         for x in (tok.astype(F32), cot.astype(F32)):
             for odd in (0, 8):
@@ -462,17 +465,28 @@
             column = jnp.sum(jnp.where(square, row, 0.0), axis=1, keepdims=True)
             last = jnp.where(lane == k, column, last)
         rows = jnp.concatenate([inw, bcw, outw, last.astype(BF16)], 1)
-        return jnp.concatenate(blocks, 0).astype(BF16), jnp.broadcast_to(rows[None], (32, 8, 512))
-
-    args = (tokens, cotangents, in_weight, bc_weight, out_rows, dt_rows)
+        sub = lax.broadcasted_iota(jnp.int32, (8, 128), 0)
+        table = jnp.zeros((8, 128), F32)
+        for k in range(4):
+            r, h = k // 2, k % 2
+            values = (rates[r : r + 1, h : h + 1], biases[r : r + 1, h : h + 1], gains[:, h : h + 1])
+            for at, value in enumerate(values):
+                table = jnp.where((sub == k) & (lane == at), value, table)
+        return (
+            jnp.concatenate(blocks, 0).astype(BF16),
+            jnp.broadcast_to(rows[None], (32, 8, 512)),
+            table,
+        )
+
     if PLAIN:
         return fill(*args)
 
     def fn(ins, outs):
-        outs[0][...], outs[1][...] = fill(*(r[...] for r in ins))
-
-    n = tokens.shape[1]
-    return call(fn, [((128, n), BF16), ((32, 8, 512), BF16)], args, 1_000_000, grant=None)
+        for ref, value in zip(outs, fill(*(r[...] for r in ins))):
+            ref[...] = value
+
+    outs = [((128, args[0].shape[1]), BF16), ((32, 8, 512), BF16), ((8, 128), F32)]
+    return call(fn, outs, args, 1_000_000, grant=None)
 
 
 def add_rows(grads, wide, decay_rate, scale):
@@ -555,24 +569,26 @@
     seq_count = lax.axis_size(SEQ)
     tok_rows = tokens.shape[0]
     scale = (tok_rows * seq_count) ** (-0.5)
-    own, rows = pack(
-        tokens.T, out_grad.T, in_weight, bc_weight, out_weight.T, dt_weight.T
-    )
-    across, around = lax.axis_index("chan_0"), lax.axis_index("chan_1")
+    own, rows, params = pack(
+        tokens.T,
+        out_grad.T,
+        in_weight,
+        bc_weight,
+        out_weight.T,
+        dt_weight.T,
+        decay_rate,
+        dt_bias,
+        skip_gain.reshape(1, -1),
+    )
+    around = lax.axis_index("chan_1")
     order = jnp.stack(
-        [((across - d) % 4) * 2 + (around ^ e) for d in range(4) for e in range(2)]
-        + [lax.axis_index(CORE)]
+        [2 * k + (around ^ e) for k in range(4) for e in range(2)] + [lax.axis_index(CORE)]
     ).astype(jnp.int32)
     other = lax.ppermute(own, "chan_1", SWAP)
     pair = jnp.concatenate([own, other], 0)
-    parts = [pair] + [
-        lax.ppermute(pair, "chan_0", [(k, (k + d) % 4) for k in range(4)])
-        for d in (1, 2, 3)
-    ]
+    parts = lax.all_gather(pair, "chan_0", axis=0, tiled=True)
     here = exchange(rows, ZY).reshape(-1, 512)
     there = lax.ppermute(here, CORE, SWAP)
-    params = jnp.stack([decay_rate.reshape(-1), dt_bias.reshape(-1), jnp.tile(skip_gain, 2)], 1)
-    params = jnp.pad(params, ((0, 4), (0, 125)))
     sums, pre, bc, cot, vec = project(order, parts, here, there, params)
     sums = exchange(sums.reshape(64, 8, 128), SEQ).reshape(512, 128)
     mixed, dgated, dbc, extra = within(pre, bc, cot, vec, params)

time: 122 us -> 121 us (level)
  blocking collectives: 50.6 us -> 66.3 us
  starting transfers between devices: 39.2 us -> 29 us
  waiting for transfers between devices: 18.8 us -> 14.7 us
  local copies, waits for them, and re-layouts: 2.19 us -> 0.11 us
    all_gather x0 -> x1, blocking collectives: none -> 13.4 us  [body(): parts = lax.all_gather(pair, 'chan_0', axis=0, tiled=True)]
    ppermute x3 -> x0, starting transfers between devices: 10.2 us -> none  [body(): lax.ppermute(pair, 'chan_0', [(k, (k + d) % 4) for k in range(4)])]
    ppermute x3 -> x0, waiting for transfers between devices: 4.02 us -> none  [body(): lax.ppermute(pair, 'chan_0', [(k, (k + d) % 4) for k in range(4)])]
    all_to_all x3, blocking collectives: 50.6 us -> 53 us  [exchange(): return lax.all_to_all(array, axis, 0, 0, tiled=True)]
    unnamed x9 -> x6, local copies, waits for them, and re-layouts: 1.85 us -> 0.02 us
  transfers between devices with their start and end apart: 8 -> 5, of which waited for: 5 -> 3; matrix products, arithmetic and copies ran while one was open for 0% -> 0% of each run, Pallas kernels for 1% -> 1%
where the time goes in v5:
time: 121 us; the launch traced here: 120 us
  blocking collectives  66.3 us (55%)
  starting transfers between devices  29 us (24%)
  waiting for transfers between devices  14.7 us (12%)
  Pallas kernels  9.37 us (8%)
    all_to_all x3, blocking collectives, exchange(): return lax.all_to_all(array, axis, 0, 0, tiled=True)  53 us
    all_to_all x2, starting transfers between devices, exchange(): return lax.all_to_all(array, axis, 0, 0, tiled=True)  20.1 us
    all_gather x1, blocking collectives, body(): parts = lax.all_gather(pair, 'chan_0', axis=0, tiled=True)  13.4 us
    all_to_all x2, waiting for transfers between devices, exchange(): return lax.all_to_all(array, axis, 0, 0, tiled=True)  13.3 us
    pallas_call x8, Pallas kernels, call(): pl.pallas_call(kernel, out_shape=[jax.ShapeDtypeStruct(s, d) for s, d in...  9.37 us
    ppermute x1, starting transfers between devices, body(): other = lax.ppermute(own, 'chan_1', SWAP)  5.04 us
  transfers between devices with their start and end apart: 5, of which 3 were waited for; matrix products, arithmetic and copies ran while one was open for 0% of the time, Pallas kernels for 1%

profile of v5, /device:TPU:16, one launch (start us, length us, event | category | flops | bytes accessed | tf_op | source)
XLA Modules:
  0.0 120.3 jit_solution(1592600350255504867)
XLA Ops:
  0.6 1.7 %shard_map.152 = (bf16[128,256]{1,0:T(8,128)(2,1)}, bf16[32,8,512]{2,1,0:T(8,128)(2,1)}, f32[8,128]{1,0:T(8,128)}) custom-call(bf16[64,256]{1,0:T(8,128)(2,1)} %bitcast.31, bf16[64,256]{1,0:T(8,128)(2,1)} %bitcast.32, bf16[8,128]{1,0:T(8,128)(2,1)} %refs_2_.1, bf16[8,128]{1,0:T(8,128)(2,1)} %refs_3_.1, bf16[8,128]{1,0:T(8,128)(2,1)} %bitcast.33, ...), custom_call_target="tpu_custom_call" | custom-call | flops 1000000 | bytes 71752 | tf_op jit(solution)/shard_map/pallas_call | solution.py:265
  2.3 0.0 copy-start.2
  2.3 14.0 %all-to-all-start = ((bf16[32,8,512]{2,1,0:T(8,128)(2,1)}), bf16[32,8,512]{2,1,0:T(8,128)(2,1)S(1)}, u32[]{:S(2)}, u32[]{:S(2)}) async-start(bf16[32,8,512]{2,1,0:T(8,128)(2,1)} %get-tuple-element.45), calls=%async_computation | async-start | bytes 524288 | tf_op jit(solution)/shard_map/all_to_all | solution.py:563
  16.3 0.0 copy-done.2
  16.3 5.0 %collective-permute-start = (bf16[128,256]{1,0:T(8,128)(2,1)S(1)}, bf16[128,256]{1,0:T(8,128)(2,1)S(1)}, u32[]{:S(2)}, u32[]{:S(2)}) collective-permute-start(bf16[128,256]{1,0:T(8,128)(2,1)S(1)} %copy-done.2), channel_id=1, source_target_pairs={{0,1},{1,0},{2,3},{3,2},{4,5},{5,4},{6,7},{7,6},{8,9},{9,8},{10,11... | collective-permute-start | bytes 196616 | tf_op jit(solution)/shard_map/ppermute | solution.py:587
  21.3 0.1 stack.39.refs_0_
  21.4 5.7 %all-to-all-done = bf16[32,8,512]{2,1,0:T(8,128)(2,1)S(1)} async-done(((bf16[32,8,512]{2,1,0:T(8,128)(2,1)}), bf16[32,8,512]{2,1,0:T(8,128)(2,1)S(1)}, u32[]{:S(2)}, u32[]{:S(2)}) %all-to-all-start) | async-done | bytes 262176 | tf_op jit(solution)/shard_map/all_to_all | solution.py:563
  27.1 1.9 %collective-permute-start.1 = (bf16[256,512]{1,0:T(8,128)(2,1)S(1)}, bf16[256,512]{1,0:T(8,128)(2,1)S(1)}, u32[]{:S(2)}, u32[]{:S(2)}) collective-permute-start(bf16[256,512]{1,0:T(8,128)(2,1)S(1)} %bitcast.24), channel_id=1, source_target_pairs={{0,8},{8,0},{1,9},{9,1},{2,10},{10,2},{3,11},{11,3},{4,12},{12,4},... | collective-permute-start | bytes 786440 | tf_op jit(solution)/shard_map/ppermute | solution.py:591
  29.0 0.0 collective-permute-done
  29.1 0.0 copy-start
  29.1 13.4 %all_gather.3.refs_1_ = bf16[1024,256]{1,0:T(8,128)(2,1)S(1)} all-gather(bf16[256,256]{1,0:T(8,128)(2,1)S(1)} %pad_maximum_fusion), channel_id=1, replica_groups=mesh['seq_0'=8,'seq_1'=4,'seq_2'=2,'chan_0'=4,'chan_1'=2] {'chan_0'}, dimensions={0}, use_global_device_ids=true | all-gather | bytes 655360 | tf_op jit(solution)/shard_map/all_gather | solution.py:589
  42.5 0.0 collective-permute-done.1.refs_3_
  42.5 0.0 copy-done
  42.5 1.4 %shard_map.153 = (bf16[512,128]{1,0:T(8,128)(2,1)S(1)}, f32[128,256]{1,0:T(8,128)S(1)}, f32[128,256]{1,0:T(8,128)S(1)}, f32[128,256]{1,0:T(8,128)S(1)}, f32[48,256]{1,0:T(8,128)S(1)}) custom-call(s32[9]{0:T(128)S(1)} %stack.39.refs_0_, bf16[1024,256]{1,0:T(8,128)(2,1)S(1)} %all_gather.3.refs_1_, bf16[256,512]{1,0:T(8,128)(2,1)S(1)} %bitcast.25, ...), custom_call_target="tpu_custom_call" | custom-call | flops 300000000 | bytes 1052708 | tf_op jit(solution)/shard_map/pallas_call | solution.py:265
  43.9 16.9 %all_to_all.25 = bf16[64,8,128]{2,1,0:T(8,128)(2,1)S(1)} all-to-all(bf16[64,8,128]{2,1,0:T(8,128)(2,1)S(1)} %bitcast.30), channel_id=1, replica_groups=mesh['seq_0'=8,'seq_1'=4,'seq_2'=2,'chan_0'=4,'chan_1'=2] {'seq_0','seq_..., dimensions={0} | all-to-all | bytes 262144 | tf_op jit(solution)/shard_map/all_to_all | solution.py:563
  60.8 1.0 shard_map.155
  61.8 6.1 %all-to-all-start.2 = ((bf16[64,8,128]{2,1,0:T(8,128)(2,1)}), bf16[64,8,128]{2,1,0:T(8,128)(2,1)S(1)}, u32[]{:S(2)}, u32[]{:S(2)}) async-start(bf16[64,8,128]{2,1,0:T(8,128)(2,1)} %bitcast.17), calls=%async_computation.2 | async-start | bytes 262144 | tf_op jit(solution)/shard_map/all_to_all | solution.py:563
  67.9 1.7 %shard_map.154 = (f32[256,256]{1,0:T(8,128)S(1)}, f32[256,256]{1,0:T(8,128)S(1)}, f32[128,256]{1,0:T(8,128)S(1)}, f32[24,256]{1,0:T(8,128)S(1)}) custom-call(f32[128,256]{1,0:T(8,128)S(1)} %get-tuple-element.47.refs_0_.refs_5_, f32[128,256]{1,0:T(8,128)S(1)} %get-tuple-element.48.refs_1_.refs_6_, f32[128,256]{1,0:T(8,128)S(1)} %get-tuple-element.49.refs_2_.refs_7_, ...), custom_call_target="tpu_custom_call" | custom-call | flops 300000000 | bytes 446464 | tf_op jit(solution)/shard_map/pallas_call | solution.py:265
  69.6 7.6 %all-to-all-done.2 = bf16[64,8,128]{2,1,0:T(8,128)(2,1)S(1)} async-done(((bf16[64,8,128]{2,1,0:T(8,128)(2,1)}), bf16[64,8,128]{2,1,0:T(8,128)(2,1)S(1)}, u32[]{:S(2)}, u32[]{:S(2)}) %all-to-all-start.2) | async-done | bytes 131104 | tf_op jit(solution)/shard_map/all_to_all | solution.py:563
  77.2 2.0 %shard_map.156 = (bf16[8,72,256]{2,1,0:T(8,128)(2,1)S(1)}, f32[256,512]{1,0:T(8,128)S(1)}, bf16[256,512]{1,0:T(8,128)(2,1)S(1)}) custom-call(s32[9]{0:T(128)S(1)} %stack.39.refs_0_, bf16[1024,256]{1,0:T(8,128)(2,1)S(1)} %all_gather.3.refs_1_, bf16[256,512]{1,0:T(8,128)(2,1)S(1)} %bitcast.26, bf16[256,512]{1,0:T(8,128)(2,1)S(1)} %collective-permute-done.1.refs_3_, ...), custom_call_target="tpu_custom_call" | custom-call | flops 600000000 | bytes 2306084 | tf_op jit(solution)/shard_map/pallas_call | solution.py:265
  79.2 2.0 %collective-permute-start.2 = (bf16[256,512]{1,0:T(8,128)(2,1)S(1)}, bf16[256,512]{1,0:T(8,128)(2,1)S(1)}, u32[]{:S(2)}, u32[]{:S(2)}) collective-permute-start(bf16[256,512]{1,0:T(8,128)(2,1)S(1)} %get-tuple-element.58), channel_id=1, source_target_pairs={{0,8},{8,0},{1,9},{9,1},{2,10},{10,2},{3,11},{11,3},{4,12},{12,4},... | collective-permute-start | bytes 786440 | tf_op jit(solution)/shard_map/ppermute | solution.py:599
  81.2 1.4 %collective-permute-done.2.refs_1_ = bf16[256,512]{1,0:T(8,128)(2,1)S(1)} collective-permute-done((bf16[256,512]{1,0:T(8,128)(2,1)S(1)}, bf16[256,512]{1,0:T(8,128)(2,1)S(1)}, u32[]{:S(2)}, u32[]{:S(2)}) %collective-permute-start.2) | collective-permute-done | bytes 262176 | tf_op jit(solution)/shard_map/ppermute | solution.py:599
  82.6 0.2 shard_map.157
  82.8 0.0 copy-start.1
  82.8 16.3 %all_to_all.26.refs_0_ = bf16[32,8,512]{2,1,0:T(8,128)(2,1)S(1)} all-to-all(bf16[32,8,512]{2,1,0:T(8,128)(2,1)S(1)} %bitcast.27), channel_id=1, replica_groups=mesh['seq_0'=8,'seq_1'=4,'seq_2'=2,'chan_0'=4,'chan_1'=2] {'seq_0','seq_1'}, dimensions={0} | all-to-all | bytes 524288 | tf_op jit(solution)/shard_map/all_to_all | solution.py:563
  99.1 0.0 copy-done.1
  99.1 0.8 shard_map.158
  99.9 19.8 %all_to_all.27.refs_0_ = bf16[8,72,256]{2,1,0:T(8,128)(2,1)S(1)} all-to-all(bf16[8,72,256]{2,1,0:T(8,128)(2,1)S(1)} %constant_dynamic-update-slice_fusion), channel_id=1, replica_groups=mesh['seq_0'=8,'seq_1'=4,'seq_2'=2,'chan_0'=4,'chan_1'=2] {'chan_0','cha..., dimensions={0} | all-to-all | bytes 589824 | tf_op jit(solution)/shard_map/all_to_all | solution.py:563
  119.6 0.7 shard_map.159
  (2 shorter events, 0.0 us)
Async XLA Ops:
  2.3 14.0 %copy-start.2 = (bf16[128,256]{1,0:T(8,128)(2,1)S(1)}, bf16[128,256]{1,0:T(8,128)(2,1)}, u32[]{:S(2)}) copy-start(bf16[128,256]{1,0:T(8,128)(2,1)} %get-tuple-element.44) | copy-start | bytes 196612
  2.3 24.8 %all-to-all-start = ((bf16[32,8,512]{2,1,0:T(8,128)(2,1)}), bf16[32,8,512]{2,1,0:T(8,128)(2,1)S(1)}, u32[]{:S(2)}, u32[]{:S(2)}) async-start(bf16[32,8,512]{2,1,0:T(8,128)(2,1)} %get-tuple-element.45), calls=%async_computation | async-start | bytes 524288 | tf_op jit(solution)/shard_map/all_to_all | solution.py:563
  16.3 12.8 %collective-permute-start = (bf16[128,256]{1,0:T(8,128)(2,1)S(1)}, bf16[128,256]{1,0:T(8,128)(2,1)S(1)}, u32[]{:S(2)}, u32[]{:S(2)}) collective-permute-start(bf16[128,256]{1,0:T(8,128)(2,1)S(1)} %copy-done.2), channel_id=1, source_target_pairs={{0,1},{1,0},{2,3},{3,2},{4,5},{5,4},{6,7},{7,6},{8,9},{9,8},{10,11... | collective-permute-start | bytes 196616 | tf_op jit(solution)/shard_map/ppermute | solution.py:587
  27.1 15.3 %collective-permute-start.1 = (bf16[256,512]{1,0:T(8,128)(2,1)S(1)}, bf16[256,512]{1,0:T(8,128)(2,1)S(1)}, u32[]{:S(2)}, u32[]{:S(2)}) collective-permute-start(bf16[256,512]{1,0:T(8,128)(2,1)S(1)} %bitcast.24), channel_id=1, source_target_pairs={{0,8},{8,0},{1,9},{9,1},{2,10},{10,2},{3,11},{11,3},{4,12},{12,4},... | collective-permute-start | bytes 786440 | tf_op jit(solution)/shard_map/ppermute | solution.py:591
  29.1 13.4 %copy-start = (f32[8,128]{1,0:T(8,128)S(1)}, f32[8,128]{1,0:T(8,128)}, u32[]{:S(2)}) copy-start(f32[8,128]{1,0:T(8,128)} %get-tuple-element.46.refs_4_) | copy-start | bytes 12292
  61.8 15.4 %all-to-all-start.2 = ((bf16[64,8,128]{2,1,0:T(8,128)(2,1)}), bf16[64,8,128]{2,1,0:T(8,128)(2,1)S(1)}, u32[]{:S(2)}, u32[]{:S(2)}) async-start(bf16[64,8,128]{2,1,0:T(8,128)(2,1)} %bitcast.17), calls=%async_computation.2 | async-start | bytes 262144 | tf_op jit(solution)/shard_map/all_to_all | solution.py:563
  79.2 3.4 %collective-permute-start.2 = (bf16[256,512]{1,0:T(8,128)(2,1)S(1)}, bf16[256,512]{1,0:T(8,128)(2,1)S(1)}, u32[]{:S(2)}, u32[]{:S(2)}) collective-permute-start(bf16[256,512]{1,0:T(8,128)(2,1)S(1)} %get-tuple-element.58), channel_id=1, source_target_pairs={{0,8},{8,0},{1,9},{9,1},{2,10},{10,2},{3,11},{11,3},{4,12},{12,4},... | collective-permute-start | bytes 786440 | tf_op jit(solution)/shard_map/ppermute | solution.py:599
  82.8 16.3 %copy-start.1 = (f32[2,2]{1,0:T(2,128)S(1)}, f32[2,2]{1,0:T(2,128)}, u32[]{:S(2)}) copy-start(f32[2,2]{1,0:T(2,128)} %refs_1_.1) | copy-start | bytes 52

commit v6 on v5

--- a/solution.py
+++ b/solution.py
@@ -220,7 +220,7 @@
     dbias = jnp.sum(dz, axis=1, keepdims=True)
     dskip = jnp.sum(extra[16:24], axis=1, keepdims=True)
     dzs = jnp.concatenate([dz, jnp.zeros((120, n), F32)], 0).astype(BF16)
-    dbcs = halves(dbc) if FINE else (dbc.astype(BF16),)
+    dbcs = halves(dbc)
     front, inside = weights[:, :width], weights[:, 128:256]
     dinput = low(jnp.concatenate([front, front], 1), jnp.concatenate(dpre, 0), NN)
     dinput = dinput + low(
@@ -228,10 +228,12 @@
         jnp.concatenate([dzs, *dbcs], 0),
         NN,
     )
-    dfront = low(u, dpre[0], NT) + low(u, dpre[1], NT)
+    dfront = low(u, jnp.concatenate(dpre, 0), NT)
+    dfront = dfront[:, :width] + dfront[:, width:]
     rest = low(u, jnp.concatenate([dbcs[0], dzs], 0), NT)
-    dinside = rest[:, :width] + (low(u, dbcs[1], NT) if FINE else 0.0)
-    dout = low(q, lower[0], NT) + low(q, lower[1], NT)
+    dinside = rest[:, :width] + low(u, dbcs[1], NT)
+    dout = low(q, jnp.concatenate(lower, 0), NT)
+    dout = dout[:, :width] + dout[:, width:]
     lane = lax.broadcasted_iota(jnp.int32, (1, width), 1)
     numbers = jnp.zeros((1, width), F32)
     for k in range(4):
@@ -252,7 +254,6 @@
 
 PLAIN = False
 SWAP = [(0, 1), (1, 0)]
-FINE = True
 
 
 def call(fn, outs, args, flops, scratch=(), scalars=0, grant=24 << 20):
@@ -275,8 +276,8 @@
 
 def gathered(order, parts, own, other):
     if PLAIN:
-        n = parts.shape[1]
-        blocks = parts.reshape(8, 2, 2, 32, n)
+        n = parts[0].shape[1]
+        blocks = jnp.concatenate(parts, 0).reshape(8, 2, 2, 32, n)
         mine = order[8]
         u, q = (
             jnp.concatenate([blocks[:, k, mine], blocks[:, k, 1 - mine]], 0).reshape(512, n)
@@ -288,9 +289,9 @@
     up, down, rows = [], [], []
     for at, weights in ((mine, own), (32 - mine, other)):
         for k in range(8):
-            base = 128 * k
-            up.append(parts[pl.ds(pl.multiple_of(base + at, 32), 32), :])
-            down.append(parts[pl.ds(pl.multiple_of(base + 64 + at, 32), 32), :])
+            part, base = parts[k // 2], 128 * (k % 2)
+            up.append(part[pl.ds(pl.multiple_of(base + at, 32), 32), :])
+            down.append(part[pl.ds(pl.multiple_of(base + 64 + at, 32), 32), :])
             rows.append(weights[pl.ds(pl.multiple_of(order[k] * 32, 32), 32), :])
     return jnp.concatenate(up, 0), jnp.concatenate(down, 0), jnp.concatenate(rows, 0)
 
@@ -301,17 +302,17 @@
         return (jnp.stack(sends, 1).reshape(512, 128).astype(BF16), *rest)
 
     def fn(ins, outs, lines):
-        sends, *rest = stage_project(*gathered(*ins[:4]), ins[4][...])
+        sends, *rest = stage_project(*gathered(ins[0], ins[1:5], *ins[5:7]), ins[7][...])
         for j, part in enumerate(sends):
             lines[pl.ds(j, STATE, stride=8), :] = part
         outs[0][...] = lines[...].astype(BF16)
         for ref, value in zip(outs[1:], rest):
             ref[...] = value
 
-    n = parts.shape[1]
+    n = parts[0].shape[1]
     outs = [((512, 128), BF16), ((128, n), F32), ((128, n), F32), ((128, n), F32), ((48, n), F32)]
     lines = pltpu.VMEM((512, 128), F32)
-    return call(fn, outs, (order, parts, own, other, params), 300_000_000, (lines,), 1)
+    return call(fn, outs, (order, *parts, own, other, params), 300_000_000, (lines,), 1)
 
 
 def within(pre, bc, cot, vec, params):
@@ -351,7 +352,7 @@
             for j in range(4)
         ]
         dinput, grads = stage_finish(
-            *gathered(*ins[:4]), *(r[...] for r in ins[4:-1]), carried
+            *gathered(order, ins[1:5], *ins[5:7]), *(r[...] for r in ins[7:-1]), carried
         )
         dinput = dinput.astype(BF16)
         give = grads[256:].astype(BF16)
@@ -368,7 +369,7 @@
 
     outs = [((8, 72, n), BF16), ((256, 512), F32), ((256, 512), BF16)]
     lines = pltpu.VMEM((512, 128), F32)
-    args = (order, parts, own, other, *more, back)
+    args = (order, *parts, own, other, *more, back)
     return call(fn, outs, args, 600_000_000, (lines,), 1)
 
 
@@ -580,15 +581,19 @@
         dt_bias,
         skip_gain.reshape(1, -1),
     )
-    around = lax.axis_index("chan_1")
-    order = jnp.stack(
-        [2 * k + (around ^ e) for k in range(4) for e in range(2)] + [lax.axis_index(CORE)]
-    ).astype(jnp.int32)
     other = lax.ppermute(own, "chan_1", SWAP)
     pair = jnp.concatenate([own, other], 0)
-    parts = lax.all_gather(pair, "chan_0", axis=0, tiled=True)
+    parts = [pair] + [
+        lax.ppermute(pair, "chan_0", [(k, (k + d) % 4) for k in range(4)])
+        for d in (1, 2, 3)
+    ]
     here = exchange(rows, ZY).reshape(-1, 512)
     there = lax.ppermute(here, CORE, SWAP)
+    across, around = lax.axis_index("chan_0"), lax.axis_index("chan_1")
+    order = jnp.stack(
+        [(across - d) % 4 * 2 + (around ^ e) for d in range(4) for e in range(2)]
+        + [lax.axis_index(CORE)]
+    ).astype(jnp.int32)
     sums, pre, bc, cot, vec = project(order, parts, here, there, params)
     sums = exchange(sums.reshape(64, 8, 128), SEQ).reshape(512, 128)
     mixed, dgated, dbc, extra = within(pre, bc, cot, vec, params)

time: 121 us -> 122 us (level)
  blocking collectives: 66.3 us -> 50.6 us
  starting transfers between devices: 29 us -> 39.2 us
  waiting for transfers between devices: 14.7 us -> 21 us
    all_gather x1 -> x0, blocking collectives: 13.4 us -> none  [body(): parts = lax.all_gather(pair, 'chan_0', axis=0, tiled=True)]
    ppermute x0 -> x3, starting transfers between devices: none -> 10.2 us  [body(): lax.ppermute(pair, 'chan_0', [(k, (k + d) % 4) for k in range(4)])]
    ppermute x0 -> x3, waiting for transfers between devices: none -> 6.19 us  [body(): lax.ppermute(pair, 'chan_0', [(k, (k + d) % 4) for k in range(4)])]
    all_to_all x3, blocking collectives: 53 us -> 50.6 us  [exchange(): return lax.all_to_all(array, axis, 0, 0, tiled=True)]
  transfers between devices with their start and end apart: 5 -> 8, of which waited for: 3 -> 5; matrix products, arithmetic and copies ran while one was open for 0% -> 0% of each run, Pallas kernels for 1% -> 1%
where the time goes in v6:
time: 122 us; the launch traced here: 121 us
  blocking collectives  50.6 us (41%)
  starting transfers between devices  39.2 us (32%)
  waiting for transfers between devices  21 us (17%)
  Pallas kernels  9.3 us (8%)
    all_to_all x3, blocking collectives, exchange(): return lax.all_to_all(array, axis, 0, 0, tiled=True)  50.6 us
    all_to_all x2, starting transfers between devices, exchange(): return lax.all_to_all(array, axis, 0, 0, tiled=True)  20.1 us
    all_to_all x2, waiting for transfers between devices, exchange(): return lax.all_to_all(array, axis, 0, 0, tiled=True)  13.4 us
    ppermute x3, starting transfers between devices, body(): lax.ppermute(pair, 'chan_0', [(k, (k + d) % 4) for k in range(4)])  10.2 us
    pallas_call x8, Pallas kernels, call(): pl.pallas_call(kernel, out_shape=[jax.ShapeDtypeStruct(s, d) for s, d in...  9.3 us
    ppermute x3, waiting for transfers between devices, body(): lax.ppermute(pair, 'chan_0', [(k, (k + d) % 4) for k in range(4)])  6.19 us
    ppermute x1, starting transfers between devices, body(): other = lax.ppermute(own, 'chan_1', SWAP)  5.04 us
  transfers between devices with their start and end apart: 8, of which 5 were waited for; matrix products, arithmetic and copies ran while one was open for 0% of the time, Pallas kernels for 1%

profile of v6, /device:TPU:16, one launch (start us, length us, event | category | flops | bytes accessed | tf_op | source)
XLA Modules:
  0.0 121.1 jit_solution(9657899675070478165)
XLA Ops:
  0.6 1.7 %shard_map.152 = (bf16[128,256]{1,0:T(8,128)(2,1)}, bf16[32,8,512]{2,1,0:T(8,128)(2,1)}, f32[8,128]{1,0:T(8,128)}) custom-call(bf16[64,256]{1,0:T(8,128)(2,1)} %bitcast.31, bf16[64,256]{1,0:T(8,128)(2,1)} %bitcast.32, bf16[8,128]{1,0:T(8,128)(2,1)} %refs_2_.1, bf16[8,128]{1,0:T(8,128)(2,1)} %refs_3_.1, bf16[8,128]{1,0:T(8,128)(2,1)} %bitcast.33, ...), custom_call_target="tpu_custom_call" | custom-call | flops 1000000 | bytes 71752 | tf_op jit(solution)/shard_map/pallas_call | solution.py:266
  2.3 0.0 copy-start.2
  2.3 14.0 %all-to-all-start = ((bf16[32,8,512]{2,1,0:T(8,128)(2,1)}), bf16[32,8,512]{2,1,0:T(8,128)(2,1)S(1)}, u32[]{:S(2)}, u32[]{:S(2)}) async-start(bf16[32,8,512]{2,1,0:T(8,128)(2,1)} %get-tuple-element.45), calls=%async_computation | async-start | bytes 524288 | tf_op jit(solution)/shard_map/all_to_all | solution.py:564
  16.3 0.0 copy-done.2
  16.3 5.0 %collective-permute-start = (bf16[128,256]{1,0:T(8,128)(2,1)S(1)}, bf16[128,256]{1,0:T(8,128)(2,1)S(1)}, u32[]{:S(2)}, u32[]{:S(2)}) collective-permute-start(bf16[128,256]{1,0:T(8,128)(2,1)S(1)} %copy-done.2), channel_id=1, source_target_pairs={{0,1},{1,0},{2,3},{3,2},{4,5},{5,4},{6,7},{7,6},{8,9},{9,8},{10,11... | collective-permute-start | bytes 196616 | tf_op jit(solution)/shard_map/ppermute | solution.py:584
  21.3 5.8 %all-to-all-done = bf16[32,8,512]{2,1,0:T(8,128)(2,1)S(1)} async-done(((bf16[32,8,512]{2,1,0:T(8,128)(2,1)}), bf16[32,8,512]{2,1,0:T(8,128)(2,1)S(1)}, u32[]{:S(2)}, u32[]{:S(2)}) %all-to-all-start) | async-done | bytes 262176 | tf_op jit(solution)/shard_map/all_to_all | solution.py:564
  27.1 1.9 %collective-permute-start.4 = (bf16[256,512]{1,0:T(8,128)(2,1)S(1)}, bf16[256,512]{1,0:T(8,128)(2,1)S(1)}, u32[]{:S(2)}, u32[]{:S(2)}) collective-permute-start(bf16[256,512]{1,0:T(8,128)(2,1)S(1)} %bitcast.24), channel_id=1, source_target_pairs={{0,8},{8,0},{1,9},{9,1},{2,10},{10,2},{3,11},{11,3},{4,12},{12,4},... | collective-permute-start | bytes 786440 | tf_op jit(solution)/shard_map/ppermute | solution.py:591
  29.1 0.0 collective-permute-done
  29.1 4.7 %collective-permute-start.3 = (bf16[256,256]{1,0:T(8,128)(2,1)S(1)}, bf16[256,256]{1,0:T(8,128)(2,1)S(1)}, u32[]{:S(2)}, u32[]{:S(2)}) collective-permute-start(bf16[256,256]{1,0:T(8,128)(2,1)S(1)} %constant_dynamic-update-slice_fusion.refs_1_), channel_id=1, source_target_pairs={{0,6},{2,0},{4,2},{6,4},{1,7},{3,1},{5,3},{7,5},{8,14},{10,8},{12,... | collective-permute-start | bytes 393224 | tf_op jit(solution)/shard_map/ppermute | solution.py:587
  33.8 2.7 %collective-permute-start.2 = (bf16[256,256]{1,0:T(8,128)(2,1)S(1)}, bf16[256,256]{1,0:T(8,128)(2,1)S(1)}, u32[]{:S(2)}, u32[]{:S(2)}) collective-permute-start(bf16[256,256]{1,0:T(8,128)(2,1)S(1)} %constant_dynamic-update-slice_fusion.refs_1_), channel_id=1, source_target_pairs={{0,4},{2,6},{4,0},{6,2},{1,5},{3,7},{5,1},{7,3},{8,12},{10,14},{12... | collective-permute-start | bytes 393224 | tf_op jit(solution)/shard_map/ppermute | solution.py:587
  36.5 2.8 %collective-permute-start.1 = (bf16[256,256]{1,0:T(8,128)(2,1)S(1)}, bf16[256,256]{1,0:T(8,128)(2,1)S(1)}, u32[]{:S(2)}, u32[]{:S(2)}) collective-permute-start(bf16[256,256]{1,0:T(8,128)(2,1)S(1)} %constant_dynamic-update-slice_fusion.refs_1_), channel_id=1, source_target_pairs={{0,2},{2,4},{4,6},{6,0},{1,3},{3,5},{5,7},{7,1},{8,10},{10,12},{12... | collective-permute-start | bytes 393224 | tf_op jit(solution)/shard_map/ppermute | solution.py:587
  39.4 0.0 copy-start
  39.4 0.1 stack.39.refs_0_
  39.5 0.0 collective-permute-done.3.refs_4_
  39.5 4.1 %collective-permute-done.2.refs_3_ = bf16[256,256]{1,0:T(8,128)(2,1)S(1)} collective-permute-done((bf16[256,256]{1,0:T(8,128)(2,1)S(1)}, bf16[256,256]{1,0:T(8,128)(2,1)S(1)}, u32[]{:S(2)}, u32[]{:S(2)}) %collective-permute-start.2) | collective-permute-done | bytes 131104 | tf_op jit(solution)/shard_map/ppermute | solution.py:587
  43.5 2.1 %collective-permute-done.1.refs_2_ = bf16[256,256]{1,0:T(8,128)(2,1)S(1)} collective-permute-done((bf16[256,256]{1,0:T(8,128)(2,1)S(1)}, bf16[256,256]{1,0:T(8,128)(2,1)S(1)}, u32[]{:S(2)}, u32[]{:S(2)}) %collective-permute-start.1) | collective-permute-done | bytes 131104 | tf_op jit(solution)/shard_map/ppermute | solution.py:587
  45.6 0.0 collective-permute-done.4.refs_6_
  45.6 0.0 copy-done
  45.6 1.4 %shard_map.153 = (bf16[512,128]{1,0:T(8,128)(2,1)S(1)}, f32[128,256]{1,0:T(8,128)S(1)}, f32[128,256]{1,0:T(8,128)S(1)}, f32[128,256]{1,0:T(8,128)S(1)}, f32[48,256]{1,0:T(8,128)S(1)}) custom-call(s32[9]{0:T(128)S(1)} %stack.39.refs_0_, bf16[256,256]{1,0:T(8,128)(2,1)S(1)} %constant_dynamic-update-slice_fusion.refs_1_, ...), custom_call_target="tpu_custom_call" | custom-call | flops 300000000 | bytes 1052708 | tf_op jit(solution)/shard_map/pallas_call | solution.py:266
  47.1 16.4 %all_to_all.25 = bf16[64,8,128]{2,1,0:T(8,128)(2,1)S(1)} all-to-all(bf16[64,8,128]{2,1,0:T(8,128)(2,1)S(1)} %bitcast.30), channel_id=1, replica_groups=mesh['seq_0'=8,'seq_1'=4,'seq_2'=2,'chan_0'=4,'chan_1'=2] {'seq_0','seq_..., dimensions={0} | all-to-all | bytes 262144 | tf_op jit(solution)/shard_map/all_to_all | solution.py:564
  63.4 1.1 shard_map.155
  64.5 6.1 %all-to-all-start.2 = ((bf16[64,8,128]{2,1,0:T(8,128)(2,1)}), bf16[64,8,128]{2,1,0:T(8,128)(2,1)S(1)}, u32[]{:S(2)}, u32[]{:S(2)}) async-start(bf16[64,8,128]{2,1,0:T(8,128)(2,1)} %bitcast.17), calls=%async_computation.2 | async-start | bytes 262144 | tf_op jit(solution)/shard_map/all_to_all | solution.py:564
  70.6 1.7 %shard_map.154 = (f32[256,256]{1,0:T(8,128)S(1)}, f32[256,256]{1,0:T(8,128)S(1)}, f32[128,256]{1,0:T(8,128)S(1)}, f32[24,256]{1,0:T(8,128)S(1)}) custom-call(f32[128,256]{1,0:T(8,128)S(1)} %get-tuple-element.47.refs_0_.refs_8_, f32[128,256]{1,0:T(8,128)S(1)} %get-tuple-element.48.refs_1_.refs_9_, f32[128,256]{1,0:T(8,128)S(1)} %get-tuple-element.49.refs_2_.refs_10_, ...), custom_call_target="tpu_custom_call" | custom-call | flops 300000000 | bytes 446464 | tf_op jit(solution)/shard_map/pallas_call | solution.py:266
  72.3 7.6 %all-to-all-done.2 = bf16[64,8,128]{2,1,0:T(8,128)(2,1)S(1)} async-done(((bf16[64,8,128]{2,1,0:T(8,128)(2,1)}), bf16[64,8,128]{2,1,0:T(8,128)(2,1)S(1)}, u32[]{:S(2)}, u32[]{:S(2)}) %all-to-all-start.2) | async-done | bytes 131104 | tf_op jit(solution)/shard_map/all_to_all | solution.py:564
  79.8 1.9 %shard_map.156 = (bf16[8,72,256]{2,1,0:T(8,128)(2,1)S(1)}, f32[256,512]{1,0:T(8,128)S(1)}, bf16[256,512]{1,0:T(8,128)(2,1)S(1)}) custom-call(s32[9]{0:T(128)S(1)} %stack.39.refs_0_, bf16[256,256]{1,0:T(8,128)(2,1)S(1)} %constant_dynamic-update-slice_fusion.refs_1_, bf16[256,256]{1,0:T(8,128)(2,1)S(1)} %collective-permute-done.1.refs_2_, ...), custom_call_target="tpu_custom_call" | custom-call | flops 600000000 | bytes 2306084 | tf_op jit(solution)/shard_map/pallas_call | solution.py:266
  81.7 2.0 %collective-permute-start.5 = (bf16[256,512]{1,0:T(8,128)(2,1)S(1)}, bf16[256,512]{1,0:T(8,128)(2,1)S(1)}, u32[]{:S(2)}, u32[]{:S(2)}) collective-permute-start(bf16[256,512]{1,0:T(8,128)(2,1)S(1)} %get-tuple-element.58), channel_id=1, source_target_pairs={{0,8},{8,0},{1,9},{9,1},{2,10},{10,2},{3,11},{11,3},{4,12},{12,4},... | collective-permute-start | bytes 786440 | tf_op jit(solution)/shard_map/ppermute | solution.py:604
  83.8 1.4 %collective-permute-done.5.refs_1_ = bf16[256,512]{1,0:T(8,128)(2,1)S(1)} collective-permute-done((bf16[256,512]{1,0:T(8,128)(2,1)S(1)}, bf16[256,512]{1,0:T(8,128)(2,1)S(1)}, u32[]{:S(2)}, u32[]{:S(2)}) %collective-permute-start.5) | collective-permute-done | bytes 262176 | tf_op jit(solution)/shard_map/ppermute | solution.py:604
  85.2 0.2 shard_map.157
  85.3 0.0 copy-start.1
  85.4 16.3 %all_to_all.26.refs_0_ = bf16[32,8,512]{2,1,0:T(8,128)(2,1)S(1)} all-to-all(bf16[32,8,512]{2,1,0:T(8,128)(2,1)S(1)} %bitcast.27), channel_id=1, replica_groups=mesh['seq_0'=8,'seq_1'=4,'seq_2'=2,'chan_0'=4,'chan_1'=2] {'seq_0','seq_1'}, dimensions={0} | all-to-all | bytes 524288 | tf_op jit(solution)/shard_map/all_to_all | solution.py:564
  101.6 0.0 copy-done.1
  101.6 0.8 shard_map.158
  102.4 18.0 %all_to_all.27.refs_0_ = bf16[8,72,256]{2,1,0:T(8,128)(2,1)S(1)} all-to-all(bf16[8,72,256]{2,1,0:T(8,128)(2,1)S(1)} %constant_dynamic-update-slice_fusion.2), channel_id=1, replica_groups=mesh['seq_0'=8,'seq_1'=4,'seq_2'=2,'chan_0'=4,'chan_1'=2] {'chan_0','cha..., dimensions={0} | all-to-all | bytes 589824 | tf_op jit(solution)/shard_map/all_to_all | solution.py:564
  120.4 0.7 shard_map.159
  (3 shorter events, 0.0 us)
Async XLA Ops:
  2.3 14.0 %copy-start.2 = (bf16[128,256]{1,0:T(8,128)(2,1)S(1)}, bf16[128,256]{1,0:T(8,128)(2,1)}, u32[]{:S(2)}) copy-start(bf16[128,256]{1,0:T(8,128)(2,1)} %get-tuple-element.44) | copy-start | bytes 196612
  2.3 24.8 %all-to-all-start = ((bf16[32,8,512]{2,1,0:T(8,128)(2,1)}), bf16[32,8,512]{2,1,0:T(8,128)(2,1)S(1)}, u32[]{:S(2)}, u32[]{:S(2)}) async-start(bf16[32,8,512]{2,1,0:T(8,128)(2,1)} %get-tuple-element.45), calls=%async_computation | async-start | bytes 524288 | tf_op jit(solution)/shard_map/all_to_all | solution.py:564
  16.3 12.8 %collective-permute-start = (bf16[128,256]{1,0:T(8,128)(2,1)S(1)}, bf16[128,256]{1,0:T(8,128)(2,1)S(1)}, u32[]{:S(2)}, u32[]{:S(2)}) collective-permute-start(bf16[128,256]{1,0:T(8,128)(2,1)S(1)} %copy-done.2), channel_id=1, source_target_pairs={{0,1},{1,0},{2,3},{3,2},{4,5},{5,4},{6,7},{7,6},{8,9},{9,8},{10,11... | collective-permute-start | bytes 196616 | tf_op jit(solution)/shard_map/ppermute | solution.py:584
  27.1 18.5 %collective-permute-start.4 = (bf16[256,512]{1,0:T(8,128)(2,1)S(1)}, bf16[256,512]{1,0:T(8,128)(2,1)S(1)}, u32[]{:S(2)}, u32[]{:S(2)}) collective-permute-start(bf16[256,512]{1,0:T(8,128)(2,1)S(1)} %bitcast.24), channel_id=1, source_target_pairs={{0,8},{8,0},{1,9},{9,1},{2,10},{10,2},{3,11},{11,3},{4,12},{12,4},... | collective-permute-start | bytes 786440 | tf_op jit(solution)/shard_map/ppermute | solution.py:591
  29.1 10.4 %collective-permute-start.3 = (bf16[256,256]{1,0:T(8,128)(2,1)S(1)}, bf16[256,256]{1,0:T(8,128)(2,1)S(1)}, u32[]{:S(2)}, u32[]{:S(2)}) collective-permute-start(bf16[256,256]{1,0:T(8,128)(2,1)S(1)} %constant_dynamic-update-slice_fusion.refs_1_), channel_id=1, source_target_pairs={{0,6},{2,0},{4,2},{6,4},{1,7},{3,1},{5,3},{7,5},{8,14},{10,8},{12,... | collective-permute-start | bytes 393224 | tf_op jit(solution)/shard_map/ppermute | solution.py:587
  33.8 9.8 %collective-permute-start.2 = (bf16[256,256]{1,0:T(8,128)(2,1)S(1)}, bf16[256,256]{1,0:T(8,128)(2,1)S(1)}, u32[]{:S(2)}, u32[]{:S(2)}) collective-permute-start(bf16[256,256]{1,0:T(8,128)(2,1)S(1)} %constant_dynamic-update-slice_fusion.refs_1_), channel_id=1, source_target_pairs={{0,4},{2,6},{4,0},{6,2},{1,5},{3,7},{5,1},{7,3},{8,12},{10,14},{12... | collective-permute-start | bytes 393224 | tf_op jit(solution)/shard_map/ppermute | solution.py:587
  36.5 9.2 %collective-permute-start.1 = (bf16[256,256]{1,0:T(8,128)(2,1)S(1)}, bf16[256,256]{1,0:T(8,128)(2,1)S(1)}, u32[]{:S(2)}, u32[]{:S(2)}) collective-permute-start(bf16[256,256]{1,0:T(8,128)(2,1)S(1)} %constant_dynamic-update-slice_fusion.refs_1_), channel_id=1, source_target_pairs={{0,2},{2,4},{4,6},{6,0},{1,3},{3,5},{5,7},{7,1},{8,10},{10,12},{12... | collective-permute-start | bytes 393224 | tf_op jit(solution)/shard_map/ppermute | solution.py:587
  39.4 6.3 %copy-start = (f32[8,128]{1,0:T(8,128)S(1)}, f32[8,128]{1,0:T(8,128)}, u32[]{:S(2)}) copy-start(f32[8,128]{1,0:T(8,128)} %get-tuple-element.46.refs_7_.refs_4_) | copy-start | bytes 12292
  64.5 15.4 %all-to-all-start.2 = ((bf16[64,8,128]{2,1,0:T(8,128)(2,1)}), bf16[64,8,128]{2,1,0:T(8,128)(2,1)S(1)}, u32[]{:S(2)}, u32[]{:S(2)}) async-start(bf16[64,8,128]{2,1,0:T(8,128)(2,1)} %bitcast.17), calls=%async_computation.2 | async-start | bytes 262144 | tf_op jit(solution)/shard_map/all_to_all | solution.py:564
  81.7 3.4 %collective-permute-start.5 = (bf16[256,512]{1,0:T(8,128)(2,1)S(1)}, bf16[256,512]{1,0:T(8,128)(2,1)S(1)}, u32[]{:S(2)}, u32[]{:S(2)}) collective-permute-start(bf16[256,512]{1,0:T(8,128)(2,1)S(1)} %get-tuple-element.58), channel_id=1, source_target_pairs={{0,8},{8,0},{1,9},{9,1},{2,10},{10,2},{3,11},{11,3},{4,12},{12,4},... | collective-permute-start | bytes 786440 | tf_op jit(solution)/shard_map/ppermute | solution.py:604
  85.3 16.3 %copy-start.1 = (f32[2,2]{1,0:T(2,128)S(1)}, f32[2,2]{1,0:T(2,128)}, u32[]{:S(2)}) copy-start(f32[2,2]{1,0:T(2,128)} %refs_1_.1) | copy-start | bytes 52

commit v7 on v6

--- a/solution.py
+++ b/solution.py
@@ -165,7 +165,7 @@
     return mixed, dgated, dbc, extra
 
 
-def stage_finish(u, q, weights, params, pre, bc, cot, vec, mixed, dgated, dbc, extra, carried):
+def stage_finish(params, pre, bc, cot, vec, mixed, dgated, dbc, extra, carried):
     width = 128
     n = pre.shape[1]
     sig = sigmoid(pre)
@@ -220,20 +220,6 @@
     dbias = jnp.sum(dz, axis=1, keepdims=True)
     dskip = jnp.sum(extra[16:24], axis=1, keepdims=True)
     dzs = jnp.concatenate([dz, jnp.zeros((120, n), F32)], 0).astype(BF16)
-    dbcs = halves(dbc)
-    front, inside = weights[:, :width], weights[:, 128:256]
-    dinput = low(jnp.concatenate([front, front], 1), jnp.concatenate(dpre, 0), NN)
-    dinput = dinput + low(
-        jnp.concatenate([weights[:, 384:512]] + [inside] * len(dbcs), 1),
-        jnp.concatenate([dzs, *dbcs], 0),
-        NN,
-    )
-    dfront = low(u, jnp.concatenate(dpre, 0), NT)
-    dfront = dfront[:, :width] + dfront[:, width:]
-    rest = low(u, jnp.concatenate([dbcs[0], dzs], 0), NT)
-    dinside = rest[:, :width] + low(u, dbcs[1], NT)
-    dout = low(q, jnp.concatenate(lower, 0), NT)
-    dout = dout[:, :width] + dout[:, width:]
     lane = lax.broadcasted_iota(jnp.int32, (1, width), 1)
     numbers = jnp.zeros((1, width), F32)
     for k in range(4):
@@ -243,9 +229,33 @@
         numbers = jnp.where(lane == 16 + k, dskip[k : k + 1], numbers)
     rough = numbers.astype(BF16).astype(F32)
     fine = rolled(jnp.broadcast_to(numbers - rough, (8, width)), 32)[:1]
-    last = rest[:, width:] + jnp.broadcast_to(rough + fine, (u.shape[0], width))
-    grads = jnp.concatenate([dfront, dinside, dout, last], 1)
-    return dinput, grads
+    numbers = jnp.broadcast_to(rough + fine, (8, width))
+    front = jnp.concatenate([*dpre, *halves(dbc), dzs], 0)
+    return front, jnp.concatenate(lower, 0), numbers
+
+
+def stage_outer(u, q, front, lower, numbers):
+    width = 128
+    dfront = low(u, front[: 2 * width], NT)
+    dinside = low(u, front[2 * width : 4 * width], NT)
+    dstep = low(u, front[4 * width :], NT)
+    dout = low(q, lower, NT)
+    return jnp.concatenate(
+        [
+            dfront[:, :width] + dfront[:, width:],
+            dinside[:, :width] + dinside[:, width:],
+            dout[:, :width] + dout[:, width:],
+            dstep + jnp.broadcast_to(numbers[:1], (u.shape[0], width)),
+        ],
+        1,
+    )
+
+
+def stage_input(weights, front):
+    outer, inside = weights[:, :128], weights[:, 128:256]
+    return low(jnp.concatenate([outer, outer], 1), front[:256], NN) + low(
+        jnp.concatenate([inside, inside, weights[:, 384:]], 1), front[256:], NN
+    )
 
 
 def rolled(x, by):
@@ -274,26 +284,32 @@
     )(*args)
 
 
-def gathered(order, parts, own, other):
+def features(order, parts, partner):
     if PLAIN:
         n = parts[0].shape[1]
         blocks = jnp.concatenate(parts, 0).reshape(8, 2, 2, 32, n)
-        mine = order[8]
-        u, q = (
-            jnp.concatenate([blocks[:, k, mine], blocks[:, k, 1 - mine]], 0).reshape(512, n)
-            for k in (0, 1)
-        )
-        halves_ = [w.reshape(8, 32, -1)[order[:8]] for w in (own, other)]
-        return u, q, jnp.concatenate(halves_, 0).reshape(512, -1)
-    mine = order[8] * 32
-    up, down, rows = [], [], []
-    for at, weights in ((mine, own), (32 - mine, other)):
-        for k in range(8):
-            part, base = parts[k // 2], 128 * (k % 2)
-            up.append(part[pl.ds(pl.multiple_of(base + at, 32), 32), :])
-            down.append(part[pl.ds(pl.multiple_of(base + 64 + at, 32), 32), :])
-            rows.append(weights[pl.ds(pl.multiple_of(order[k] * 32, 32), 32), :])
-    return jnp.concatenate(up, 0), jnp.concatenate(down, 0), jnp.concatenate(rows, 0)
+        side = 1 - order[8] if partner else order[8]
+        return tuple(blocks[:, k, side].reshape(256, n) for k in (0, 1))
+    at = (1 - order[8]) * 32 if partner else order[8] * 32
+    up, down = [], []
+    for k in range(8):
+        part, base = parts[k // 2], 128 * (k % 2)
+        up.append(part[pl.ds(pl.multiple_of(base + at, 32), 32), :])
+        down.append(part[pl.ds(pl.multiple_of(base + 64 + at, 32), 32), :])
+    return jnp.concatenate(up, 0), jnp.concatenate(down, 0)
+
+
+def matching(order, weights):
+    if PLAIN:
+        return weights.reshape(8, 32, -1)[order[:8]].reshape(256, -1)
+    rows = [weights[pl.ds(pl.multiple_of(order[k] * 32, 32), 32), :] for k in range(8)]
+    return jnp.concatenate(rows, 0)
+
+
+def gathered(order, parts, own, other):
+    first, second = features(order, parts, False), features(order, parts, True)
+    u, q = (jnp.concatenate(pair, 0) for pair in zip(first, second))
+    return u, q, jnp.concatenate([matching(order, own), matching(order, other)], 0)
 
 
 def project(order, parts, own, other, params):
@@ -328,21 +344,16 @@
     return call(fn, outs, (pre, bc, cot, vec, params), 300_000_000)
 
 
-def finish(order, parts, own, other, params, pre, bc, cot, vec, mixed, dgated, dbc, extra, back):
+def finish(order, parts, params, pre, bc, cot, vec, mixed, dgated, dbc, extra, back):
     more = (params, pre, bc, cot, vec, mixed, dgated, dbc, extra)
     n = pre.shape[1]
     if PLAIN:
         rows = back.astype(F32).reshape(64, 8, 128)
         carried = [rows[:, j] + rows[:, 4 + j] for j in range(4)]
-        dinput, grads = stage_finish(*gathered(order, parts, own, other), *more, carried)
-        at, mine = order[:8], order[8]
-        dinput = dinput.astype(BF16).reshape(2, 8, 32, n)
-        dinput = jnp.where(mine == 0, dinput, dinput[::-1]).transpose(1, 0, 2, 3)
-        wide = jnp.zeros((8, 72, n), BF16).at[at, :64].set(dinput.reshape(8, 64, n))
-        grads = grads.reshape(2, 8, 32, 512)
-        keep = jnp.zeros((8, 32, 512), F32).at[at].set(grads[0]).reshape(256, 512)
-        give = jnp.zeros((8, 32, 512), F32).at[at].set(grads[1]).reshape(256, 512)
-        return wide, keep, give.astype(BF16)
+        results = stage_finish(*more, carried)
+        grads = stage_outer(*features(order, parts, True), *results).reshape(8, 32, 512)
+        give = jnp.zeros((8, 32, 512), F32).at[order[:8]].set(grads).reshape(256, 512)
+        return give.astype(BF16), *results
 
     def fn(ins, outs, lines):
         order = ins[0]
@@ -351,26 +362,49 @@
             lines[pl.ds(j, STATE, stride=8), :] + lines[pl.ds(4 + j, STATE, stride=8), :]
             for j in range(4)
         ]
-        dinput, grads = stage_finish(
-            *gathered(order, ins[1:5], *ins[5:7]), *(r[...] for r in ins[7:-1]), carried
-        )
-        dinput = dinput.astype(BF16)
-        give = grads[256:].astype(BF16)
+        results = stage_finish(*(r[...] for r in ins[5:-1]), carried)
+        grads = stage_outer(*features(order, ins[1:5], True), *results).astype(BF16)
+        for k in range(8):
+            rows = pl.ds(pl.multiple_of(order[k] * 32, 32), 32)
+            outs[0][rows, :] = grads[32 * k : 32 * k + 32]
+        for ref, value in zip(outs[1:], results):
+            ref[...] = value
+
+    outs = [((256, 512), BF16), ((640, n), BF16), ((256, n), BF16), ((8, 128), F32)]
+    lines = pltpu.VMEM((512, 128), F32)
+    return call(fn, outs, (order, *parts, *more, back), 400_000_000, (lines,), 1)
+
+
+def finish_own(order, parts, own, other, front, lower, numbers):
+    n = front.shape[1]
+    if PLAIN:
+        at, mine = order[:8], order[8]
+        weights = jnp.concatenate([matching(order, own), matching(order, other)], 0)
+        dinput = stage_input(weights, front).astype(BF16).reshape(2, 8, 32, n)
+        dinput = jnp.where(mine == 0, dinput, dinput[::-1]).transpose(1, 0, 2, 3)
+        wide = jnp.zeros((8, 72, n), BF16).at[at, :64].set(dinput.reshape(8, 64, n))
+        grads = stage_outer(*features(order, parts, False), front, lower, numbers)
+        keep = jnp.zeros((8, 32, 512), F32).at[at].set(grads.reshape(8, 32, 512))
+        return wide, keep.reshape(256, 512)
+
+    def fn(ins, outs):
+        order = ins[0]
+        front, lower, numbers = (r[...] for r in ins[7:])
+        weights = jnp.concatenate([matching(order, ins[5]), matching(order, ins[6])], 0)
+        dinput = stage_input(weights, front).astype(BF16)
+        grads = stage_outer(*features(order, ins[1:5], False), front, lower, numbers)
         mine = order[8] * 32
         for k in range(8):
             at = order[k]
             block = slice(32 * k, 32 * k + 32)
-            rows = pl.ds(pl.multiple_of(at * 32, 32), 32)
             outs[0][at, pl.ds(pl.multiple_of(mine, 32), 32), :] = dinput[block]
             outs[0][at, pl.ds(pl.multiple_of(32 - mine, 32), 32), :] = dinput[256:][block]
             outs[0][at, 64:, :] = jnp.zeros((8, n), BF16)
-            outs[1][rows, :] = grads[block]
-            outs[2][rows, :] = give[block]
-
-    outs = [((8, 72, n), BF16), ((256, 512), F32), ((256, 512), BF16)]
-    lines = pltpu.VMEM((512, 128), F32)
-    args = (order, *parts, own, other, *more, back)
-    return call(fn, outs, args, 600_000_000, (lines,), 1)
+            outs[1][pl.ds(pl.multiple_of(at * 32, 32), 32), :] = grads[block]
+
+    outs = [((8, 72, n), BF16), ((256, 512), F32)]
+    args = (order, *parts, own, other, front, lower, numbers)
+    return call(fn, outs, args, 400_000_000, (), 1)
 
 
 def join(keep, got):
@@ -598,10 +632,12 @@
     sums = exchange(sums.reshape(64, 8, 128), SEQ).reshape(512, 128)
     mixed, dgated, dbc, extra = within(pre, bc, cot, vec, params)
     back = exchange(carry(sums).reshape(64, 8, 128), SEQ).reshape(512, 128)
-    wide, keep, give = finish(
-        order, parts, here, there, params, pre, bc, cot, vec, mixed, dgated, dbc, extra, back
-    )
-    grads = join(keep, lax.ppermute(give, CORE, SWAP))
+    give, *results = finish(
+        order, parts, params, pre, bc, cot, vec, mixed, dgated, dbc, extra, back
+    )
+    got = lax.ppermute(give, CORE, SWAP)
+    wide, keep = finish_own(order, parts, here, there, *results)
+    grads = join(keep, got)
     grads = exchange(grads.reshape(32, 8, 512), ZY)
     wide, in_weight_grad, out_rows, dt_rows, rate_grad, bias_grad, skip_grad = add_rows(
         grads, wide, decay_rate, scale

time: 122 us -> 121 us (level)
    pallas_call x8 -> x9, Pallas kernels: 9.3 us -> 9.9 us  [call(): pl.pallas_call(kernel, out_shape=[jax.ShapeDtypeStruct(s, d) for s, d in...]
  transfers between devices with their start and end apart: 8 -> 8, of which waited for: 5 -> 5; matrix products, arithmetic and copies ran while one was open for 0% -> 0% of each run, Pallas kernels for 1% -> 2%
where the time goes in v7:
time: 121 us
  blocking collectives  50.6 us (42%)
  starting transfers between devices  39.2 us (32%)
  waiting for transfers between devices  19.9 us (16%)
  Pallas kernels  9.9 us (8%)
    all_to_all x3, blocking collectives, exchange(): return lax.all_to_all(array, axis, 0, 0, tiled=True)  50.6 us
    all_to_all x2, starting transfers between devices, exchange(): return lax.all_to_all(array, axis, 0, 0, tiled=True)  20.1 us
    all_to_all x2, waiting for transfers between devices, exchange(): return lax.all_to_all(array, axis, 0, 0, tiled=True)  13.4 us
    ppermute x3, starting transfers between devices, body(): lax.ppermute(pair, 'chan_0', [(k, (k + d) % 4) for k in range(4)])  10.2 us
    pallas_call x9, Pallas kernels, call(): pl.pallas_call(kernel, out_shape=[jax.ShapeDtypeStruct(s, d) for s, d in...  9.9 us
    ppermute x3, waiting for transfers between devices, body(): lax.ppermute(pair, 'chan_0', [(k, (k + d) % 4) for k in range(4)])  6.19 us
    ppermute x1, starting transfers between devices, body(): other = lax.ppermute(own, 'chan_1', SWAP)  5.04 us
  transfers between devices with their start and end apart: 8, of which 5 were waited for; matrix products, arithmetic and copies ran while one was open for 0% of the time, Pallas kernels for 2%

profile of v7, /device:TPU:16, one launch (start us, length us, event | category | flops | bytes accessed | tf_op | source)
XLA Modules:
  0.0 120.6 jit_solution(15196631588540532242)
XLA Ops:
  0.6 1.6 %shard_map.152 = (bf16[128,256]{1,0:T(8,128)(2,1)}, bf16[32,8,512]{2,1,0:T(8,128)(2,1)}, f32[8,128]{1,0:T(8,128)}) custom-call(bf16[64,256]{1,0:T(8,128)(2,1)} %bitcast.31, bf16[64,256]{1,0:T(8,128)(2,1)} %bitcast.32, bf16[8,128]{1,0:T(8,128)(2,1)} %refs_2_.1, bf16[8,128]{1,0:T(8,128)(2,1)} %refs_3_.1, bf16[8,128]{1,0:T(8,128)(2,1)} %bitcast.33, ...), custom_call_target="tpu_custom_call" | custom-call | flops 1000000 | bytes 71752 | tf_op jit(solution)/shard_map/pallas_call | solution.py:276
  2.3 0.0 copy-start.2
  2.3 14.0 %all-to-all-start = ((bf16[32,8,512]{2,1,0:T(8,128)(2,1)}), bf16[32,8,512]{2,1,0:T(8,128)(2,1)S(1)}, u32[]{:S(2)}, u32[]{:S(2)}) async-start(bf16[32,8,512]{2,1,0:T(8,128)(2,1)} %get-tuple-element.48), calls=%async_computation | async-start | bytes 524288 | tf_op jit(solution)/shard_map/all_to_all | solution.py:598
  16.3 0.0 copy-done.2
  16.3 5.0 %collective-permute-start = (bf16[128,256]{1,0:T(8,128)(2,1)S(1)}, bf16[128,256]{1,0:T(8,128)(2,1)S(1)}, u32[]{:S(2)}, u32[]{:S(2)}) collective-permute-start(bf16[128,256]{1,0:T(8,128)(2,1)S(1)} %copy-done.2), channel_id=1, source_target_pairs={{0,1},{1,0},{2,3},{3,2},{4,5},{5,4},{6,7},{7,6},{8,9},{9,8},{10,11... | collective-permute-start | bytes 196616 | tf_op jit(solution)/shard_map/ppermute | solution.py:618
  21.3 5.8 %all-to-all-done = bf16[32,8,512]{2,1,0:T(8,128)(2,1)S(1)} async-done(((bf16[32,8,512]{2,1,0:T(8,128)(2,1)}), bf16[32,8,512]{2,1,0:T(8,128)(2,1)S(1)}, u32[]{:S(2)}, u32[]{:S(2)}) %all-to-all-start) | async-done | bytes 262176 | tf_op jit(solution)/shard_map/all_to_all | solution.py:598
  27.1 1.9 %collective-permute-start.4 = (bf16[256,512]{1,0:T(8,128)(2,1)S(1)}, bf16[256,512]{1,0:T(8,128)(2,1)S(1)}, u32[]{:S(2)}, u32[]{:S(2)}) collective-permute-start(bf16[256,512]{1,0:T(8,128)(2,1)S(1)} %bitcast.24), channel_id=1, source_target_pairs={{0,8},{8,0},{1,9},{9,1},{2,10},{10,2},{3,11},{11,3},{4,12},{12,4},... | collective-permute-start | bytes 786440 | tf_op jit(solution)/shard_map/ppermute | solution.py:625
  29.1 0.0 collective-permute-done
  29.1 4.7 %collective-permute-start.3 = (bf16[256,256]{1,0:T(8,128)(2,1)S(1)}, bf16[256,256]{1,0:T(8,128)(2,1)S(1)}, u32[]{:S(2)}, u32[]{:S(2)}) collective-permute-start(bf16[256,256]{1,0:T(8,128)(2,1)S(1)} %constant_dynamic-update-slice_fusion.refs_1_), channel_id=1, source_target_pairs={{0,6},{2,0},{4,2},{6,4},{1,7},{3,1},{5,3},{7,5},{8,14},{10,8},{12,... | collective-permute-start | bytes 393224 | tf_op jit(solution)/shard_map/ppermute | solution.py:621
  33.8 2.7 %collective-permute-start.2 = (bf16[256,256]{1,0:T(8,128)(2,1)S(1)}, bf16[256,256]{1,0:T(8,128)(2,1)S(1)}, u32[]{:S(2)}, u32[]{:S(2)}) collective-permute-start(bf16[256,256]{1,0:T(8,128)(2,1)S(1)} %constant_dynamic-update-slice_fusion.refs_1_), channel_id=1, source_target_pairs={{0,4},{2,6},{4,0},{6,2},{1,5},{3,7},{5,1},{7,3},{8,12},{10,14},{12... | collective-permute-start | bytes 393224 | tf_op jit(solution)/shard_map/ppermute | solution.py:621
  36.5 2.8 %collective-permute-start.1 = (bf16[256,256]{1,0:T(8,128)(2,1)S(1)}, bf16[256,256]{1,0:T(8,128)(2,1)S(1)}, u32[]{:S(2)}, u32[]{:S(2)}) collective-permute-start(bf16[256,256]{1,0:T(8,128)(2,1)S(1)} %constant_dynamic-update-slice_fusion.refs_1_), channel_id=1, source_target_pairs={{0,2},{2,4},{4,6},{6,0},{1,3},{3,5},{5,7},{7,1},{8,10},{10,12},{12... | collective-permute-start | bytes 393224 | tf_op jit(solution)/shard_map/ppermute | solution.py:621
  39.3 0.0 copy-start
  39.3 0.1 stack.39.refs_0_
  39.4 0.0 collective-permute-done.3.refs_4_
  39.4 4.1 %collective-permute-done.2.refs_3_ = bf16[256,256]{1,0:T(8,128)(2,1)S(1)} collective-permute-done((bf16[256,256]{1,0:T(8,128)(2,1)S(1)}, bf16[256,256]{1,0:T(8,128)(2,1)S(1)}, u32[]{:S(2)}, u32[]{:S(2)}) %collective-permute-start.2) | collective-permute-done | bytes 131104 | tf_op jit(solution)/shard_map/ppermute | solution.py:621
  43.5 2.1 %collective-permute-done.1.refs_2_ = bf16[256,256]{1,0:T(8,128)(2,1)S(1)} collective-permute-done((bf16[256,256]{1,0:T(8,128)(2,1)S(1)}, bf16[256,256]{1,0:T(8,128)(2,1)S(1)}, u32[]{:S(2)}, u32[]{:S(2)}) %collective-permute-start.1) | collective-permute-done | bytes 131104 | tf_op jit(solution)/shard_map/ppermute | solution.py:621
  45.6 0.0 collective-permute-done.4.refs_6_
  45.6 0.0 copy-done
  45.6 1.4 %shard_map.153 = (bf16[512,128]{1,0:T(8,128)(2,1)S(1)}, f32[128,256]{1,0:T(8,128)S(1)}, f32[128,256]{1,0:T(8,128)S(1)}, f32[128,256]{1,0:T(8,128)S(1)}, f32[48,256]{1,0:T(8,128)S(1)}) custom-call(s32[9]{0:T(128)S(1)} %stack.39.refs_0_, bf16[256,256]{1,0:T(8,128)(2,1)S(1)} %constant_dynamic-update-slice_fusion.refs_1_, ...), custom_call_target="tpu_custom_call" | custom-call | flops 300000000 | bytes 1052708 | tf_op jit(solution)/shard_map/pallas_call | solution.py:276
  47.0 16.4 %all_to_all.25 = bf16[64,8,128]{2,1,0:T(8,128)(2,1)S(1)} all-to-all(bf16[64,8,128]{2,1,0:T(8,128)(2,1)S(1)} %bitcast.30), channel_id=1, replica_groups=mesh['seq_0'=8,'seq_1'=4,'seq_2'=2,'chan_0'=4,'chan_1'=2] {'seq_0','seq_..., dimensions={0} | all-to-all | bytes 262144 | tf_op jit(solution)/shard_map/all_to_all | solution.py:598
  63.4 1.0 shard_map.155
  64.4 6.1 %all-to-all-start.2 = ((bf16[64,8,128]{2,1,0:T(8,128)(2,1)}), bf16[64,8,128]{2,1,0:T(8,128)(2,1)S(1)}, u32[]{:S(2)}, u32[]{:S(2)}) async-start(bf16[64,8,128]{2,1,0:T(8,128)(2,1)} %bitcast.17), calls=%async_computation.2 | async-start | bytes 262144 | tf_op jit(solution)/shard_map/all_to_all | solution.py:598
  70.5 1.7 %shard_map.154 = (f32[256,256]{1,0:T(8,128)S(1)}, f32[256,256]{1,0:T(8,128)S(1)}, f32[128,256]{1,0:T(8,128)S(1)}, f32[24,256]{1,0:T(8,128)S(1)}) custom-call(f32[128,256]{1,0:T(8,128)S(1)} %get-tuple-element.50.refs_0_.refs_6_, f32[128,256]{1,0:T(8,128)S(1)} %get-tuple-element.51.refs_1_.refs_7_, f32[128,256]{1,0:T(8,128)S(1)} %get-tuple-element.52.refs_2_.refs_8_, ...), custom_call_target="tpu_custom_call" | custom-call | flops 300000000 | bytes 446464 | tf_op jit(solution)/shard_map/pallas_call | solution.py:276
  72.2 7.6 %all-to-all-done.2 = bf16[64,8,128]{2,1,0:T(8,128)(2,1)S(1)} async-done(((bf16[64,8,128]{2,1,0:T(8,128)(2,1)}), bf16[64,8,128]{2,1,0:T(8,128)(2,1)S(1)}, u32[]{:S(2)}, u32[]{:S(2)}) %all-to-all-start.2) | async-done | bytes 131104 | tf_op jit(solution)/shard_map/all_to_all | solution.py:598
  79.8 1.5 %shard_map.156 = (bf16[256,512]{1,0:T(8,128)(2,1)S(1)}, bf16[640,256]{1,0:T(8,128)(2,1)S(1)}, bf16[256,256]{1,0:T(8,128)(2,1)S(1)}, f32[8,128]{1,0:T(8,128)S(1)}) custom-call(s32[9]{0:T(128)S(1)} %stack.39.refs_0_, bf16[256,256]{1,0:T(8,128)(2,1)S(1)} %constant_dynamic-update-slice_fusion.refs_1_, bf16[256,256]{1,0:T(8,128)(2,1)S(1)} %collective-permute-done.1.refs_2_, ...), custom_call_target="tpu_custom_call" | custom-call | flops 400000000 | bytes 1781796 | tf_op jit(solution)/shard_map/pallas_call | solution.py:276
  81.3 2.0 %collective-permute-start.5 = (bf16[256,512]{1,0:T(8,128)(2,1)S(1)}, bf16[256,512]{1,0:T(8,128)(2,1)S(1)}, u32[]{:S(2)}, u32[]{:S(2)}) collective-permute-start(bf16[256,512]{1,0:T(8,128)(2,1)S(1)} %get-tuple-element.64), channel_id=1, source_target_pairs={{0,8},{8,0},{1,9},{9,1},{2,10},{10,2},{3,11},{11,3},{4,12},{12,4},... | collective-permute-start | bytes 786440 | tf_op jit(solution)/shard_map/ppermute | solution.py:638
  83.3 1.0 shard_map.157
  84.4 0.4 collective-permute-done.5.refs_1_
  84.7 0.2 shard_map.158
  84.9 0.0 copy-start.1
  84.9 16.3 %all_to_all.26.refs_0_ = bf16[32,8,512]{2,1,0:T(8,128)(2,1)S(1)} all-to-all(bf16[32,8,512]{2,1,0:T(8,128)(2,1)S(1)} %bitcast.27), channel_id=1, replica_groups=mesh['seq_0'=8,'seq_1'=4,'seq_2'=2,'chan_0'=4,'chan_1'=2] {'seq_0','seq_1'}, dimensions={0} | all-to-all | bytes 524288 | tf_op jit(solution)/shard_map/all_to_all | solution.py:598
  101.2 0.0 copy-done.1
  101.2 0.8 shard_map.159
  102.0 18.0 %all_to_all.27.refs_0_ = bf16[8,72,256]{2,1,0:T(8,128)(2,1)S(1)} all-to-all(bf16[8,72,256]{2,1,0:T(8,128)(2,1)S(1)} %constant_dynamic-update-slice_fusion.2), channel_id=1, replica_groups=mesh['seq_0'=8,'seq_1'=4,'seq_2'=2,'chan_0'=4,'chan_1'=2] {'chan_0','cha..., dimensions={0} | all-to-all | bytes 589824 | tf_op jit(solution)/shard_map/all_to_all | solution.py:598
  120.0 0.7 shard_map.160
  (3 shorter events, 0.0 us)
Async XLA Ops:
  2.3 14.0 %copy-start.2 = (bf16[128,256]{1,0:T(8,128)(2,1)S(1)}, bf16[128,256]{1,0:T(8,128)(2,1)}, u32[]{:S(2)}) copy-start(bf16[128,256]{1,0:T(8,128)(2,1)} %get-tuple-element.47) | copy-start | bytes 196612
  2.3 24.8 %all-to-all-start = ((bf16[32,8,512]{2,1,0:T(8,128)(2,1)}), bf16[32,8,512]{2,1,0:T(8,128)(2,1)S(1)}, u32[]{:S(2)}, u32[]{:S(2)}) async-start(bf16[32,8,512]{2,1,0:T(8,128)(2,1)} %get-tuple-element.48), calls=%async_computation | async-start | bytes 524288 | tf_op jit(solution)/shard_map/all_to_all | solution.py:598
  16.3 12.8 %collective-permute-start = (bf16[128,256]{1,0:T(8,128)(2,1)S(1)}, bf16[128,256]{1,0:T(8,128)(2,1)S(1)}, u32[]{:S(2)}, u32[]{:S(2)}) collective-permute-start(bf16[128,256]{1,0:T(8,128)(2,1)S(1)} %copy-done.2), channel_id=1, source_target_pairs={{0,1},{1,0},{2,3},{3,2},{4,5},{5,4},{6,7},{7,6},{8,9},{9,8},{10,11... | collective-permute-start | bytes 196616 | tf_op jit(solution)/shard_map/ppermute | solution.py:618
  27.1 18.5 %collective-permute-start.4 = (bf16[256,512]{1,0:T(8,128)(2,1)S(1)}, bf16[256,512]{1,0:T(8,128)(2,1)S(1)}, u32[]{:S(2)}, u32[]{:S(2)}) collective-permute-start(bf16[256,512]{1,0:T(8,128)(2,1)S(1)} %bitcast.24), channel_id=1, source_target_pairs={{0,8},{8,0},{1,9},{9,1},{2,10},{10,2},{3,11},{11,3},{4,12},{12,4},... | collective-permute-start | bytes 786440 | tf_op jit(solution)/shard_map/ppermute | solution.py:625
  29.1 10.4 %collective-permute-start.3 = (bf16[256,256]{1,0:T(8,128)(2,1)S(1)}, bf16[256,256]{1,0:T(8,128)(2,1)S(1)}, u32[]{:S(2)}, u32[]{:S(2)}) collective-permute-start(bf16[256,256]{1,0:T(8,128)(2,1)S(1)} %constant_dynamic-update-slice_fusion.refs_1_), channel_id=1, source_target_pairs={{0,6},{2,0},{4,2},{6,4},{1,7},{3,1},{5,3},{7,5},{8,14},{10,8},{12,... | collective-permute-start | bytes 393224 | tf_op jit(solution)/shard_map/ppermute | solution.py:621
  33.8 9.8 %collective-permute-start.2 = (bf16[256,256]{1,0:T(8,128)(2,1)S(1)}, bf16[256,256]{1,0:T(8,128)(2,1)S(1)}, u32[]{:S(2)}, u32[]{:S(2)}) collective-permute-start(bf16[256,256]{1,0:T(8,128)(2,1)S(1)} %constant_dynamic-update-slice_fusion.refs_1_), channel_id=1, source_target_pairs={{0,4},{2,6},{4,0},{6,2},{1,5},{3,7},{5,1},{7,3},{8,12},{10,14},{12... | collective-permute-start | bytes 393224 | tf_op jit(solution)/shard_map/ppermute | solution.py:621
  36.5 9.2 %collective-permute-start.1 = (bf16[256,256]{1,0:T(8,128)(2,1)S(1)}, bf16[256,256]{1,0:T(8,128)(2,1)S(1)}, u32[]{:S(2)}, u32[]{:S(2)}) collective-permute-start(bf16[256,256]{1,0:T(8,128)(2,1)S(1)} %constant_dynamic-update-slice_fusion.refs_1_), channel_id=1, source_target_pairs={{0,2},{2,4},{4,6},{6,0},{1,3},{3,5},{5,7},{7,1},{8,10},{10,12},{12... | collective-permute-start | bytes 393224 | tf_op jit(solution)/shard_map/ppermute | solution.py:621
  39.3 6.3 %copy-start = (f32[8,128]{1,0:T(8,128)S(1)}, f32[8,128]{1,0:T(8,128)}, u32[]{:S(2)}) copy-start(f32[8,128]{1,0:T(8,128)} %get-tuple-element.49.refs_7_.refs_4_.refs_5_) | copy-start | bytes 12292
  64.4 15.4 %all-to-all-start.2 = ((bf16[64,8,128]{2,1,0:T(8,128)(2,1)}), bf16[64,8,128]{2,1,0:T(8,128)(2,1)S(1)}, u32[]{:S(2)}, u32[]{:S(2)}) async-start(bf16[64,8,128]{2,1,0:T(8,128)(2,1)} %bitcast.17), calls=%async_computation.2 | async-start | bytes 262144 | tf_op jit(solution)/shard_map/all_to_all | solution.py:598
  81.3 3.4 %collective-permute-start.5 = (bf16[256,512]{1,0:T(8,128)(2,1)S(1)}, bf16[256,512]{1,0:T(8,128)(2,1)S(1)}, u32[]{:S(2)}, u32[]{:S(2)}) collective-permute-start(bf16[256,512]{1,0:T(8,128)(2,1)S(1)} %get-tuple-element.64), channel_id=1, source_target_pairs={{0,8},{8,0},{1,9},{9,1},{2,10},{10,2},{3,11},{11,3},{4,12},{12,4},... | collective-permute-start | bytes 786440 | tf_op jit(solution)/shard_map/ppermute | solution.py:638
  84.9 16.3 %copy-start.1 = (f32[2,2]{1,0:T(2,128)S(1)}, f32[2,2]{1,0:T(2,128)}, u32[]{:S(2)}) copy-start(f32[2,2]{1,0:T(2,128)} %refs_1_.1) | copy-start | bytes 52

commit v8 on v7

--- a/solution.py
+++ b/solution.py
@@ -616,11 +616,10 @@
         skip_gain.reshape(1, -1),
     )
     other = lax.ppermute(own, "chan_1", SWAP)
-    pair = jnp.concatenate([own, other], 0)
-    parts = [pair] + [
-        lax.ppermute(pair, "chan_0", [(k, (k + d) % 4) for k in range(4)])
-        for d in (1, 2, 3)
-    ]
+    parts = [jnp.concatenate([own, other], 0)]
+    for d in (1, 2, 3):
+        ring = [(k, (k + d) % 4) for k in range(4)]
+        parts.append(lax.ppermute(parts[0], "chan_0", ring))
     here = exchange(rows, ZY).reshape(-1, 512)
     there = lax.ppermute(here, CORE, SWAP)
     across, around = lax.axis_index("chan_0"), lax.axis_index("chan_1")

time: 121 us -> 121 us (level)
  no operation moved by 1% of the time
where the time goes in v8:
time: 121 us
  blocking collectives  50.6 us (42%)
  starting transfers between devices  39.2 us (32%)
  waiting for transfers between devices  19.9 us (16%)
  Pallas kernels  9.9 us (8%)
    all_to_all x3, blocking collectives, exchange(): return lax.all_to_all(array, axis, 0, 0, tiled=True)  50.6 us
    all_to_all x2, starting transfers between devices, exchange(): return lax.all_to_all(array, axis, 0, 0, tiled=True)  20.1 us
    all_to_all x2, waiting for transfers between devices, exchange(): return lax.all_to_all(array, axis, 0, 0, tiled=True)  13.4 us
    ppermute x3, starting transfers between devices, body(): parts.append(lax.ppermute(parts[0], 'chan_0', ring))  10.2 us
    pallas_call x9, Pallas kernels, call(): pl.pallas_call(kernel, out_shape=[jax.ShapeDtypeStruct(s, d) for s, d in...  9.9 us
    ppermute x3, waiting for transfers between devices, body(): parts.append(lax.ppermute(parts[0], 'chan_0', ring))  6.19 us
    ppermute x1, starting transfers between devices, body(): other = lax.ppermute(own, 'chan_1', SWAP)  5.04 us
  transfers between devices with their start and end apart: 8, of which 5 were waited for; matrix products, arithmetic and copies ran while one was open for 0% of the time, Pallas kernels for 2%

profile of v8, /device:TPU:16, one launch (start us, length us, event | category | flops | bytes accessed | tf_op | source)
XLA Modules:
  0.0 120.6 jit_solution(15196631588540532242)
XLA Ops:
  0.6 1.6 %shard_map.152 = (bf16[128,256]{1,0:T(8,128)(2,1)}, bf16[32,8,512]{2,1,0:T(8,128)(2,1)}, f32[8,128]{1,0:T(8,128)}) custom-call(bf16[64,256]{1,0:T(8,128)(2,1)} %bitcast.31, bf16[64,256]{1,0:T(8,128)(2,1)} %bitcast.32, bf16[8,128]{1,0:T(8,128)(2,1)} %refs_2_.1, bf16[8,128]{1,0:T(8,128)(2,1)} %refs_3_.1, bf16[8,128]{1,0:T(8,128)(2,1)} %bitcast.33, ...), custom_call_target="tpu_custom_call" | custom-call | flops 1000000 | bytes 71752 | tf_op jit(solution)/shard_map/pallas_call | solution.py:276
  2.3 0.0 copy-start.2
  2.3 14.0 %all-to-all-start = ((bf16[32,8,512]{2,1,0:T(8,128)(2,1)}), bf16[32,8,512]{2,1,0:T(8,128)(2,1)S(1)}, u32[]{:S(2)}, u32[]{:S(2)}) async-start(bf16[32,8,512]{2,1,0:T(8,128)(2,1)} %get-tuple-element.48), calls=%async_computation | async-start | bytes 524288 | tf_op jit(solution)/shard_map/all_to_all | solution.py:598
  16.3 0.0 copy-done.2
  16.3 5.0 %collective-permute-start = (bf16[128,256]{1,0:T(8,128)(2,1)S(1)}, bf16[128,256]{1,0:T(8,128)(2,1)S(1)}, u32[]{:S(2)}, u32[]{:S(2)}) collective-permute-start(bf16[128,256]{1,0:T(8,128)(2,1)S(1)} %copy-done.2), channel_id=1, source_target_pairs={{0,1},{1,0},{2,3},{3,2},{4,5},{5,4},{6,7},{7,6},{8,9},{9,8},{10,11... | collective-permute-start | bytes 196616 | tf_op jit(solution)/shard_map/ppermute | solution.py:618
  21.3 5.8 %all-to-all-done = bf16[32,8,512]{2,1,0:T(8,128)(2,1)S(1)} async-done(((bf16[32,8,512]{2,1,0:T(8,128)(2,1)}), bf16[32,8,512]{2,1,0:T(8,128)(2,1)S(1)}, u32[]{:S(2)}, u32[]{:S(2)}) %all-to-all-start) | async-done | bytes 262176 | tf_op jit(solution)/shard_map/all_to_all | solution.py:598
  27.1 1.9 %collective-permute-start.4 = (bf16[256,512]{1,0:T(8,128)(2,1)S(1)}, bf16[256,512]{1,0:T(8,128)(2,1)S(1)}, u32[]{:S(2)}, u32[]{:S(2)}) collective-permute-start(bf16[256,512]{1,0:T(8,128)(2,1)S(1)} %bitcast.24), channel_id=1, source_target_pairs={{0,8},{8,0},{1,9},{9,1},{2,10},{10,2},{3,11},{11,3},{4,12},{12,4},... | collective-permute-start | bytes 786440 | tf_op jit(solution)/shard_map/ppermute | solution.py:624
  29.1 0.0 collective-permute-done
  29.1 4.7 %collective-permute-start.3 = (bf16[256,256]{1,0:T(8,128)(2,1)S(1)}, bf16[256,256]{1,0:T(8,128)(2,1)S(1)}, u32[]{:S(2)}, u32[]{:S(2)}) collective-permute-start(bf16[256,256]{1,0:T(8,128)(2,1)S(1)} %constant_dynamic-update-slice_fusion.refs_1_), channel_id=1, source_target_pairs={{0,6},{2,0},{4,2},{6,4},{1,7},{3,1},{5,3},{7,5},{8,14},{10,8},{12,... | collective-permute-start | bytes 393224 | tf_op jit(solution)/shard_map/ppermute | solution.py:622
  33.8 2.7 %collective-permute-start.2 = (bf16[256,256]{1,0:T(8,128)(2,1)S(1)}, bf16[256,256]{1,0:T(8,128)(2,1)S(1)}, u32[]{:S(2)}, u32[]{:S(2)}) collective-permute-start(bf16[256,256]{1,0:T(8,128)(2,1)S(1)} %constant_dynamic-update-slice_fusion.refs_1_), channel_id=1, source_target_pairs={{0,4},{2,6},{4,0},{6,2},{1,5},{3,7},{5,1},{7,3},{8,12},{10,14},{12... | collective-permute-start | bytes 393224 | tf_op jit(solution)/shard_map/ppermute | solution.py:622
  36.5 2.8 %collective-permute-start.1 = (bf16[256,256]{1,0:T(8,128)(2,1)S(1)}, bf16[256,256]{1,0:T(8,128)(2,1)S(1)}, u32[]{:S(2)}, u32[]{:S(2)}) collective-permute-start(bf16[256,256]{1,0:T(8,128)(2,1)S(1)} %constant_dynamic-update-slice_fusion.refs_1_), channel_id=1, source_target_pairs={{0,2},{2,4},{4,6},{6,0},{1,3},{3,5},{5,7},{7,1},{8,10},{10,12},{12... | collective-permute-start | bytes 393224 | tf_op jit(solution)/shard_map/ppermute | solution.py:622
  39.3 0.0 copy-start
  39.3 0.1 stack.39.refs_0_
  39.4 0.0 collective-permute-done.3.refs_4_
  39.4 4.1 %collective-permute-done.2.refs_3_ = bf16[256,256]{1,0:T(8,128)(2,1)S(1)} collective-permute-done((bf16[256,256]{1,0:T(8,128)(2,1)S(1)}, bf16[256,256]{1,0:T(8,128)(2,1)S(1)}, u32[]{:S(2)}, u32[]{:S(2)}) %collective-permute-start.2) | collective-permute-done | bytes 131104 | tf_op jit(solution)/shard_map/ppermute | solution.py:622
  43.5 2.1 %collective-permute-done.1.refs_2_ = bf16[256,256]{1,0:T(8,128)(2,1)S(1)} collective-permute-done((bf16[256,256]{1,0:T(8,128)(2,1)S(1)}, bf16[256,256]{1,0:T(8,128)(2,1)S(1)}, u32[]{:S(2)}, u32[]{:S(2)}) %collective-permute-start.1) | collective-permute-done | bytes 131104 | tf_op jit(solution)/shard_map/ppermute | solution.py:622
  45.6 0.0 collective-permute-done.4.refs_6_
  45.6 0.0 copy-done
  45.6 1.4 %shard_map.153 = (bf16[512,128]{1,0:T(8,128)(2,1)S(1)}, f32[128,256]{1,0:T(8,128)S(1)}, f32[128,256]{1,0:T(8,128)S(1)}, f32[128,256]{1,0:T(8,128)S(1)}, f32[48,256]{1,0:T(8,128)S(1)}) custom-call(s32[9]{0:T(128)S(1)} %stack.39.refs_0_, bf16[256,256]{1,0:T(8,128)(2,1)S(1)} %constant_dynamic-update-slice_fusion.refs_1_, ...), custom_call_target="tpu_custom_call" | custom-call | flops 300000000 | bytes 1052708 | tf_op jit(solution)/shard_map/pallas_call | solution.py:276
  47.0 16.4 %all_to_all.25 = bf16[64,8,128]{2,1,0:T(8,128)(2,1)S(1)} all-to-all(bf16[64,8,128]{2,1,0:T(8,128)(2,1)S(1)} %bitcast.30), channel_id=1, replica_groups=mesh['seq_0'=8,'seq_1'=4,'seq_2'=2,'chan_0'=4,'chan_1'=2] {'seq_0','seq_..., dimensions={0} | all-to-all | bytes 262144 | tf_op jit(solution)/shard_map/all_to_all | solution.py:598
  63.4 1.0 shard_map.155
  64.4 6.1 %all-to-all-start.2 = ((bf16[64,8,128]{2,1,0:T(8,128)(2,1)}), bf16[64,8,128]{2,1,0:T(8,128)(2,1)S(1)}, u32[]{:S(2)}, u32[]{:S(2)}) async-start(bf16[64,8,128]{2,1,0:T(8,128)(2,1)} %bitcast.17), calls=%async_computation.2 | async-start | bytes 262144 | tf_op jit(solution)/shard_map/all_to_all | solution.py:598
  70.5 1.7 %shard_map.154 = (f32[256,256]{1,0:T(8,128)S(1)}, f32[256,256]{1,0:T(8,128)S(1)}, f32[128,256]{1,0:T(8,128)S(1)}, f32[24,256]{1,0:T(8,128)S(1)}) custom-call(f32[128,256]{1,0:T(8,128)S(1)} %get-tuple-element.50.refs_0_.refs_6_, f32[128,256]{1,0:T(8,128)S(1)} %get-tuple-element.51.refs_1_.refs_7_, f32[128,256]{1,0:T(8,128)S(1)} %get-tuple-element.52.refs_2_.refs_8_, ...), custom_call_target="tpu_custom_call" | custom-call | flops 300000000 | bytes 446464 | tf_op jit(solution)/shard_map/pallas_call | solution.py:276
  72.2 7.6 %all-to-all-done.2 = bf16[64,8,128]{2,1,0:T(8,128)(2,1)S(1)} async-done(((bf16[64,8,128]{2,1,0:T(8,128)(2,1)}), bf16[64,8,128]{2,1,0:T(8,128)(2,1)S(1)}, u32[]{:S(2)}, u32[]{:S(2)}) %all-to-all-start.2) | async-done | bytes 131104 | tf_op jit(solution)/shard_map/all_to_all | solution.py:598
  79.8 1.5 %shard_map.156 = (bf16[256,512]{1,0:T(8,128)(2,1)S(1)}, bf16[640,256]{1,0:T(8,128)(2,1)S(1)}, bf16[256,256]{1,0:T(8,128)(2,1)S(1)}, f32[8,128]{1,0:T(8,128)S(1)}) custom-call(s32[9]{0:T(128)S(1)} %stack.39.refs_0_, bf16[256,256]{1,0:T(8,128)(2,1)S(1)} %constant_dynamic-update-slice_fusion.refs_1_, bf16[256,256]{1,0:T(8,128)(2,1)S(1)} %collective-permute-done.1.refs_2_, ...), custom_call_target="tpu_custom_call" | custom-call | flops 400000000 | bytes 1781796 | tf_op jit(solution)/shard_map/pallas_call | solution.py:276
  81.3 2.0 %collective-permute-start.5 = (bf16[256,512]{1,0:T(8,128)(2,1)S(1)}, bf16[256,512]{1,0:T(8,128)(2,1)S(1)}, u32[]{:S(2)}, u32[]{:S(2)}) collective-permute-start(bf16[256,512]{1,0:T(8,128)(2,1)S(1)} %get-tuple-element.64), channel_id=1, source_target_pairs={{0,8},{8,0},{1,9},{9,1},{2,10},{10,2},{3,11},{11,3},{4,12},{12,4},... | collective-permute-start | bytes 786440 | tf_op jit(solution)/shard_map/ppermute | solution.py:637
  83.3 1.0 shard_map.157
  84.4 0.4 collective-permute-done.5.refs_1_
  84.7 0.2 shard_map.158
  84.9 0.0 copy-start.1
  84.9 16.3 %all_to_all.26.refs_0_ = bf16[32,8,512]{2,1,0:T(8,128)(2,1)S(1)} all-to-all(bf16[32,8,512]{2,1,0:T(8,128)(2,1)S(1)} %bitcast.27), channel_id=1, replica_groups=mesh['seq_0'=8,'seq_1'=4,'seq_2'=2,'chan_0'=4,'chan_1'=2] {'seq_0','seq_1'}, dimensions={0} | all-to-all | bytes 524288 | tf_op jit(solution)/shard_map/all_to_all | solution.py:598
  101.2 0.0 copy-done.1
  101.2 0.8 shard_map.159
  102.0 18.0 %all_to_all.27.refs_0_ = bf16[8,72,256]{2,1,0:T(8,128)(2,1)S(1)} all-to-all(bf16[8,72,256]{2,1,0:T(8,128)(2,1)S(1)} %constant_dynamic-update-slice_fusion.2), channel_id=1, replica_groups=mesh['seq_0'=8,'seq_1'=4,'seq_2'=2,'chan_0'=4,'chan_1'=2] {'chan_0','cha..., dimensions={0} | all-to-all | bytes 589824 | tf_op jit(solution)/shard_map/all_to_all | solution.py:598
  120.0 0.7 shard_map.160
  (3 shorter events, 0.0 us)
Async XLA Ops:
  2.3 14.0 %copy-start.2 = (bf16[128,256]{1,0:T(8,128)(2,1)S(1)}, bf16[128,256]{1,0:T(8,128)(2,1)}, u32[]{:S(2)}) copy-start(bf16[128,256]{1,0:T(8,128)(2,1)} %get-tuple-element.47) | copy-start | bytes 196612
  2.3 24.8 %all-to-all-start = ((bf16[32,8,512]{2,1,0:T(8,128)(2,1)}), bf16[32,8,512]{2,1,0:T(8,128)(2,1)S(1)}, u32[]{:S(2)}, u32[]{:S(2)}) async-start(bf16[32,8,512]{2,1,0:T(8,128)(2,1)} %get-tuple-element.48), calls=%async_computation | async-start | bytes 524288 | tf_op jit(solution)/shard_map/all_to_all | solution.py:598
  16.3 12.8 %collective-permute-start = (bf16[128,256]{1,0:T(8,128)(2,1)S(1)}, bf16[128,256]{1,0:T(8,128)(2,1)S(1)}, u32[]{:S(2)}, u32[]{:S(2)}) collective-permute-start(bf16[128,256]{1,0:T(8,128)(2,1)S(1)} %copy-done.2), channel_id=1, source_target_pairs={{0,1},{1,0},{2,3},{3,2},{4,5},{5,4},{6,7},{7,6},{8,9},{9,8},{10,11... | collective-permute-start | bytes 196616 | tf_op jit(solution)/shard_map/ppermute | solution.py:618
  27.1 18.5 %collective-permute-start.4 = (bf16[256,512]{1,0:T(8,128)(2,1)S(1)}, bf16[256,512]{1,0:T(8,128)(2,1)S(1)}, u32[]{:S(2)}, u32[]{:S(2)}) collective-permute-start(bf16[256,512]{1,0:T(8,128)(2,1)S(1)} %bitcast.24), channel_id=1, source_target_pairs={{0,8},{8,0},{1,9},{9,1},{2,10},{10,2},{3,11},{11,3},{4,12},{12,4},... | collective-permute-start | bytes 786440 | tf_op jit(solution)/shard_map/ppermute | solution.py:624
  29.1 10.4 %collective-permute-start.3 = (bf16[256,256]{1,0:T(8,128)(2,1)S(1)}, bf16[256,256]{1,0:T(8,128)(2,1)S(1)}, u32[]{:S(2)}, u32[]{:S(2)}) collective-permute-start(bf16[256,256]{1,0:T(8,128)(2,1)S(1)} %constant_dynamic-update-slice_fusion.refs_1_), channel_id=1, source_target_pairs={{0,6},{2,0},{4,2},{6,4},{1,7},{3,1},{5,3},{7,5},{8,14},{10,8},{12,... | collective-permute-start | bytes 393224 | tf_op jit(solution)/shard_map/ppermute | solution.py:622
  33.8 9.8 %collective-permute-start.2 = (bf16[256,256]{1,0:T(8,128)(2,1)S(1)}, bf16[256,256]{1,0:T(8,128)(2,1)S(1)}, u32[]{:S(2)}, u32[]{:S(2)}) collective-permute-start(bf16[256,256]{1,0:T(8,128)(2,1)S(1)} %constant_dynamic-update-slice_fusion.refs_1_), channel_id=1, source_target_pairs={{0,4},{2,6},{4,0},{6,2},{1,5},{3,7},{5,1},{7,3},{8,12},{10,14},{12... | collective-permute-start | bytes 393224 | tf_op jit(solution)/shard_map/ppermute | solution.py:622
  36.5 9.2 %collective-permute-start.1 = (bf16[256,256]{1,0:T(8,128)(2,1)S(1)}, bf16[256,256]{1,0:T(8,128)(2,1)S(1)}, u32[]{:S(2)}, u32[]{:S(2)}) collective-permute-start(bf16[256,256]{1,0:T(8,128)(2,1)S(1)} %constant_dynamic-update-slice_fusion.refs_1_), channel_id=1, source_target_pairs={{0,2},{2,4},{4,6},{6,0},{1,3},{3,5},{5,7},{7,1},{8,10},{10,12},{12... | collective-permute-start | bytes 393224 | tf_op jit(solution)/shard_map/ppermute | solution.py:622
  39.3 6.3 %copy-start = (f32[8,128]{1,0:T(8,128)S(1)}, f32[8,128]{1,0:T(8,128)}, u32[]{:S(2)}) copy-start(f32[8,128]{1,0:T(8,128)} %get-tuple-element.49.refs_7_.refs_4_.refs_5_) | copy-start | bytes 12292
  64.4 15.4 %all-to-all-start.2 = ((bf16[64,8,128]{2,1,0:T(8,128)(2,1)}), bf16[64,8,128]{2,1,0:T(8,128)(2,1)S(1)}, u32[]{:S(2)}, u32[]{:S(2)}) async-start(bf16[64,8,128]{2,1,0:T(8,128)(2,1)} %bitcast.17), calls=%async_computation.2 | async-start | bytes 262144 | tf_op jit(solution)/shard_map/all_to_all | solution.py:598
  81.3 3.4 %collective-permute-start.5 = (bf16[256,512]{1,0:T(8,128)(2,1)S(1)}, bf16[256,512]{1,0:T(8,128)(2,1)S(1)}, u32[]{:S(2)}, u32[]{:S(2)}) collective-permute-start(bf16[256,512]{1,0:T(8,128)(2,1)S(1)} %get-tuple-element.64), channel_id=1, source_target_pairs={{0,8},{8,0},{1,9},{9,1},{2,10},{10,2},{3,11},{11,3},{4,12},{12,4},... | collective-permute-start | bytes 786440 | tf_op jit(solution)/shard_map/ppermute | solution.py:637
  84.9 16.3 %copy-start.1 = (f32[2,2]{1,0:T(2,128)S(1)}, f32[2,2]{1,0:T(2,128)}, u32[]{:S(2)}) copy-start(f32[2,2]{1,0:T(2,128)} %refs_1_.1) | copy-start | bytes 52

commit v9 on v8

--- a/solution.py
+++ b/solution.py
@@ -86,7 +86,7 @@
     decay = -rate * step
     from_start, from_end = running(decay)
     run = jnp.where(forward_rows(n), from_start, from_end)
-    total = jnp.sum(decay, axis=1, keepdims=True)
+    total = jnp.where(forward_rows(1), run[:, n - 1 : n], run[:, :1])
     grown = jnp.exp(run)
     tail = jnp.exp(total - run)
     gated = pre * sigmoid(pre)
@@ -399,7 +399,6 @@
             block = slice(32 * k, 32 * k + 32)
             outs[0][at, pl.ds(pl.multiple_of(mine, 32), 32), :] = dinput[block]
             outs[0][at, pl.ds(pl.multiple_of(32 - mine, 32), 32), :] = dinput[256:][block]
-            outs[0][at, 64:, :] = jnp.zeros((8, n), BF16)
             outs[1][pl.ds(pl.multiple_of(at * 32, 32), 32), :] = grads[block]
 
     outs = [((8, 72, n), BF16), ((256, 512), F32)]
@@ -566,16 +565,18 @@
 
     if PLAIN:
         inside, *rest = add(grads, decay_rate)
-    else:
-
-        def fn(ins, outs):
-            for ref, value in zip(outs, add(ins[0][...], ins[1][...])):
-                ref[...] = value
-
-        shapes = [(8, 128), (8, 128), (2, 8), (2, 2), (2, 2), (1, 2)]
-        outs = [((8, 8, 256), BF16)] + [(shape, F32) for shape in shapes]
-        inside, *rest = call(fn, outs, (grads, decay_rate), 1_000_000)
-    return wide.at[:, 64:].set(inside), *rest
+        return wide.at[:, 64:].set(inside), *rest
+
+    def fn(ins, outs):
+        inside, *rest = add(ins[0][...], ins[1][...])
+        outs[0][:, :64, :] = ins[2][:, :64, :]
+        outs[0][:, 64:, :] = inside
+        for ref, value in zip(outs[1:], rest):
+            ref[...] = value
+
+    shapes = [(8, 128), (8, 128), (2, 8), (2, 2), (2, 2), (1, 2)]
+    outs = [(wide.shape, BF16)] + [(shape, F32) for shape in shapes]
+    return call(fn, outs, (grads, decay_rate, wide), 1_000_000)
 
 
 def add_parts(parts, scale):

time: 121 us -> 122 us (level)
  no operation moved by 1% of the time
where the time goes in v9:
time: 122 us; the launch traced here: 121 us
  blocking collectives  50.6 us (41%)
  starting transfers between devices  39.2 us (32%)
  waiting for transfers between devices  19.9 us (16%)
  Pallas kernels  10 us (8%)
    all_to_all x3, blocking collectives, exchange(): return lax.all_to_all(array, axis, 0, 0, tiled=True)  50.6 us
    all_to_all x2, starting transfers between devices, exchange(): return lax.all_to_all(array, axis, 0, 0, tiled=True)  20.1 us
    all_to_all x2, waiting for transfers between devices, exchange(): return lax.all_to_all(array, axis, 0, 0, tiled=True)  13.4 us
    ppermute x3, starting transfers between devices, body(): parts.append(lax.ppermute(parts[0], 'chan_0', ring))  10.2 us
    pallas_call x9, Pallas kernels, call(): pl.pallas_call(kernel, out_shape=[jax.ShapeDtypeStruct(s, d) for s, d in...  10 us
    ppermute x3, waiting for transfers between devices, body(): parts.append(lax.ppermute(parts[0], 'chan_0', ring))  6.19 us
    ppermute x1, starting transfers between devices, body(): other = lax.ppermute(own, 'chan_1', SWAP)  5.04 us
  transfers between devices with their start and end apart: 8, of which 5 were waited for; matrix products, arithmetic and copies ran while one was open for 0% of the time, Pallas kernels for 2%

profile of v9, /device:TPU:16, one launch (start us, length us, event | category | flops | bytes accessed | tf_op | source)
XLA Modules:
  0.0 121.4 jit_solution(3071352223247844372)
XLA Ops:
  0.6 1.6 %shard_map.152 = (bf16[128,256]{1,0:T(8,128)(2,1)}, bf16[32,8,512]{2,1,0:T(8,128)(2,1)}, f32[8,128]{1,0:T(8,128)}) custom-call(bf16[64,256]{1,0:T(8,128)(2,1)} %bitcast.31, bf16[64,256]{1,0:T(8,128)(2,1)} %bitcast.32, bf16[8,128]{1,0:T(8,128)(2,1)} %refs_2_.1, bf16[8,128]{1,0:T(8,128)(2,1)} %refs_3_.1, bf16[8,128]{1,0:T(8,128)(2,1)} %bitcast.33, ...), custom_call_target="tpu_custom_call" | custom-call | flops 1000000 | bytes 71752 | tf_op jit(solution)/shard_map/pallas_call | solution.py:276
  2.3 0.0 copy-start.2
  2.3 14.0 %all-to-all-start = ((bf16[32,8,512]{2,1,0:T(8,128)(2,1)}), bf16[32,8,512]{2,1,0:T(8,128)(2,1)S(1)}, u32[]{:S(2)}, u32[]{:S(2)}) async-start(bf16[32,8,512]{2,1,0:T(8,128)(2,1)} %get-tuple-element.36), calls=%async_computation | async-start | bytes 524288 | tf_op jit(solution)/shard_map/all_to_all | solution.py:599
  16.3 0.0 copy-done.2
  16.3 5.0 %collective-permute-start = (bf16[128,256]{1,0:T(8,128)(2,1)S(1)}, bf16[128,256]{1,0:T(8,128)(2,1)S(1)}, u32[]{:S(2)}, u32[]{:S(2)}) collective-permute-start(bf16[128,256]{1,0:T(8,128)(2,1)S(1)} %copy-done.2), channel_id=1, source_target_pairs={{0,1},{1,0},{2,3},{3,2},{4,5},{5,4},{6,7},{7,6},{8,9},{9,8},{10,11... | collective-permute-start | bytes 196616 | tf_op jit(solution)/shard_map/ppermute | solution.py:619
  21.3 5.8 %all-to-all-done = bf16[32,8,512]{2,1,0:T(8,128)(2,1)S(1)} async-done(((bf16[32,8,512]{2,1,0:T(8,128)(2,1)}), bf16[32,8,512]{2,1,0:T(8,128)(2,1)S(1)}, u32[]{:S(2)}, u32[]{:S(2)}) %all-to-all-start) | async-done | bytes 262176 | tf_op jit(solution)/shard_map/all_to_all | solution.py:599
  27.1 1.9 %collective-permute-start.4 = (bf16[256,512]{1,0:T(8,128)(2,1)S(1)}, bf16[256,512]{1,0:T(8,128)(2,1)S(1)}, u32[]{:S(2)}, u32[]{:S(2)}) collective-permute-start(bf16[256,512]{1,0:T(8,128)(2,1)S(1)} %bitcast.24), channel_id=1, source_target_pairs={{0,8},{8,0},{1,9},{9,1},{2,10},{10,2},{3,11},{11,3},{4,12},{12,4},... | collective-permute-start | bytes 786440 | tf_op jit(solution)/shard_map/ppermute | solution.py:625
  29.1 0.0 collective-permute-done
  29.1 4.7 %collective-permute-start.3 = (bf16[256,256]{1,0:T(8,128)(2,1)S(1)}, bf16[256,256]{1,0:T(8,128)(2,1)S(1)}, u32[]{:S(2)}, u32[]{:S(2)}) collective-permute-start(bf16[256,256]{1,0:T(8,128)(2,1)S(1)} %constant_dynamic-update-slice_fusion.refs_1_), channel_id=1, source_target_pairs={{0,6},{2,0},{4,2},{6,4},{1,7},{3,1},{5,3},{7,5},{8,14},{10,8},{12,... | collective-permute-start | bytes 393224 | tf_op jit(solution)/shard_map/ppermute | solution.py:623
  33.8 2.7 %collective-permute-start.2 = (bf16[256,256]{1,0:T(8,128)(2,1)S(1)}, bf16[256,256]{1,0:T(8,128)(2,1)S(1)}, u32[]{:S(2)}, u32[]{:S(2)}) collective-permute-start(bf16[256,256]{1,0:T(8,128)(2,1)S(1)} %constant_dynamic-update-slice_fusion.refs_1_), channel_id=1, source_target_pairs={{0,4},{2,6},{4,0},{6,2},{1,5},{3,7},{5,1},{7,3},{8,12},{10,14},{12... | collective-permute-start | bytes 393224 | tf_op jit(solution)/shard_map/ppermute | solution.py:623
  36.5 2.8 %collective-permute-start.1 = (bf16[256,256]{1,0:T(8,128)(2,1)S(1)}, bf16[256,256]{1,0:T(8,128)(2,1)S(1)}, u32[]{:S(2)}, u32[]{:S(2)}) collective-permute-start(bf16[256,256]{1,0:T(8,128)(2,1)S(1)} %constant_dynamic-update-slice_fusion.refs_1_), channel_id=1, source_target_pairs={{0,2},{2,4},{4,6},{6,0},{1,3},{3,5},{5,7},{7,1},{8,10},{10,12},{12... | collective-permute-start | bytes 393224 | tf_op jit(solution)/shard_map/ppermute | solution.py:623
  39.3 0.0 copy-start
  39.3 0.1 stack.39.refs_0_
  39.4 0.0 collective-permute-done.3.refs_4_
  39.4 4.1 %collective-permute-done.2.refs_3_ = bf16[256,256]{1,0:T(8,128)(2,1)S(1)} collective-permute-done((bf16[256,256]{1,0:T(8,128)(2,1)S(1)}, bf16[256,256]{1,0:T(8,128)(2,1)S(1)}, u32[]{:S(2)}, u32[]{:S(2)}) %collective-permute-start.2) | collective-permute-done | bytes 131104 | tf_op jit(solution)/shard_map/ppermute | solution.py:623
  43.5 2.1 %collective-permute-done.1.refs_2_ = bf16[256,256]{1,0:T(8,128)(2,1)S(1)} collective-permute-done((bf16[256,256]{1,0:T(8,128)(2,1)S(1)}, bf16[256,256]{1,0:T(8,128)(2,1)S(1)}, u32[]{:S(2)}, u32[]{:S(2)}) %collective-permute-start.1) | collective-permute-done | bytes 131104 | tf_op jit(solution)/shard_map/ppermute | solution.py:623
  45.6 0.0 collective-permute-done.4.refs_6_
  45.6 0.0 copy-done
  45.6 1.5 %shard_map.153 = (bf16[512,128]{1,0:T(8,128)(2,1)S(1)}, f32[128,256]{1,0:T(8,128)S(1)}, f32[128,256]{1,0:T(8,128)S(1)}, f32[128,256]{1,0:T(8,128)S(1)}, f32[48,256]{1,0:T(8,128)S(1)}) custom-call(s32[9]{0:T(128)S(1)} %stack.39.refs_0_, bf16[256,256]{1,0:T(8,128)(2,1)S(1)} %constant_dynamic-update-slice_fusion.refs_1_, ...), custom_call_target="tpu_custom_call" | custom-call | flops 300000000 | bytes 1052708 | tf_op jit(solution)/shard_map/pallas_call | solution.py:276
  47.1 16.4 %all_to_all.25 = bf16[64,8,128]{2,1,0:T(8,128)(2,1)S(1)} all-to-all(bf16[64,8,128]{2,1,0:T(8,128)(2,1)S(1)} %bitcast.30), channel_id=1, replica_groups=mesh['seq_0'=8,'seq_1'=4,'seq_2'=2,'chan_0'=4,'chan_1'=2] {'seq_0','seq_..., dimensions={0} | all-to-all | bytes 262144 | tf_op jit(solution)/shard_map/all_to_all | solution.py:599
  63.5 1.0 shard_map.155
  64.5 6.1 %all-to-all-start.2 = ((bf16[64,8,128]{2,1,0:T(8,128)(2,1)}), bf16[64,8,128]{2,1,0:T(8,128)(2,1)S(1)}, u32[]{:S(2)}, u32[]{:S(2)}) async-start(bf16[64,8,128]{2,1,0:T(8,128)(2,1)} %bitcast.17), calls=%async_computation.2 | async-start | bytes 262144 | tf_op jit(solution)/shard_map/all_to_all | solution.py:599
  70.6 1.7 %shard_map.154 = (f32[256,256]{1,0:T(8,128)S(1)}, f32[256,256]{1,0:T(8,128)S(1)}, f32[128,256]{1,0:T(8,128)S(1)}, f32[24,256]{1,0:T(8,128)S(1)}) custom-call(f32[128,256]{1,0:T(8,128)S(1)} %get-tuple-element.38.refs_0_.refs_6_, f32[128,256]{1,0:T(8,128)S(1)} %get-tuple-element.39.refs_1_.refs_7_, f32[128,256]{1,0:T(8,128)S(1)} %get-tuple-element.40.refs_2_.refs_8_, ...), custom_call_target="tpu_custom_call" | custom-call | flops 300000000 | bytes 446464 | tf_op jit(solution)/shard_map/pallas_call | solution.py:276
  72.3 7.6 %all-to-all-done.2 = bf16[64,8,128]{2,1,0:T(8,128)(2,1)S(1)} async-done(((bf16[64,8,128]{2,1,0:T(8,128)(2,1)}), bf16[64,8,128]{2,1,0:T(8,128)(2,1)S(1)}, u32[]{:S(2)}, u32[]{:S(2)}) %all-to-all-start.2) | async-done | bytes 131104 | tf_op jit(solution)/shard_map/all_to_all | solution.py:599
  79.9 1.5 %shard_map.156 = (bf16[256,512]{1,0:T(8,128)(2,1)S(1)}, bf16[640,256]{1,0:T(8,128)(2,1)S(1)}, bf16[256,256]{1,0:T(8,128)(2,1)S(1)}, f32[8,128]{1,0:T(8,128)S(1)}) custom-call(s32[9]{0:T(128)S(1)} %stack.39.refs_0_, bf16[256,256]{1,0:T(8,128)(2,1)S(1)} %constant_dynamic-update-slice_fusion.refs_1_, bf16[256,256]{1,0:T(8,128)(2,1)S(1)} %collective-permute-done.1.refs_2_, ...), custom_call_target="tpu_custom_call" | custom-call | flops 400000000 | bytes 1781796 | tf_op jit(solution)/shard_map/pallas_call | solution.py:276
  81.4 2.0 %collective-permute-start.5 = (bf16[256,512]{1,0:T(8,128)(2,1)S(1)}, bf16[256,512]{1,0:T(8,128)(2,1)S(1)}, u32[]{:S(2)}, u32[]{:S(2)}) collective-permute-start(bf16[256,512]{1,0:T(8,128)(2,1)S(1)} %get-tuple-element.51), channel_id=1, source_target_pairs={{0,8},{8,0},{1,9},{9,1},{2,10},{10,2},{3,11},{11,3},{4,12},{12,4},... | collective-permute-start | bytes 786440 | tf_op jit(solution)/shard_map/ppermute | solution.py:638
  83.4 1.0 shard_map.157
  84.5 0.4 collective-permute-done.5.refs_1_
  84.8 0.2 shard_map.158
  85.0 16.3 %all_to_all.26.refs_0_ = bf16[32,8,512]{2,1,0:T(8,128)(2,1)S(1)} all-to-all(bf16[32,8,512]{2,1,0:T(8,128)(2,1)S(1)} %bitcast.27), channel_id=1, replica_groups=mesh['seq_0'=8,'seq_1'=4,'seq_2'=2,'chan_0'=4,'chan_1'=2] {'seq_0','seq_1'}, dimensions={0} | all-to-all | bytes 524288 | tf_op jit(solution)/shard_map/all_to_all | solution.py:599
  101.3 0.0 copy-start.1
  101.3 0.7 copy-done.1
  102.0 0.8 shard_map.159
  102.8 18.0 %all_to_all.27.refs_0_ = bf16[8,72,256]{2,1,0:T(8,128)(2,1)S(1)} all-to-all(bf16[8,72,256]{2,1,0:T(8,128)(2,1)S(1)} %get-tuple-element.53), channel_id=1, replica_groups=mesh['seq_0'=8,'seq_1'=4,'seq_2'=2,'chan_0'=4,'chan_1'=2] {'chan_0','cha..., dimensions={0} | all-to-all | bytes 589824 | tf_op jit(solution)/shard_map/all_to_all | solution.py:599
  120.7 0.7 shard_map.160
  (2 shorter events, 0.0 us)
Async XLA Ops:
  2.3 14.0 %copy-start.2 = (bf16[128,256]{1,0:T(8,128)(2,1)S(1)}, bf16[128,256]{1,0:T(8,128)(2,1)}, u32[]{:S(2)}) copy-start(bf16[128,256]{1,0:T(8,128)(2,1)} %get-tuple-element.35) | copy-start | bytes 196612
  2.3 24.8 %all-to-all-start = ((bf16[32,8,512]{2,1,0:T(8,128)(2,1)}), bf16[32,8,512]{2,1,0:T(8,128)(2,1)S(1)}, u32[]{:S(2)}, u32[]{:S(2)}) async-start(bf16[32,8,512]{2,1,0:T(8,128)(2,1)} %get-tuple-element.36), calls=%async_computation | async-start | bytes 524288 | tf_op jit(solution)/shard_map/all_to_all | solution.py:599
  16.3 12.8 %collective-permute-start = (bf16[128,256]{1,0:T(8,128)(2,1)S(1)}, bf16[128,256]{1,0:T(8,128)(2,1)S(1)}, u32[]{:S(2)}, u32[]{:S(2)}) collective-permute-start(bf16[128,256]{1,0:T(8,128)(2,1)S(1)} %copy-done.2), channel_id=1, source_target_pairs={{0,1},{1,0},{2,3},{3,2},{4,5},{5,4},{6,7},{7,6},{8,9},{9,8},{10,11... | collective-permute-start | bytes 196616 | tf_op jit(solution)/shard_map/ppermute | solution.py:619
  27.1 18.5 %collective-permute-start.4 = (bf16[256,512]{1,0:T(8,128)(2,1)S(1)}, bf16[256,512]{1,0:T(8,128)(2,1)S(1)}, u32[]{:S(2)}, u32[]{:S(2)}) collective-permute-start(bf16[256,512]{1,0:T(8,128)(2,1)S(1)} %bitcast.24), channel_id=1, source_target_pairs={{0,8},{8,0},{1,9},{9,1},{2,10},{10,2},{3,11},{11,3},{4,12},{12,4},... | collective-permute-start | bytes 786440 | tf_op jit(solution)/shard_map/ppermute | solution.py:625
  29.1 10.4 %collective-permute-start.3 = (bf16[256,256]{1,0:T(8,128)(2,1)S(1)}, bf16[256,256]{1,0:T(8,128)(2,1)S(1)}, u32[]{:S(2)}, u32[]{:S(2)}) collective-permute-start(bf16[256,256]{1,0:T(8,128)(2,1)S(1)} %constant_dynamic-update-slice_fusion.refs_1_), channel_id=1, source_target_pairs={{0,6},{2,0},{4,2},{6,4},{1,7},{3,1},{5,3},{7,5},{8,14},{10,8},{12,... | collective-permute-start | bytes 393224 | tf_op jit(solution)/shard_map/ppermute | solution.py:623
  33.8 9.8 %collective-permute-start.2 = (bf16[256,256]{1,0:T(8,128)(2,1)S(1)}, bf16[256,256]{1,0:T(8,128)(2,1)S(1)}, u32[]{:S(2)}, u32[]{:S(2)}) collective-permute-start(bf16[256,256]{1,0:T(8,128)(2,1)S(1)} %constant_dynamic-update-slice_fusion.refs_1_), channel_id=1, source_target_pairs={{0,4},{2,6},{4,0},{6,2},{1,5},{3,7},{5,1},{7,3},{8,12},{10,14},{12... | collective-permute-start | bytes 393224 | tf_op jit(solution)/shard_map/ppermute | solution.py:623
  36.5 9.2 %collective-permute-start.1 = (bf16[256,256]{1,0:T(8,128)(2,1)S(1)}, bf16[256,256]{1,0:T(8,128)(2,1)S(1)}, u32[]{:S(2)}, u32[]{:S(2)}) collective-permute-start(bf16[256,256]{1,0:T(8,128)(2,1)S(1)} %constant_dynamic-update-slice_fusion.refs_1_), channel_id=1, source_target_pairs={{0,2},{2,4},{4,6},{6,0},{1,3},{3,5},{5,7},{7,1},{8,10},{10,12},{12... | collective-permute-start | bytes 393224 | tf_op jit(solution)/shard_map/ppermute | solution.py:623
  39.3 6.3 %copy-start = (f32[8,128]{1,0:T(8,128)S(1)}, f32[8,128]{1,0:T(8,128)}, u32[]{:S(2)}) copy-start(f32[8,128]{1,0:T(8,128)} %get-tuple-element.37.refs_7_.refs_4_.refs_5_) | copy-start | bytes 12292
  64.5 15.4 %all-to-all-start.2 = ((bf16[64,8,128]{2,1,0:T(8,128)(2,1)}), bf16[64,8,128]{2,1,0:T(8,128)(2,1)S(1)}, u32[]{:S(2)}, u32[]{:S(2)}) async-start(bf16[64,8,128]{2,1,0:T(8,128)(2,1)} %bitcast.17), calls=%async_computation.2 | async-start | bytes 262144 | tf_op jit(solution)/shard_map/all_to_all | solution.py:599
  81.4 3.4 %collective-permute-start.5 = (bf16[256,512]{1,0:T(8,128)(2,1)S(1)}, bf16[256,512]{1,0:T(8,128)(2,1)S(1)}, u32[]{:S(2)}, u32[]{:S(2)}) collective-permute-start(bf16[256,512]{1,0:T(8,128)(2,1)S(1)} %get-tuple-element.51), channel_id=1, source_target_pairs={{0,8},{8,0},{1,9},{9,1},{2,10},{10,2},{3,11},{11,3},{4,12},{12,4},... | collective-permute-start | bytes 786440 | tf_op jit(solution)/shard_map/ppermute | solution.py:638
  101.3 0.7 copy-start.1
